TPU v7x, 32 devices: a whole 2x2x4 slice. The times are simulated.
32 devices in a mesh: exp: 4 (over x, core), fsdp: 8 (over z, y).
Axes of the slice: x: 2, y: 2, z: 4, core: 2. Of those that a mesh axis runs over, the one named last changes fastest.
Arguments:
- patches: bfloat16 [32768, 768], P(('exp', 'fsdp')), may hold values from -6 to 6
- cond_embed: bfloat16 [128, 768], P(('exp', 'fsdp')), may hold values from -4 to 4, as said below
- image_kind: int32 [32], P(('exp', 'fsdp')), may hold values from 0 to 1, as said below
- expert_ids: int32 [32768, 2], P(('exp', 'fsdp')), may hold values from 0 to 7, all different within a row; in each aligned block of 1024 rows (0 to 1023, 1024 to 2047, ...) at most 288 rows name the same one
- out_grad: bfloat16 [32768, 768], P(('exp', 'fsdp')), may hold values from -6 to 6
- modulate_weight: bfloat16 [768, 4608], P('fsdp', 'exp'), may hold values from -0.21875 to 0.21875
- attend_weight: bfloat16 [768, 2304], P('fsdp', 'exp'), may hold values from -0.21875 to 0.21875
- output_weight: bfloat16 [768, 768], P('fsdp', 'exp'), may hold values from -2 to 2
- router_weight: bfloat16 [768, 8], P('fsdp', 'exp'), may hold values from -0.15625 to 0.15625
- shared_in: bfloat16 [768, 3072], P('fsdp', 'exp'), may hold values from -0.21875 to 0.21875
- shared_out: bfloat16 [3072, 768], P('fsdp', 'exp'), may hold values from -0.109375 to 0.109375
- expert_in: bfloat16 [8, 768, 3072], P('exp', None, 'fsdp'), may hold values from -0.21875 to 0.21875
- expert_out: bfloat16 [8, 3072, 768], P('exp', 'fsdp'), may hold values from -0.109375 to 0.109375
Outputs:
- block_out: bfloat16 [32768, 768], P(('exp', 'fsdp'))
- patches_grad: float32 [32768, 768], P(('exp', 'fsdp'))
- cond_grad: float32 [128, 768], P(('exp', 'fsdp'))
- modulate_grad: float32 [768, 4608], P('fsdp', 'exp')
- attend_grad: float32 [768, 2304], P('fsdp', 'exp')
- output_grad: float32 [768, 768], P('fsdp', 'exp')
- router_grad: float32 [768, 8], P('fsdp', 'exp')
- shared_in_grad: float32 [768, 3072], P('fsdp', 'exp')
- shared_out_grad: float32 [3072, 768], P('fsdp', 'exp')
- expert_in_grad: float32 [8, 768, 3072], P('exp', None, 'fsdp')
- expert_out_grad: float32 [8, 3072, 768], P('exp', 'fsdp')
Inputs may be any that keep to these rules, and one draw needn't show every extreme that they name: `image_kind`: each group of 1024 patches holds one image (1) or four images of 256 patches (0). `cond_embed`: the rows of the blocks of a group whose image_kind is 1 are equal. `expert_ids`: the two experts of a row differ; among the rows of one device no expert is named more than 288 times, and that bound is reached.
All inputs are finite; a program needn't handle non-finite values.
Results may differ from a plain program's by a relative error of at most 0.02.
Values may be sent and summed in bfloat16 or wider, within the bound.
No kernel may reach another device: no remote copies, remote signals or barrier semaphores. Data moves between devices by JAX's collectives and lax.ppermute only.
A program may use at most 256 MiB of HBM per device.

v0:
```python
import jax
import jax.numpy as jnp
from jax import lax
from jax.sharding import PartitionSpec as P

H = 12
HD = 64
E = 8
TOPK = 2
SHORT = 256
GROUP = 1024
CAP = 288


eps_norm = 1e-06
tanh_gain = 0.7978845608028654


def layer_norm(values):
    centered = values - jnp.mean(values, axis=-1, keepdims=True)
    inverse = lax.rsqrt(jnp.mean(centered * centered, axis=-1, keepdims=True) + eps_norm)
    return (centered * inverse, inverse)


def norm_back(grad, normed, inverse):
    return inverse * (
        grad
        - jnp.mean(grad, axis=-1, keepdims=True)
        - normed * jnp.mean(grad * normed, axis=-1, keepdims=True)
    )


def gelu_tanh(values):
    return jax.nn.gelu(values, approximate=True)


def gelu_slope(values):
    hyper = jnp.tanh(tanh_gain * (values + 0.044715 * values * values * values))
    return 0.5 * (1.0 + hyper) + 0.5 * values * (1.0 - hyper * hyper) * tanh_gain * (
        1.0 + 3.0 * 0.044715 * values * values
    )


def silu_slope(values):
    sigma = jax.nn.sigmoid(values)
    return sigma * (1.0 + values * (1.0 - sigma))


def slot_table(expert_ids):
    flat = expert_ids.reshape(-1)
    onehot = (flat[:, None] == jnp.arange(E, dtype=jnp.int32)[None, :]).astype(jnp.int32)
    before = jnp.cumsum(onehot, axis=0) - onehot
    return jnp.sum(before * onehot, axis=1).reshape(expert_ids.shape)


def group_mask(long_flag):
    block = jnp.arange(GROUP, dtype=jnp.int32) // SHORT
    return (block[:, None] == block[None, :]) | (long_flag == 1)


def head_pairs(part):
    return part.reshape(GROUP, H // 2, 2, HD).transpose(1, 0, 2, 3)


def attend_group(inputs):
    triple_group, long_flag = inputs
    allowed = group_mask(long_flag)
    scale = HD ** (-0.5)

    def one_pair(items):
        query_pair, key_pair, value_pair = items
        scores = (
            jnp.einsum("qhd,khd->hqk", query_pair, key_pair, preferred_element_type=jnp.float32)
            * scale
        )
        masked = jnp.where(allowed[None], scores, -1e30)
        peak = jnp.max(masked, axis=-1, keepdims=True)
        weights = jnp.exp(masked - peak)
        total = jnp.sum(weights, axis=-1, keepdims=True)
        attention = (weights / total).astype(jnp.bfloat16)
        mixed = jnp.einsum(
            "hqk,khd->qhd", attention, value_pair, preferred_element_type=jnp.float32
        )
        return (mixed.astype(jnp.bfloat16), (peak + jnp.log(total))[..., 0])

    mixed, logsum = lax.map(
        one_pair,
        (
            head_pairs(triple_group[:, 0]),
            head_pairs(triple_group[:, 1]),
            head_pairs(triple_group[:, 2]),
        ),
    )
    return (mixed.transpose(1, 0, 2, 3).reshape(GROUP, H * HD), logsum)


def attend_back(inputs):
    triple_group, logsum, grad_mixed, long_flag = inputs
    allowed = group_mask(long_flag)
    scale = HD ** (-0.5)

    def one_pair(items):
        query_pair, key_pair, value_pair, logsum_pair, grad_pair = items
        scores = (
            jnp.einsum("qhd,khd->hqk", query_pair, key_pair, preferred_element_type=jnp.float32)
            * scale
        )
        masked = jnp.where(allowed[None], scores, -1e30)
        attention = jnp.exp(masked - logsum_pair[..., None])
        grad_value = jnp.einsum(
            "hqk,qhd->khd",
            attention.astype(jnp.bfloat16),
            grad_pair,
            preferred_element_type=jnp.float32,
        )
        grad_attention = jnp.einsum(
            "qhd,khd->hqk", grad_pair, value_pair, preferred_element_type=jnp.float32
        )
        inner = jnp.sum(attention * grad_attention, axis=-1, keepdims=True)
        grad_scores = (attention * (grad_attention - inner)).astype(jnp.bfloat16)
        grad_query = (
            jnp.einsum("hqk,khd->qhd", grad_scores, key_pair, preferred_element_type=jnp.float32)
            * scale
        )
        grad_key = (
            jnp.einsum("hqk,qhd->khd", grad_scores, query_pair, preferred_element_type=jnp.float32)
            * scale
        )
        return jnp.stack((grad_query, grad_key, grad_value), axis=0).astype(jnp.bfloat16)

    grad_pairs = lax.map(
        one_pair,
        (
            head_pairs(triple_group[:, 0]),
            head_pairs(triple_group[:, 1]),
            head_pairs(triple_group[:, 2]),
            logsum,
            head_pairs(grad_mixed.reshape(GROUP, H, HD)),
        ),
    )
    return grad_pairs.transpose(2, 1, 0, 3, 4).reshape(GROUP, 3 * H * HD)


def gather_dense(first, second, third, fourth, fifth, sixth):
    first, second, third, fourth, fifth, sixth = (
        lax.all_gather(first, "fsdp", axis=0, tiled=True),
        lax.all_gather(second, "fsdp", axis=0, tiled=True),
        lax.all_gather(third, "fsdp", axis=0, tiled=True),
        lax.all_gather(fourth, "fsdp", axis=0, tiled=True),
        lax.all_gather(fifth, "fsdp", axis=0, tiled=True),
        lax.all_gather(sixth, "fsdp", axis=0, tiled=True),
    )
    return (
        lax.all_gather(first, "exp", axis=1, tiled=True),
        lax.all_gather(second, "exp", axis=1, tiled=True),
        lax.all_gather(third, "exp", axis=1, tiled=True),
        lax.all_gather(fourth, "exp", axis=1, tiled=True),
        lax.all_gather(fifth, "exp", axis=1, tiled=True),
        lax.all_gather(sixth, "exp", axis=1, tiled=True),
    )


def scatter_dense(first, second, third, fourth, fifth, sixth):
    first, second, third, fourth, fifth, sixth = (
        lax.psum_scatter(first.astype(jnp.bfloat16), "exp", scatter_dimension=1, tiled=True).astype(
            jnp.float32
        ),
        lax.psum_scatter(
            second.astype(jnp.bfloat16), "exp", scatter_dimension=1, tiled=True
        ).astype(jnp.float32),
        lax.psum_scatter(third.astype(jnp.bfloat16), "exp", scatter_dimension=1, tiled=True).astype(
            jnp.float32
        ),
        lax.psum_scatter(
            fourth.astype(jnp.bfloat16), "exp", scatter_dimension=1, tiled=True
        ).astype(jnp.float32),
        lax.psum_scatter(fifth.astype(jnp.bfloat16), "exp", scatter_dimension=1, tiled=True).astype(
            jnp.float32
        ),
        lax.psum_scatter(sixth.astype(jnp.bfloat16), "exp", scatter_dimension=1, tiled=True).astype(
            jnp.float32
        ),
    )
    return (
        lax.psum_scatter(
            first.astype(jnp.bfloat16), "fsdp", scatter_dimension=0, tiled=True
        ).astype(jnp.float32),
        lax.psum_scatter(
            second.astype(jnp.bfloat16), "fsdp", scatter_dimension=0, tiled=True
        ).astype(jnp.float32),
        lax.psum_scatter(
            third.astype(jnp.bfloat16), "fsdp", scatter_dimension=0, tiled=True
        ).astype(jnp.float32),
        lax.psum_scatter(
            fourth.astype(jnp.bfloat16), "fsdp", scatter_dimension=0, tiled=True
        ).astype(jnp.float32),
        lax.psum_scatter(
            fifth.astype(jnp.bfloat16), "fsdp", scatter_dimension=0, tiled=True
        ).astype(jnp.float32),
        lax.psum_scatter(
            sixth.astype(jnp.bfloat16), "fsdp", scatter_dimension=0, tiled=True
        ).astype(jnp.float32),
    )


def gather_experts(expert_in, expert_out):
    return (
        lax.all_gather(expert_in, "fsdp", axis=2, tiled=True),
        lax.all_gather(expert_out, "fsdp", axis=1, tiled=True),
    )


def local(
    patches,
    cond_embed,
    image_kind,
    expert_ids,
    out_grad,
    modulate_weight,
    attend_weight,
    output_weight,
    router_weight,
    shared_in,
    shared_out,
    expert_in,
    expert_out,
):
    tok_count, width = patches.shape
    blocks = tok_count // SHORT
    groups = tok_count // GROUP
    modulate_full, attend_full, output_full, router_full, upward_full, downward_full = gather_dense(
        modulate_weight, attend_weight, output_weight, router_weight, shared_in, shared_out
    )
    cond_float = cond_embed.astype(jnp.float32)
    cond_act = jax.nn.silu(cond_float).astype(jnp.bfloat16)
    modulation = jnp.dot(cond_act, modulate_full, preferred_element_type=jnp.float32).reshape(
        blocks, 1, 6, width
    )
    shift_first = modulation[:, :, 0]
    scale_first = modulation[:, :, 1]
    gate_first = modulation[:, :, 2]
    shift_second = modulation[:, :, 3]
    scale_second = modulation[:, :, 4]
    gate_second = modulation[:, :, 5]
    inputs = patches.astype(jnp.float32).reshape(blocks, SHORT, width)
    normed_first, inverse_first = layer_norm(inputs)
    attend_in = (
        (normed_first * (1.0 + scale_first) + shift_first)
        .astype(jnp.bfloat16)
        .reshape(tok_count, width)
    )
    triple = jnp.dot(attend_in, attend_full, preferred_element_type=jnp.float32).astype(
        jnp.bfloat16
    )
    triple = triple.reshape(groups, GROUP, 3, H, HD)
    attended, logsum = lax.map(attend_group, (triple, image_kind))
    attended = attended.reshape(tok_count, width)
    projected = jnp.dot(attended, output_full, preferred_element_type=jnp.float32).reshape(
        blocks, SHORT, width
    )
    residual = inputs + gate_first * projected
    normed_second, inverse_second = layer_norm(residual)
    branch_in = (
        (normed_second * (1.0 + scale_second) + shift_second)
        .astype(jnp.bfloat16)
        .reshape(tok_count, width)
    )
    logits = jnp.dot(branch_in, router_full, preferred_element_type=jnp.float32)
    gates = jax.nn.softmax(jnp.take_along_axis(logits, expert_ids, axis=1), axis=-1)
    shared_pre = jnp.dot(branch_in, upward_full, preferred_element_type=jnp.float32)
    shared_act = gelu_tanh(shared_pre).astype(jnp.bfloat16)
    shared_res = jnp.dot(shared_act, downward_full, preferred_element_type=jnp.float32)
    slots = slot_table(expert_ids)
    send_rows = (
        jnp.zeros((E, CAP, width), jnp.bfloat16)
        .at[expert_ids, slots]
        .set(jnp.broadcast_to(branch_in[:, None, :], (tok_count, TOPK, width)))
    )
    received = lax.all_to_all(send_rows, "exp", split_axis=0, concat_axis=1, tiled=True)
    up_full, down_full = gather_experts(expert_in, expert_out)
    expert_pre = jnp.einsum("erd,edf->erf", received, up_full, preferred_element_type=jnp.float32)
    expert_act = gelu_tanh(expert_pre).astype(jnp.bfloat16)
    expert_res = jnp.einsum(
        "erf,efd->erd", expert_act, down_full, preferred_element_type=jnp.float32
    ).astype(jnp.bfloat16)
    returned = lax.all_to_all(expert_res, "exp", split_axis=1, concat_axis=0, tiled=True)
    picked = returned[expert_ids, slots].astype(jnp.float32)
    mixture = jnp.sum(gates[:, :, None] * picked, axis=1)
    branch_out = (shared_res + mixture).reshape(blocks, SHORT, width)
    block_out = (residual + gate_second * branch_out).reshape(tok_count, width).astype(jnp.bfloat16)
    back_modulate, back_attend, back_output, back_router, back_upward, back_downward = gather_dense(
        modulate_weight, attend_weight, output_weight, router_weight, shared_in, shared_out
    )
    back_up, back_down = gather_experts(expert_in, expert_out)
    grad_out = out_grad.astype(jnp.float32).reshape(blocks, SHORT, width)
    grad_gate_second = jnp.sum(grad_out * branch_out, axis=1)
    grad_branch = (gate_second * grad_out).astype(jnp.bfloat16).reshape(tok_count, width)
    grad_branch_wide = grad_branch.astype(jnp.float32)
    shared_out_grad = jnp.einsum(
        "tf,td->fd", shared_act, grad_branch, preferred_element_type=jnp.float32
    )
    grad_shared_pre = (
        jnp.einsum("td,fd->tf", grad_branch, back_downward, preferred_element_type=jnp.float32)
        * gelu_slope(shared_pre)
    ).astype(jnp.bfloat16)
    shared_in_grad = jnp.einsum(
        "td,tf->df", branch_in, grad_shared_pre, preferred_element_type=jnp.float32
    )
    grad_branch_in = jnp.einsum(
        "tf,df->td", grad_shared_pre, back_upward, preferred_element_type=jnp.float32
    )
    grad_gates = jnp.sum(grad_branch_wide[:, None, :] * picked, axis=-1)
    grad_picked = (gates[:, :, None] * grad_branch_wide[:, None, :]).astype(jnp.bfloat16)
    grad_send = jnp.zeros((E, CAP, width), jnp.bfloat16).at[expert_ids, slots].set(grad_picked)
    grad_received = lax.all_to_all(grad_send, "exp", split_axis=0, concat_axis=1, tiled=True)
    expert_out_grad = jnp.einsum(
        "erf,erd->efd", expert_act, grad_received, preferred_element_type=jnp.float32
    )
    grad_expert_pre = (
        jnp.einsum("erd,efd->erf", grad_received, back_down, preferred_element_type=jnp.float32)
        * gelu_slope(expert_pre)
    ).astype(jnp.bfloat16)
    expert_in_grad = jnp.einsum(
        "erd,erf->edf", received, grad_expert_pre, preferred_element_type=jnp.float32
    )
    grad_rows = jnp.einsum(
        "erf,edf->erd", grad_expert_pre, back_up, preferred_element_type=jnp.float32
    ).astype(jnp.bfloat16)
    grad_returned = lax.all_to_all(grad_rows, "exp", split_axis=1, concat_axis=0, tiled=True)
    grad_branch_in = grad_branch_in + jnp.sum(
        grad_returned[expert_ids, slots].astype(jnp.float32), axis=1
    )
    grad_chosen = gates * (grad_gates - jnp.sum(gates * grad_gates, axis=-1, keepdims=True))
    choose = (expert_ids[:, :, None] == jnp.arange(E, dtype=jnp.int32)[None, None, :]).astype(
        jnp.float32
    )
    grad_logits = jnp.sum(choose * grad_chosen[:, :, None], axis=1).astype(jnp.bfloat16)
    router_grad = jnp.einsum(
        "td,te->de", branch_in, grad_logits, preferred_element_type=jnp.float32
    )
    grad_branch_in = grad_branch_in + jnp.einsum(
        "te,de->td", grad_logits, back_router, preferred_element_type=jnp.float32
    )
    grad_norm_in = grad_branch_in.reshape(blocks, SHORT, width)
    grad_shift_second = jnp.sum(grad_norm_in, axis=1)
    grad_scale_second = jnp.sum(grad_norm_in * normed_second, axis=1)
    grad_residual = grad_out + norm_back(
        grad_norm_in * (1.0 + scale_second), normed_second, inverse_second
    )
    grad_gate_first = jnp.sum(grad_residual * projected, axis=1)
    grad_projected = (gate_first * grad_residual).astype(jnp.bfloat16).reshape(tok_count, width)
    output_grad = jnp.einsum(
        "td,te->de", attended, grad_projected, preferred_element_type=jnp.float32
    )
    grad_attended = jnp.einsum(
        "te,de->td", grad_projected, back_output, preferred_element_type=jnp.float32
    ).astype(jnp.bfloat16)
    grad_triple = lax.map(
        attend_back, (triple, logsum, grad_attended.reshape(groups, GROUP, width), image_kind)
    )
    grad_triple = grad_triple.reshape(tok_count, 3 * width)
    attend_grad = jnp.einsum(
        "td,te->de", attend_in, grad_triple, preferred_element_type=jnp.float32
    )
    grad_attend_in = jnp.einsum(
        "te,de->td", grad_triple, back_attend, preferred_element_type=jnp.float32
    ).reshape(blocks, SHORT, width)
    grad_shift_first = jnp.sum(grad_attend_in, axis=1)
    grad_scale_first = jnp.sum(grad_attend_in * normed_first, axis=1)
    patches_grad = grad_residual + norm_back(
        grad_attend_in * (1.0 + scale_first), normed_first, inverse_first
    )
    patches_grad = patches_grad.reshape(tok_count, width)
    grad_modulation = jnp.stack(
        (
            grad_shift_first,
            grad_scale_first,
            grad_gate_first,
            grad_shift_second,
            grad_scale_second,
            grad_gate_second,
        ),
        axis=1,
    )
    grad_modulation = grad_modulation.reshape(blocks, 6 * width).astype(jnp.bfloat16)
    modulate_grad = jnp.einsum(
        "bd,be->de", cond_act, grad_modulation, preferred_element_type=jnp.float32
    )
    cond_grad = jnp.einsum(
        "be,de->bd", grad_modulation, back_modulate, preferred_element_type=jnp.float32
    ) * silu_slope(cond_float)
    modulate_grad, attend_grad, output_grad, router_grad, shared_in_grad, shared_out_grad = (
        scatter_dense(
            modulate_grad, attend_grad, output_grad, router_grad, shared_in_grad, shared_out_grad
        )
    )
    expert_in_grad, expert_out_grad = (
        lax.psum_scatter(
            expert_in_grad.astype(jnp.bfloat16), "fsdp", scatter_dimension=2, tiled=True
        ).astype(jnp.float32),
        lax.psum_scatter(
            expert_out_grad.astype(jnp.bfloat16), "fsdp", scatter_dimension=1, tiled=True
        ).astype(jnp.float32),
    )
    return (
        block_out,
        patches_grad,
        cond_grad,
        modulate_grad,
        attend_grad,
        output_grad,
        router_grad,
        shared_in_grad,
        shared_out_grad,
        expert_in_grad,
        expert_out_grad,
    )


def solution(mesh):
    in_specs = (
        P(("exp", "fsdp"), None),
        P(("exp", "fsdp"), None),
        P(("exp", "fsdp")),
        P(("exp", "fsdp"), None),
        P(("exp", "fsdp"), None),
        P("fsdp", "exp"),
        P("fsdp", "exp"),
        P("fsdp", "exp"),
        P("fsdp", "exp"),
        P("fsdp", "exp"),
        P("fsdp", "exp"),
        P("exp", None, "fsdp"),
        P("exp", "fsdp", None),
    )
    out_specs = (
        P(("exp", "fsdp"), None),
        P(("exp", "fsdp"), None),
        P(("exp", "fsdp"), None),
        P("fsdp", "exp"),
        P("fsdp", "exp"),
        P("fsdp", "exp"),
        P("fsdp", "exp"),
        P("fsdp", "exp"),
        P("fsdp", "exp"),
        P("exp", None, "fsdp"),
        P("exp", "fsdp", None),
    )
    return jax.shard_map(local, mesh=mesh, in_specs=in_specs, out_specs=out_specs, check_vma=False)
```

profile of v0, /device:TPU:0, one launch (start us, length us, event | category | flops | bytes accessed | tf_op | source)
XLA Modules:
  0.0 1964.2 jit_solution(13715575168270677484)
XLA Ops:
  9.5 49.4 %all-gather.13.cloned.1.call-done = bf16[768,1152]{1,0:T(8,128)(2,1)} async-done(((bf16[96,1152]{1,0:T(8,128)(2,1)}), bf16[768,1152]{1,0:T(8,128)(2,1)}) %all-gather.13.cloned.1.call-update) | async-done | bytes 1769488 | tf_op jit(solution)/shard_map/all_gather | solution.py:146
  58.9 34.0 %all_gather.58 = bf16[768,576]{1,0:T(8,128)(2,1)S(1)} all-gather(bf16[96,576]{1,0:T(8,128)(2,1)} %param.23), channel_id=1, replica_groups=mesh['exp'=4,'fsdp'=8] {'fsdp'}, dimensions={0}, use_global_device_ids=true | all-gather | bytes 995328 | tf_op jit(solution)/shard_map/all_gather | solution.py:147
  94.3 31.5 %all_gather.60 = bf16[768,192]{1,0:T(8,128)(2,1)S(1)} all-gather(bf16[96,192]{1,0:T(8,128)(2,1)S(1)} %copy-done.58), channel_id=1, replica_groups=mesh['exp'=4,'fsdp'=8] {'fsdp'}, dimensions={0}, use_global_device_ids=true | all-gather | bytes 331776 | tf_op jit(solution)/shard_map/all_gather | solution.py:148
  161.7 37.7 %all-gather.15.cloned.1.call-done = bf16[768,4608]{1,0:T(8,128)(2,1)} async-done(((bf16[768,1152]{1,0:T(8,128)(2,1)}), bf16[768,4608]{1,0:T(8,128)(2,1)}) %all-gather.15.cloned.1.call-update) | async-done | bytes 7077904 | tf_op jit(solution)/shard_map/all_gather | solution.py:154
  205.5 26.7 %all-gather.17.cloned.1.call-done = bf16[768,2304]{0,1:T(8,128)(2,1)} async-done(((bf16[768,576]{0,1:T(8,128)(2,1)}), bf16[768,2304]{0,1:T(8,128)(2,1)}) %all-gather.17.cloned.1.call-update) | async-done | bytes 3538960 | tf_op jit(solution)/shard_map/all_gather | solution.py:155
  250.5 58.1 %while.40 = (s32[]{:T(128)}, bf16[6,1024,2,64]{1,3,2,0:T(8,128)(2,1)}, f32[6,2,1024]{2,1,0:T(2,128)}, bf16[6,1024,2,64]{1,3,2,0:T(8,128)(2,1)}, bf16[6,1024,2,64...) while((s32[]{:T(128)}, ...), condition=%wide.region_5.6_spmd.clone, body=%wide.region_2.5_spmd.clone.sunk | while | flops 564262912 | bytes 30480988 | solution.py:86
  407.3 23.8 %all-gather.29.cloned.1.call-done = bf16[2,768,3072]{2,1,0:T(8,128)(2,1)} async-done(((bf16[2,768,384]{2,1,0:T(8,128)(2,1)}), bf16[2,768,3072]{2,1,0:T(8,128)(2,1)}) %all-gather.29.cloned.1.call-update) | async-done | bytes 9437200 | tf_op jit(solution)/shard_map/all_gather | solution.py:208
  449.6 120.0 %all-gather.31.cloned.1.call-done = bf16[2,3072,768]{2,1,0:T(8,128)(2,1)} async-done(((bf16[2,384,768]{2,1,0:T(8,128)(2,1)}), bf16[2,3072,768]{2,1,0:T(8,128)(2,1)}) %all-gather.31.cloned.1.call-update) | async-done | bytes 9437200 | tf_op jit(solution)/shard_map/all_gather | solution.py:209
  623.7 42.9 %all-to-all-done.1 = bf16[2,1152,768]{2,0,1:T(2,128)(2,1)S(1)} async-done(((bf16[2,1152,768]{2,0,1:T(2,128)(2,1)}), bf16[2,1152,768]{2,0,1:T(2,128)(2,1)S(1)}, u32[]{:S(2)}, u32[]{:S(2)}) %all-to-all-start.1) | async-done | bytes 3538976 | tf_op jit(solution)/shard_map/all_to_all | solution.py:286
  671.0 27.4 %gather_fusion = bf16[2048,768]{1,0:T(8,128)(2,1)} fusion(bf16[8,288,768]{2,1,0:T(8,128)(2,1)S(1)} %bitcast.307, s32[2048]{0:T(1024)S(1)} %copy-done), kind=kCustom, calls=%fused_computation | custom fusion | bytes 6307840 | tf_op jit(solution)/shard_map/gather | solution.py:287
  772.5 33.5 %all-to-all-done.2 = bf16[8,288,768]{2,1,0:T(8,128)(2,1)} async-done(((bf16[8,288,768]{2,1,0:T(8,128)(2,1)}), bf16[8,288,768]{2,1,0:T(8,128)(2,1)}, u32[]{:S(2)}, u32[]{:S(2)}) %all-to-all-start.2) | async-done | bytes 3538976 | tf_op jit(solution)/shard_map/all_to_all | solution.py:315
  808.4 32.7 %fusion.73 = bf16[2,1152,3072]{2,1,0:T(8,128)(2,1)} fusion(f32[2,1152,3072]{2,1,0:T(8,128)} %fusion.133, bf16[2,1152,768]{2,1,0:T(8,128)(2,1)S(1)} %bitcast.329, bf16[2,3072,768]{2,1,0:T(8,128)(2,1)} %all-gather.31.cloned.1.call-done), kind=kOutput, calls=%fused_computation.87 | convolution fusion | flops 11006115840 | bytes 55443456 | tf_op jit(solution)/shard_map/erd,efd->erf/dot_general | solution.py:320
  895.7 25.8 %all-to-all-done.3 = bf16[2,1152,768]{2,0,1:T(2,128)(2,1)S(1)} async-done(((bf16[2,1152,768]{2,0,1:T(2,128)(2,1)}), bf16[2,1152,768]{2,0,1:T(2,128)(2,1)S(1)}, u32[]{:S(2)}, u32[]{:S(2)}) %all-to-all-start.3) | async-done | bytes 3538976 | tf_op jit(solution)/shard_map/all_to_all | solution.py:329
  925.8 27.4 %gather_fusion.1 = bf16[2048,768]{1,0:T(8,128)(2,1)} fusion(bf16[8,288,768]{2,1,0:T(8,128)(2,1)S(1)} %bitcast.306, s32[2048]{0:T(1024)S(1)} %copy-done), kind=kCustom, calls=%fused_computation.1 | custom fusion | bytes 6307840 | tf_op jit(solution)/shard_map/gather | solution.py:331
  997.4 115.7 %while.41 = (s32[]{:T(128)}, bf16[6,3,1024,2,64]{2,4,3,0,1:T(8,128)(2,1)}, bf16[6,1024,2,64]{1,3,2,0:T(8,128)(2,1)}, bf16[6,1024,2,64]{1,3,2,0:T(8,128)(2,1)}, f...) while((s32[]{:T(128)}, ...), condition=%wide.region_24.25_spmd.clone, body=%wide.region_22.24_spmd.clone.sunk | while | flops 1378744320 | bytes 71368808 | solution.py:131
  1199.2 23.9 %copy.249 = bf16[2,768,3072]{1,0,2:T(2,128)(2,1)} copy(bf16[2,768,3072]{2,1,0:T(8,128)(2,1)} %convolution_convert_fusion.2) | data formatting | bytes 18874368
  1259.2 29.9 %reduce-scatter.46.cloned.1.call-done = bf16[96,2]{1,0:T(8,128)(2,1)} async-done(((bf16[768,2]{1,0:T(8,128)(2,1)}), bf16[96,2]{1,0:T(8,128)(2,1)}) %reduce-scatter.46.cloned.1.call-update) | async-done | bytes 400
  1298.5 58.7 %reduce-scatter.48.cloned.1.call-done = bf16[384,192]{1,0:T(8,128)(2,1)} async-done(((bf16[3072,192]{1,0:T(8,128)(2,1)}), bf16[384,192]{1,0:T(8,128)(2,1)}) %reduce-scatter.48.cloned.1.call-update) | async-done | bytes 147472
  1359.0 64.4 %reduce-scatter.34.cloned.1.call-done = bf16[96,768]{1,0:T(8,128)(2,1)} async-done(((bf16[768,768]{1,0:T(8,128)(2,1)}), bf16[96,768]{1,0:T(8,128)(2,1)}) %reduce-scatter.34.cloned.1.call-update) | async-done | bytes 147472 | tf_op jit(solution)/shard_map/reduce_scatter | solution.py:197
  1425.1 62.6 %reduce-scatter.44.cloned.1.call-done = bf16[96,192]{1,0:T(8,128)(2,1)} async-done(((bf16[768,192]{1,0:T(8,128)(2,1)}), bf16[96,192]{1,0:T(8,128)(2,1)}) %reduce-scatter.44.cloned.1.call-update) | async-done | bytes 36880
  1489.3 64.6 %reduce-scatter.42.cloned.1.call-done = bf16[96,576]{1,0:T(8,128)(2,1)} async-done(((bf16[768,576]{1,0:T(8,128)(2,1)}), bf16[96,576]{1,0:T(8,128)(2,1)}) %reduce-scatter.42.cloned.1.call-update) | async-done | bytes 110608
  1555.8 164.5 %reduce-scatter.50.cloned.1.call-done = bf16[384,1536]{1,0:T(8,128)(2,1)} async-done(((bf16[3072,1536]{1,0:T(8,128)(2,1)}), bf16[384,1536]{1,0:T(8,128)(2,1)}) %reduce-scatter.50.cloned.1.call-update) | async-done | bytes 1179664
  1726.7 160.2 %reduce-scatter.38.cloned.1.call-done = bf16[2,384,768]{2,1,0:T(8,128)(2,1)} async-done(((bf16[2,3072,768]{2,1,0:T(8,128)(2,1)}), bf16[2,384,768]{2,1,0:T(8,128)(2,1)}) %reduce-scatter.38.cloned.1.call-update) | async-done | bytes 1179664 | tf_op jit(solution)/shard_map/reduce_scatter | solution.py:401
  1889.7 66.1 %reduce-scatter.26.cloned.1.call-done = bf16[96,1152]{1,0:T(8,128)(2,1)} async-done(((bf16[768,1152]{1,0:T(8,128)(2,1)}), bf16[96,1152]{1,0:T(8,128)(2,1)}) %reduce-scatter.26.cloned.1.call-update) | async-done | bytes 221200 | tf_op jit(solution)/shard_map/reduce_scatter | solution.py:185
  (426 shorter events, 739.8 us)
Async XLA Ops:
  7.9 118.8 %all-gather.21.cloned.1.call-start = ((), (), s32[]{:S(2)}) async-start(), calls=%async_computation.21 | async-start | bytes 1327104 | tf_op jit(solution)/shard_map/all_gather | solution.py:150
  8.7 153.0 %all-gather.25.cloned.1.call-start = ((), (), s32[]{:S(2)}) async-start(), calls=%async_computation.23 | async-start | bytes 1327104 | tf_op jit(solution)/shard_map/all_gather | solution.py:151
  9.4 190.0 %all-gather.15.cloned.1.call-start = ((), (), s32[]{:S(2)}) async-start(), calls=%async_computation.18 | async-start | bytes 8847360 | tf_op jit(solution)/shard_map/all_gather | solution.py:154
  58.9 173.3 %all-gather.17.cloned.1.call-start = ((), (), s32[]{:S(2)}) async-start(), calls=%async_computation.19 | async-start | bytes 4423680 | tf_op jit(solution)/shard_map/all_gather | solution.py:155
  94.2 218.9 %all-gather.19.cloned.1.call-start = ((), (), s32[]{:S(2)}) async-start(), calls=%async_computation.20 | async-start | bytes 1474560 | tf_op jit(solution)/shard_map/all_gather | solution.py:156
  126.6 237.3 %all-gather.23.cloned.1.call-start = ((), (), s32[]{:S(2)}) async-start(), calls=%async_computation.22 | async-start | bytes 5898240 | tf_op jit(solution)/shard_map/all_gather | solution.py:158
  127.4 303.7 %all-gather.29.cloned.1.call-start = ((), (), s32[]{:S(2)}) async-start(), calls=%async_computation.25 | async-start | bytes 10616832 | tf_op jit(solution)/shard_map/all_gather | solution.py:208
  128.1 441.4 %all-gather.31.cloned.1.call-start = ((), (), s32[]{:S(2)}) async-start(), calls=%async_computation.26 | async-start | bytes 10616832 | tf_op jit(solution)/shard_map/all_gather | solution.py:209
  128.9 478.4 %all-gather.27.cloned.1.call-start = ((), (), s32[]{:S(2)}) async-start(), calls=%async_computation.24 | async-start | bytes 5898240 | tf_op jit(solution)/shard_map/all_gather | solution.py:159
  363.7 805.8 %reduce-scatter.36.cloned.1.call-start = ((), (), s32[]{:S(2)}) async-start(), calls=%async_computation.32 | async-start | bytes 5898240 | tf_op jit(solution)/shard_map/reduce_scatter | solution.py:180
  603.4 63.3 %all-to-all-start.1 = ((bf16[2,1152,768]{2,0,1:T(2,128)(2,1)}), bf16[2,1152,768]{2,0,1:T(2,128)(2,1)S(1)}, u32[]{:S(2)}, u32[]{:S(2)}) async-start(bf16[2,1152,768]{2,0,1:T(2,128)(2,1)} %copy.219), calls=%async_computation.1 | async-start | bytes 7077888 | tf_op jit(solution)/shard_map/all_to_all | solution.py:286
  747.1 59.0 %all-to-all-start.2 = ((bf16[8,288,768]{2,1,0:T(8,128)(2,1)}), bf16[8,288,768]{2,1,0:T(8,128)(2,1)}, u32[]{:S(2)}, u32[]{:S(2)}) async-start(bf16[8,288,768]{2,1,0:T(8,128)(2,1)} %bitcast.322), calls=%async_computation.2 | async-start | bytes 7077888 | tf_op jit(solution)/shard_map/all_to_all | solution.py:315
  751.9 420.4 %reduce-scatter.32.cloned.1.call-start = ((), (), s32[]{:S(2)}) async-start(), calls=%async_computation.30 | async-start | bytes 5898240 | tf_op jit(solution)/shard_map/reduce_scatter | solution.py:177
  880.4 292.6 %reduce-scatter.30.cloned.1.call-start = ((), (), s32[]{:S(2)}) async-start(), calls=%async_computation.29 | async-start | bytes 1474560 | tf_op jit(solution)/shard_map/reduce_scatter | solution.py:171
  994.6 180.3 %reduce-scatter.28.cloned.1.call-start = ((), (), s32[]{:S(2)}) async-start(), calls=%async_computation.28 | async-start | bytes 4423680 | tf_op jit(solution)/shard_map/reduce_scatter | solution.py:168
  1120.8 134.4 %reduce-scatter.40.cloned.1.call-start = ((), (), s32[]{:S(2)}) async-start(), calls=%async_computation.34 | async-start | bytes 8847360
  1156.2 132.8 %reduce-scatter.46.cloned.1.call-start = ((), (), s32[]{:S(2)}) async-start(), calls=%async_computation.37 | async-start | bytes 221184
  1169.4 187.8 %reduce-scatter.48.cloned.1.call-start = ((), (), s32[]{:S(2)}) async-start(), calls=%async_computation.38 | async-start | bytes 1769472
  1172.3 251.2 %reduce-scatter.34.cloned.1.call-start = ((), (), s32[]{:S(2)}) async-start(), calls=%async_computation.31 | async-start | bytes 1327104 | tf_op jit(solution)/shard_map/reduce_scatter | solution.py:197
  1172.9 314.8 %reduce-scatter.44.cloned.1.call-start = ((), (), s32[]{:S(2)}) async-start(), calls=%async_computation.36 | async-start | bytes 442368
  1174.9 379.0 %reduce-scatter.42.cloned.1.call-start = ((), (), s32[]{:S(2)}) async-start(), calls=%async_computation.35 | async-start | bytes 1105920
  1177.2 543.1 %reduce-scatter.50.cloned.1.call-start = ((), (), s32[]{:S(2)}) async-start(), calls=%async_computation.39 | async-start | bytes 10616832
  1232.2 654.6 %reduce-scatter.38.cloned.1.call-start = ((), (), s32[]{:S(2)}) async-start(), calls=%async_computation.33 | async-start | bytes 10616832 | tf_op jit(solution)/shard_map/reduce_scatter | solution.py:401
  1255.2 700.6 %reduce-scatter.26.cloned.1.call-start = ((), (), s32[]{:S(2)}) async-start(), calls=%async_computation.27 | async-start | bytes 1990656 | tf_op jit(solution)/shard_map/reduce_scatter | solution.py:185
  (70 other events, 1229.0 us)
Sparse Core Ops, SparseCore 0:
  10.2 48.6 all-gather.12
  61.0 44.8 all-gather.20
  108.0 40.2 all-gather.24
  149.7 49.6 all-gather.14
  201.4 30.7 all-gather.16
  234.2 17.4 all-gather.18
  253.2 37.4 all-gather.22
  292.8 138.2 all-gather.28
  433.2 136.2 all-gather.30
  571.0 35.6 all-gather.26
  609.2 65.9 reduce-scatter.35
  761.7 58.0 reduce-scatter.31
  994.7 21.8 reduce-scatter.29
  1121.0 36.5 reduce-scatter.27
  1159.9 63.9 reduce-scatter.39
  1227.9 61.0 reduce-scatter.45
  1293.3 63.8 reduce-scatter.47
  1360.5 62.9 reduce-scatter.33
  1427.3 60.3 reduce-scatter.43
  1491.4 62.4 reduce-scatter.41
  1557.9 162.2 reduce-scatter.49
  1724.3 162.5 reduce-scatter.37
  1890.7 65.0 reduce-scatter.25
where the time goes:
time: 1970 us; the launch traced here: 1960 us
  waiting for transfers between devices  1050 us (53%)
  matrix products  387 us (20%)
  local copies, waits for them, and re-layouts  279 us (14%)
  other arithmetic  111 us (6%)
  blocking collectives  98.7 us (5%)
    unnamed x29, waiting for transfers between devices  385 us
    reduce_scatter x1, waiting for transfers between devices, local(): lax.psum_scatter(expert_out_grad.astype(jnp.bfloat16), 'fsdp', scatter_di...  160 us
    all_gather x1, waiting for transfers between devices, gather_experts(): lax.all_gather(expert_out, 'fsdp', axis=1, tiled=True)  120 us
    unnamed x168, local copies, waits for them, and re-layouts  102 us
    reduce_scatter x1, waiting for transfers between devices, scatter_dense(): lax.psum_scatter(first.astype(jnp.bfloat16), 'fsdp', scatter_dimension=0,...  66.1 us
    reduce_scatter x1, waiting for transfers between devices, scatter_dense(): lax.psum_scatter(fifth.astype(jnp.bfloat16), 'fsdp', scatter_dimension=0,...  64.4 us
    all_gather x1, waiting for transfers between devices, gather_dense(): lax.all_gather(first, 'fsdp', axis=0, tiled=True)  49.4 us
    all_to_all x1, waiting for transfers between devices, local(): lax.all_to_all(expert_res, 'exp', split_axis=1, concat_axis=0, tiled=True)  42.9 us
  transfers between devices with their start and end apart: 27, of which 17 were waited for; matrix products, arithmetic and copies ran while one was open for 39% of the time, Pallas kernels for 0%

commit v1 on v0

v1 whole, which is shorter than its diff:
```python
import jax
import jax.numpy as jnp
from jax import lax
from jax.experimental import pallas as pl
from jax.experimental.pallas import tpu as pltpu
from jax.sharding import Mesh
from jax.sharding import PartitionSpec as P

H = 12
HD = 64
E = 8
TOPK = 2
SHORT = 256
GROUP = 1024
CAP = 288
RING_MOST = 8

F32 = jnp.float32
BF16 = jnp.bfloat16

eps_norm = 1e-06
tanh_gain = 0.7978845608028654
ALL = ("exp", "zi", "yi")


def layer_norm(values):
    centered = values - jnp.mean(values, axis=-1, keepdims=True)
    inverse = lax.rsqrt(jnp.mean(centered * centered, axis=-1, keepdims=True) + eps_norm)
    return (centered * inverse, inverse)


def norm_back(grad, normed, inverse):
    return inverse * (
        grad
        - jnp.mean(grad, axis=-1, keepdims=True)
        - normed * jnp.mean(grad * normed, axis=-1, keepdims=True)
    )


def gelu_tanh(values):
    return jax.nn.gelu(values, approximate=True)


def gelu_slope(values):
    hyper = jnp.tanh(tanh_gain * (values + 0.044715 * values * values * values))
    return 0.5 * (1.0 + hyper) + 0.5 * values * (1.0 - hyper * hyper) * tanh_gain * (
        1.0 + 3.0 * 0.044715 * values * values
    )


def silu_slope(values):
    sigma = jax.nn.sigmoid(values)
    return sigma * (1.0 + values * (1.0 - sigma))


def dot(left, right, dims):
    return lax.dot_general(left, right, (dims, ((), ())), preferred_element_type=F32)


def mm(left, right):
    return dot(left, right, ((1,), (0,)))


def mm_rt(left, right):
    return dot(left, right, ((1,), (1,)))


def mm_lt(left, right):
    return dot(left, right, ((0,), (0,)))


def slot_table(expert_ids):
    flat = expert_ids.reshape(-1)
    onehot = (flat[:, None] == jnp.arange(E, dtype=jnp.int32)[None, :]).astype(jnp.int32)
    before = jnp.cumsum(onehot, axis=0) - onehot
    return jnp.sum(before * onehot, axis=1).reshape(expert_ids.shape)


LOG2E = 1.4426950408889634
SCORE = HD ** (-0.5)


def attend_kernel(kind_ref, query_ref, key_ref, value_ref, mixed_ref, logsum_ref):
    left = lax.broadcasted_iota(jnp.int32, (GROUP, 2 * HD), 1) < HD
    keys = key_ref[...]
    zero = jnp.zeros_like(keys)
    split_keys = (jnp.where(left, keys, zero), jnp.where(left, zero, keys))

    def rows_of(part, first, count):
        rows = pl.ds(part * SHORT, SHORT)
        query = query_ref[rows, :]
        value = value_ref[pl.ds(first, count), :]
        halves = []
        for half in range(2):
            scores = mm_rt(query, split_keys[half][first : first + count])
            peak = jnp.max(scores, axis=1, keepdims=True)
            weights = jnp.exp2((scores - peak) * (SCORE * LOG2E))
            total = jnp.sum(weights, axis=1, keepdims=True)
            halves.append(mm(weights.astype(BF16), value) / total)
            logsum = peak * (SCORE * LOG2E) + jnp.log2(total)
            logsum_ref[0, 0, half, rows] = jnp.transpose(
                jnp.broadcast_to(logsum, (SHORT, 2 * HD))
            )[0]
        mixed_ref[rows, :] = jnp.where(left[:SHORT], halves[0], halves[1]).astype(BF16)

    is_long = kind_ref[pl.program_id(0)] == 1

    @pl.when(is_long)
    def _():
        for part in range(GROUP // SHORT):
            rows_of(part, 0, GROUP)

    @pl.when(jnp.logical_not(is_long))
    def _():
        for part in range(GROUP // SHORT):
            rows_of(part, part * SHORT, SHORT)


def attend(triple, image_kind):
    groups = triple.shape[0] // GROUP
    pairs = H // 2

    def part(offset):
        return pl.BlockSpec((GROUP, 2 * HD), lambda g, i, kind: (g, offset + i))

    return pl.pallas_call(
        attend_kernel,
        out_shape=(
            jax.ShapeDtypeStruct((triple.shape[0], H * HD), BF16),
            jax.ShapeDtypeStruct((groups, pairs, 8, GROUP), F32),
        ),
        grid_spec=pltpu.PrefetchScalarGridSpec(
            num_scalar_prefetch=1,
            grid=(groups, pairs),
            in_specs=[part(0), part(pairs), part(2 * pairs)],
            out_specs=(
                part(0),
                pl.BlockSpec((1, 1, 8, GROUP), lambda g, i, kind: (g, i, 0, 0)),
            ),
        ),
        compiler_params=pltpu.CompilerParams(vmem_limit_bytes=32 << 20),
        name="attend",
    )(image_kind, triple, triple, triple)


def attend_back_kernel(
    kind_ref,
    query_ref,
    key_ref,
    value_ref,
    mixed_ref,
    grad_ref,
    logsum_ref,
    grads_ref,
    key_sum,
    value_sum,
):
    left = lax.broadcasted_iota(jnp.int32, (GROUP, 2 * HD), 1) < HD

    def split(values):
        zero = jnp.zeros_like(values)
        return (jnp.where(left, values, zero), jnp.where(left, zero, values))

    split_query = split(query_ref[...])
    split_keys = split(key_ref[...])
    split_values = split(value_ref[...])
    split_grad = split(grad_ref[...])
    outer = jnp.transpose(mixed_ref[...].astype(F32) * grad_ref[...].astype(F32))
    inner = (
        jnp.sum(outer[:HD], axis=0, keepdims=True),
        jnp.sum(outer[HD:], axis=0, keepdims=True),
    )

    def rows_of(part, first, count, fresh):
        low, high = part * SHORT, (part + 1) * SHORT
        keys_at = pl.ds(first, count)
        query = query_ref[pl.ds(low, SHORT), :]
        grad = grad_ref[pl.ds(low, SHORT), :]
        key_part = value_part = query_part = None
        for half in range(2):
            keys = split_keys[half][first : first + count]
            scores = mm_rt(keys, query)
            logsum = logsum_ref[0, 0, half : half + 1, low:high]
            attention = jnp.exp2(scores * (SCORE * LOG2E) - logsum)
            moved = mm_rt(split_values[half][first : first + count], grad)
            grad_scores = (attention * (moved - inner[half][:, low:high])).astype(BF16)
            value_add = mm(attention.astype(BF16), split_grad[half][low:high])
            key_add = mm(grad_scores, split_query[half][low:high])
            query_add = mm_lt(grad_scores, keys)
            if half == 0:
                key_part, value_part, query_part = key_add, value_add, query_add
            else:
                key_part, value_part = key_part + key_add, value_part + value_add
                query_part = query_part + query_add
        grads_ref[0, pl.ds(low, SHORT), :] = (query_part * SCORE).astype(BF16)
        if fresh:
            key_sum[keys_at, :] = key_part
            value_sum[keys_at, :] = value_part
        else:
            key_sum[keys_at, :] += key_part
            value_sum[keys_at, :] += value_part

    is_long = kind_ref[pl.program_id(0)] == 1

    @pl.when(is_long)
    def _():
        for part in range(GROUP // SHORT):
            rows_of(part, 0, GROUP, part == 0)

    @pl.when(jnp.logical_not(is_long))
    def _():
        for part in range(GROUP // SHORT):
            rows_of(part, part * SHORT, SHORT, True)

    grads_ref[1, :, :] = (key_sum[...] * SCORE).astype(BF16)
    grads_ref[2, :, :] = value_sum[...].astype(BF16)


def attend_back(triple, attended, logsum, grad_attended, image_kind):
    groups = triple.shape[0] // GROUP
    pairs = H // 2

    def part(offset):
        return pl.BlockSpec((GROUP, 2 * HD), lambda g, i, kind: (g, offset + i))

    return pl.pallas_call(
        attend_back_kernel,
        out_shape=jax.ShapeDtypeStruct((3, triple.shape[0], H * HD), BF16),
        grid_spec=pltpu.PrefetchScalarGridSpec(
            num_scalar_prefetch=1,
            grid=(groups, pairs),
            in_specs=[
                part(0),
                part(pairs),
                part(2 * pairs),
                part(0),
                part(0),
                pl.BlockSpec((1, 1, 8, GROUP), lambda g, i, kind: (g, i, 0, 0)),
            ],
            out_specs=pl.BlockSpec((3, GROUP, 2 * HD), lambda g, i, kind: (0, g, i)),
            scratch_shapes=[pltpu.VMEM((GROUP, 2 * HD), F32)] * 2,
        ),
        compiler_params=pltpu.CompilerParams(vmem_limit_bytes=32 << 20),
        name="attend_back",
    )(image_kind, triple, triple, triple, attended, grad_attended, logsum)


class Ring:
    def __init__(self, mesh):
        self.n_exp = mesh.shape["exp"]
        self.n_ring = mesh.shape["zi"]
        self.n_pair = mesh.shape["yi"]
        self.bits = []
        bit = self.n_exp // 2
        while bit:
            self.bits.append(bit)
            bit //= 2
        self.direct = self.n_ring <= RING_MOST

    def step(self, value):
        n = self.n_ring
        return lax.ppermute(value, "zi", [(i, (i + 1) % n) for i in range(n)])

    def swap(self, value):
        return lax.ppermute(value, "yi", [(0, 1), (1, 0)])

    def cross(self, value, bit):
        return lax.ppermute(value, "exp", [(i, i ^ bit) for i in range(self.n_exp)])

    def place(self):
        return (lax.axis_index("exp"), lax.axis_index("zi"), lax.axis_index("yi"))

    def gather(self, block):
        e, z, y = self.place()
        rows, cols = block.shape
        if not self.direct:
            whole = lax.all_gather(block, ("zi", "yi"), axis=0, tiled=False)
            return lax.all_gather(whole, "exp", axis=0, tiled=False)
        n = self.n_ring
        held, pieces = block, [block]
        for _ in range(n - 1):
            held = self.step(held)
            pieces.append(held)
        stacked = jnp.stack(pieces, axis=0)
        order = (z - jnp.arange(n, dtype=jnp.int32)) % n
        held = jnp.take(stacked, order, axis=0)
        if self.n_pair == 2:
            other = self.swap(held)
            held = jnp.stack(
                (jnp.where(y == 0, held, other), jnp.where(y == 0, other, held)), axis=1
            )
        held = held.reshape(1, n * self.n_pair, rows, cols)
        for bit in self.bits:
            other = self.cross(held, bit)
            low = (e & bit) == 0
            held = jnp.stack((jnp.where(low, held, other), jnp.where(low, other, held)), axis=1)
            held = held.reshape(held.shape[0] * 2, n * self.n_pair, rows, cols)
        return held

    def scatter(self, blocks):
        e, z, y = self.place()
        rows, cols = blocks.shape[2:]
        if not self.direct:
            part = lax.psum_scatter(blocks, "exp", scatter_dimension=0, tiled=True)
            part = part.reshape(-1, rows, cols)
            part = lax.psum_scatter(part, ("zi", "yi"), scatter_dimension=0, tiled=True)
            return part.reshape(rows, cols).astype(F32)
        held = blocks
        for bit in reversed(self.bits):
            half = held.reshape(held.shape[0] // 2, 2, *held.shape[1:])
            mine = ((e & bit) != 0).astype(jnp.int32)
            keep = lax.dynamic_index_in_dim(half, mine, 1, keepdims=False)
            give = lax.dynamic_index_in_dim(half, 1 - mine, 1, keepdims=False)
            held = (keep.astype(F32) + self.cross(give, bit).astype(F32)).astype(BF16)
        held = held.reshape(self.n_ring, self.n_pair, rows, cols)
        if self.n_pair == 2:
            keep = lax.dynamic_index_in_dim(held, y, 1, keepdims=False)
            give = lax.dynamic_index_in_dim(held, 1 - y, 1, keepdims=False)
            held = (keep.astype(F32) + self.swap(give).astype(F32)).astype(BF16)
        else:
            held = held[:, 0]
        n = self.n_ring
        own = [
            lax.dynamic_index_in_dim(held, (z - 1 - k) % n, 0, keepdims=False) for k in range(n)
        ]
        moving = own[0].astype(F32)
        for k in range(1, n):
            moving = own[k].astype(F32) + self.step(moving.astype(BF16)).astype(F32)
        return moving


def local(
    ring,
    patches,
    cond_embed,
    image_kind,
    expert_ids,
    out_grad,
    modulate_weight,
    attend_weight,
    output_weight,
    router_weight,
    shared_in,
    shared_out,
    expert_in,
    expert_out,
):
    tok_count, width = patches.shape
    blocks = tok_count // SHORT
    n_exp, n_ring, n_pair = ring.n_exp, ring.n_ring, ring.n_pair
    n_fsdp = n_ring * n_pair
    n_all = n_exp * n_fsdp
    e, z, y = ring.place()
    kept = expert_in.shape[0] // n_pair
    mod_rows, mod_cols = modulate_weight.shape

    cond_float = cond_embed.astype(F32)
    cond_act = jax.nn.silu(cond_float).astype(BF16)
    cond_send = cond_act.reshape(blocks, n_fsdp, mod_rows).transpose(1, 0, 2)
    cond_send = jnp.broadcast_to(cond_send[None], (n_exp, n_fsdp, blocks, mod_rows))
    cond_all = lax.all_to_all(
        cond_send.reshape(n_all, blocks, mod_rows), ALL, 0, 0, tiled=True
    ).reshape(n_all * blocks, mod_rows)
    mod_part = mm(cond_all, modulate_weight).reshape(n_all, blocks, mod_cols)
    mod_part = lax.all_to_all(mod_part, ALL, 0, 0, tiled=True)
    modulation = jnp.sum(mod_part.reshape(n_exp, n_fsdp, blocks, mod_cols), axis=1)
    modulation = modulation.transpose(1, 0, 2).reshape(blocks, 1, 6, width)

    attend_blocks = ring.gather(attend_weight)
    attend_full = attend_blocks.reshape(n_exp, width, -1).transpose(1, 0, 2).reshape(width, -1)
    output_blocks = ring.gather(output_weight)
    output_full = output_blocks.reshape(n_exp, width, -1).transpose(1, 0, 2).reshape(width, -1)
    router_blocks = lax.all_to_all(
        jnp.broadcast_to(router_weight[None], (n_all,) + router_weight.shape),
        ALL,
        0,
        0,
        tiled=True,
    )
    router_full = (
        router_blocks.reshape(n_exp, width, -1).transpose(1, 0, 2).reshape(width, E)
    )
    upward_blocks = ring.gather(shared_in)
    upward_full = upward_blocks.reshape(n_exp, width, -1).transpose(1, 0, 2).reshape(width, -1)
    downward_blocks = ring.gather(shared_out)
    hidden = shared_out.shape[0] * n_fsdp
    downward_full = (
        downward_blocks.reshape(n_exp, hidden, -1).transpose(1, 0, 2).reshape(hidden, width)
    )

    if n_pair == 2:
        own_in = jnp.where(y == 0, expert_in[0], expert_in[1])
        give_in = jnp.where(y == 0, expert_in[1], expert_in[0])
        own_out = jnp.where(y == 0, expert_out[0], expert_out[1])
        give_out = jnp.where(y == 0, expert_out[1], expert_out[0])
        up_block = jnp.concatenate((own_in, ring.swap(give_in)), axis=1)
        down_block = jnp.concatenate((own_out, ring.swap(give_out)), axis=0)
    else:
        up_block, down_block = expert_in[0], expert_out[0]
    if ring.direct:
        ups, downs = [up_block], [down_block]
        for _ in range(n_ring - 1):
            ups.append(ring.step(ups[-1]))
            downs.append(ring.step(downs[-1]))
        ups, downs = ups[1:] + ups[:1], downs[1:] + downs[:1]
    else:
        ups = [lax.all_gather(up_block, "zi", axis=1, tiled=True)]
        downs = [lax.all_gather(down_block, "zi", axis=0, tiled=True)]

    shift_first = modulation[:, :, 0]
    scale_first = modulation[:, :, 1]
    gate_first = modulation[:, :, 2]
    shift_second = modulation[:, :, 3]
    scale_second = modulation[:, :, 4]
    gate_second = modulation[:, :, 5]
    inputs = patches.astype(F32).reshape(blocks, SHORT, width)
    normed_first, inverse_first = layer_norm(inputs)
    attend_in = (
        (normed_first * (1.0 + scale_first) + shift_first).astype(BF16).reshape(tok_count, width)
    )
    triple = mm(attend_in, attend_full).astype(BF16)
    attended, logsum = attend(triple, image_kind)
    projected = mm(attended, output_full).reshape(blocks, SHORT, width)
    residual = inputs + gate_first * projected
    normed_second, inverse_second = layer_norm(residual)
    branch_in = (
        (normed_second * (1.0 + scale_second) + shift_second)
        .astype(BF16)
        .reshape(tok_count, width)
    )
    logits = mm(branch_in, router_full)
    choose = expert_ids[:, :, None] == jnp.arange(E, dtype=jnp.int32)[None, None, :]
    choose = choose.astype(F32)
    gates = jax.nn.softmax(jnp.sum(choose * logits[:, None, :], axis=-1), axis=-1)

    grad_out = out_grad.astype(F32).reshape(blocks, SHORT, width)
    grad_branch = (gate_second * grad_out).astype(BF16).reshape(tok_count, width)
    grad_branch_wide = grad_branch.astype(F32)

    slots = slot_table(expert_ids)
    target = expert_ids * CAP + slots
    row_of = jnp.arange(E * CAP, dtype=jnp.int32)[:, None]
    pick0 = (row_of == target[None, :, 0]).astype(BF16)
    pick1 = (row_of == target[None, :, 1]).astype(BF16)
    send_rows = mm(pick0 + pick1, branch_in).astype(BF16).reshape(E, CAP, width)
    received = lax.all_to_all(send_rows, ("exp", "yi"), 0, 0, tiled=True)
    received = received.reshape(-1, width)
    grad_picked = (gates[:, :, None] * grad_branch_wide[:, None, :]).astype(BF16)
    grad_send = (
        (mm(pick0, grad_picked[:, 0]) + mm(pick1, grad_picked[:, 1]))
        .astype(BF16)
        .reshape(E, CAP, width)
    )
    grad_received = lax.all_to_all(grad_send, ("exp", "yi"), 0, 0, tiled=True)
    grad_received = grad_received.reshape(-1, width)

    shared_pre = mm(branch_in, upward_full)
    shared_act = gelu_tanh(shared_pre).astype(BF16)
    shared_res = mm(shared_act, downward_full)
    shared_out_grad = mm_lt(shared_act, grad_branch).astype(BF16)
    grad_shared_pre = (mm_rt(grad_branch, downward_full) * gelu_slope(shared_pre)).astype(BF16)
    shared_in_grad = mm_lt(branch_in, grad_shared_pre).astype(BF16)
    grad_branch_in = mm_rt(grad_shared_pre, upward_full)

    expert_res = 0.0
    pres, acts = [], []
    for up, down in zip(ups, downs):
        pre = mm(received, up)
        act = gelu_tanh(pre).astype(BF16)
        expert_res = expert_res + mm(act, down)
        pres.append(pre)
        acts.append(act)
    expert_res = expert_res.astype(BF16).reshape(E, CAP, width)
    returned = lax.all_to_all(expert_res, ("exp", "yi"), 0, 0, tiled=True).reshape(-1, width)
    grad_rows = 0.0
    grad_ups, grad_downs = [], []
    for up, down, pre, act in zip(ups, downs, pres, acts):
        grad_pre = (mm_rt(grad_received, down) * gelu_slope(pre)).astype(BF16)
        grad_rows = grad_rows + mm_rt(grad_pre, up)
        grad_downs.append(mm_lt(act, grad_received))
        grad_ups.append(mm_lt(received, grad_pre))
    grad_rows = grad_rows.astype(BF16).reshape(E, CAP, width)
    grad_returned = lax.all_to_all(grad_rows, ("exp", "yi"), 0, 0, tiled=True)
    grad_returned = grad_returned.reshape(-1, width)

    if ring.direct:
        up_sum, down_sum = grad_ups[0], grad_downs[0]
        for k in range(1, n_ring):
            up_sum = grad_ups[k] + ring.step(up_sum.astype(BF16)).astype(F32)
            down_sum = grad_downs[k] + ring.step(down_sum.astype(BF16)).astype(F32)
    else:
        up_sum = lax.psum_scatter(
            grad_ups[0].astype(BF16), "zi", scatter_dimension=1, tiled=True
        ).astype(F32)
        down_sum = lax.psum_scatter(
            grad_downs[0].astype(BF16), "zi", scatter_dimension=0, tiled=True
        ).astype(F32)
    if n_pair == 2:
        slice_cols = up_sum.shape[1] // 2
        own_up, give_up = up_sum[:, :slice_cols], up_sum[:, slice_cols:]
        own_down, give_down = down_sum[:slice_cols], down_sum[slice_cols:]
        got_up = ring.swap(give_up.astype(BF16)).astype(F32)
        got_down = ring.swap(give_down.astype(BF16)).astype(F32)
        expert_in_grad = jnp.stack(
            (jnp.where(y == 0, own_up, got_up), jnp.where(y == 0, got_up, own_up))
        )
        expert_out_grad = jnp.stack(
            (jnp.where(y == 0, own_down, got_down), jnp.where(y == 0, got_down, own_down))
        )
    else:
        expert_in_grad, expert_out_grad = up_sum[None], down_sum[None]

    picked0 = mm_lt(pick0, returned)
    picked1 = mm_lt(pick1, returned)
    mixture = gates[:, 0:1] * picked0 + gates[:, 1:2] * picked1
    branch_out = (shared_res + mixture).reshape(blocks, SHORT, width)
    block_out = (residual + gate_second * branch_out).reshape(tok_count, width).astype(BF16)
    grad_gate_second = jnp.sum(grad_out * branch_out, axis=1)
    grad_gates = jnp.stack(
        (
            jnp.sum(grad_branch_wide * picked0, axis=-1),
            jnp.sum(grad_branch_wide * picked1, axis=-1),
        ),
        axis=1,
    )
    grad_chosen = gates * (grad_gates - jnp.sum(gates * grad_gates, axis=-1, keepdims=True))
    grad_logits = jnp.sum(choose * grad_chosen[:, :, None], axis=1).astype(BF16)
    router_grad = mm_lt(branch_in, grad_logits)
    grad_branch_in = (
        grad_branch_in + mm_lt(pick0 + pick1, grad_returned) + mm_rt(grad_logits, router_full)
    )
    grad_norm_in = grad_branch_in.reshape(blocks, SHORT, width)
    grad_shift_second = jnp.sum(grad_norm_in, axis=1)
    grad_scale_second = jnp.sum(grad_norm_in * normed_second, axis=1)
    grad_residual = grad_out + norm_back(
        grad_norm_in * (1.0 + scale_second), normed_second, inverse_second
    )
    grad_gate_first = jnp.sum(grad_residual * projected, axis=1)
    grad_projected = (gate_first * grad_residual).astype(BF16).reshape(tok_count, width)
    output_grad = mm_lt(attended, grad_projected).astype(BF16)
    grad_attended = mm_rt(grad_projected, output_full).astype(BF16)
    grad_triple = attend_back(triple, attended, logsum, grad_attended, image_kind)
    grad_triple = grad_triple.transpose(1, 0, 2).reshape(tok_count, 3 * width)
    attend_grad = mm_lt(attend_in, grad_triple).astype(BF16)
    grad_attend_in = mm_rt(grad_triple, attend_full).reshape(blocks, SHORT, width)
    grad_shift_first = jnp.sum(grad_attend_in, axis=1)
    grad_scale_first = jnp.sum(grad_attend_in * normed_first, axis=1)
    patches_grad = grad_residual + norm_back(
        grad_attend_in * (1.0 + scale_first), normed_first, inverse_first
    )
    patches_grad = patches_grad.reshape(tok_count, width)

    grad_modulation = jnp.stack(
        (
            grad_shift_first,
            grad_scale_first,
            grad_gate_first,
            grad_shift_second,
            grad_scale_second,
            grad_gate_second,
        ),
        axis=1,
    )
    grad_modulation = grad_modulation.reshape(blocks, n_exp, mod_cols).astype(BF16)
    mod_send = jnp.broadcast_to(
        grad_modulation.transpose(1, 0, 2)[:, None], (n_exp, n_fsdp, blocks, mod_cols)
    )
    mod_all = lax.all_to_all(
        mod_send.reshape(n_all, blocks, mod_cols), ALL, 0, 0, tiled=True
    ).reshape(n_all * blocks, mod_cols)
    modulate_grad = mm_lt(cond_all, mod_all)
    cond_part = mm_rt(mod_all, modulate_weight).reshape(n_all, blocks, mod_rows)
    cond_part = lax.all_to_all(cond_part, ALL, 0, 0, tiled=True)
    cond_grad = jnp.sum(cond_part.reshape(n_exp, n_fsdp, blocks, mod_rows), axis=0)
    cond_grad = cond_grad.transpose(1, 0, 2).reshape(blocks, width) * silu_slope(cond_float)

    def dense(grad, shard):
        rows, cols = shard.shape
        return ring.scatter(
            grad.reshape(n_fsdp, rows, n_exp, cols).transpose(2, 0, 1, 3).astype(BF16)
        )

    shared_out_grad = dense(shared_out_grad, shared_out)
    shared_in_grad = dense(shared_in_grad, shared_in)
    output_grad = dense(output_grad, output_weight)
    attend_grad = dense(attend_grad, attend_weight)
    router_parts = router_grad.reshape(n_fsdp, mod_rows, n_exp, -1).transpose(2, 0, 1, 3)
    router_parts = router_parts.reshape(n_all, mod_rows, -1)
    router_grad = jnp.sum(lax.all_to_all(router_parts, ALL, 0, 0, tiled=True), axis=0)
    return (
        block_out,
        patches_grad,
        cond_grad,
        modulate_grad,
        attend_grad,
        output_grad,
        router_grad,
        shared_in_grad,
        shared_out_grad,
        expert_in_grad,
        expert_out_grad,
    )


def solution(mesh):
    n_exp, n_fsdp = mesh.shape["exp"], mesh.shape["fsdp"]
    n_pair = E // n_exp
    if n_pair not in (1, 2) or n_fsdp % n_pair:
        raise ValueError("unsupported mesh")
    fine = Mesh(mesh.devices.reshape(n_exp, n_fsdp // n_pair, n_pair), ALL)
    ring = Ring(fine)
    fsdp = ("zi", "yi")
    in_specs = (
        P(ALL, None),
        P(ALL, None),
        P(ALL),
        P(ALL, None),
        P(ALL, None),
        P(fsdp, "exp"),
        P(fsdp, "exp"),
        P(fsdp, "exp"),
        P(fsdp, "exp"),
        P(fsdp, "exp"),
        P(fsdp, "exp"),
        P("exp", None, fsdp),
        P("exp", fsdp, None),
    )
    out_specs = (
        P(ALL, None),
        P(ALL, None),
        P(ALL, None),
        P(fsdp, "exp"),
        P(fsdp, "exp"),
        P(fsdp, "exp"),
        P(fsdp, "exp"),
        P(fsdp, "exp"),
        P(fsdp, "exp"),
        P("exp", None, fsdp),
        P("exp", fsdp, None),
    )

    def step(*args):
        return local(ring, *args)

    return jax.shard_map(step, mesh=fine, in_specs=in_specs, out_specs=out_specs, check_vma=False)
```

time: 1970 us -> 1030 us (0.52)
  waiting for transfers between devices: 1050 us -> 265 us
  starting transfers between devices: 19.3 us -> 153 us
  local copies, waits for them, and re-layouts: 279 us -> 159 us
  blocking collectives: 98.7 us -> 0 us
  matrix products: 387 us -> 308 us
  Pallas kernels: 0 us -> 28.4 us
    unnamed x29 -> x0, waiting for transfers between devices: 385 us -> none
    reduce_scatter x7 -> x0, waiting for transfers between devices: 291 us -> none  [the longest x1 160 us: local(): lax.psum_scatter(expert_out_grad.astype(jnp.bfloat16), 'fsdp', scatter_di...]
    all_gather x10 -> x0, waiting for transfers between devices: 258 us -> none  [the longest x1 120 us: gather_experts(): lax.all_gather(expert_out, 'fsdp', axis=1, tiled=True)]
    ppermute x0 -> x64, waiting for transfers between devices: none -> 242 us  [the longest x36 99.6 us: step(): return lax.ppermute(value, 'zi', [(i, (i + 1) % n) for i in range(n)])]
    all_to_all x4 -> x10, waiting for transfers between devices: 119 us -> 22.4 us  [the longest x1 13.5 us: local(): cond_part = lax.all_to_all(cond_part, ALL, 0, 0, tiled=True)]
    all_gather x4 -> x0, blocking collectives: 88.6 us -> none  [the longest x1 34 us: gather_dense(): lax.all_gather(second, 'fsdp', axis=0, tiled=True)]
    ppermute x0 -> x64, starting transfers between devices: none -> 84.3 us  [the longest x36 44.9 us: step(): return lax.ppermute(value, 'zi', [(i, (i + 1) % n) for i in range(n)])]
    dot_general x66 -> x48, matrix products: 387 us -> 308 us  [dot(): lax.dot_general(left, right, (dims, ((), ())), preferred_element_type=F32)]
  transfers between devices with their start and end apart: 27 -> 74, of which waited for: 17 -> 27; matrix products, arithmetic and copies ran while one was open for 39% -> 49% of each run, Pallas kernels for 0% -> 3%
where the time goes in v1:
time: 1030 us; the launch traced here: 1020 us
  matrix products  308 us (30%)
  waiting for transfers between devices  265 us (26%)
  local copies, waits for them, and re-layouts  159 us (15%)
  starting transfers between devices  153 us (15%)
  other arithmetic  102 us (10%)
  Pallas kernels  28.4 us (3%)
    dot_general x48, matrix products, dot(): lax.dot_general(left, right, (dims, ((), ())), preferred_element_type=F32)  308 us
    ppermute x36, waiting for transfers between devices, step(): return lax.ppermute(value, 'zi', [(i, (i + 1) % n) for i in range(n)])  99.6 us
    ppermute x12, waiting for transfers between devices, swap(): return lax.ppermute(value, 'yi', [(0, 1), (1, 0)])  77.2 us
    ppermute x16, waiting for transfers between devices, cross(): return lax.ppermute(value, 'exp', [(i, i ^ bit) for i in range(self.n_exp)])  65.5 us
    ppermute x36, starting transfers between devices, step(): return lax.ppermute(value, 'zi', [(i, (i + 1) % n) for i in range(n)])  44.9 us
    reshape x6, local copies, waits for them, and re-layouts, dense(): grad.reshape(n_fsdp, rows, n_exp, cols).transpose(2, 0, 1, 3).astype(BF16)  28.6 us
    unnamed x262, local copies, waits for them, and re-layouts  25.9 us
    dot_general x6, local copies, waits for them, and re-layouts, dot(): lax.dot_general(left, right, (dims, ((), ())), preferred_element_type=F32)  25.7 us
  transfers between devices with their start and end apart: 74, of which 27 were waited for; matrix products, arithmetic and copies ran while one was open for 49% of the time, Pallas kernels for 3%

profile of v1, /device:TPU:0, one launch (start us, length us, event | category | flops | bytes accessed | tf_op | source)
XLA Modules:
  0.0 1018.8 jit_solution(2369467574089423446)
XLA Ops:
  72.7 19.6 %collective-permute-done.10 = bf16[1,8,96,192]{3,2,1,0:T(8,128)(2,1)} collective-permute-done((bf16[1,8,96,192]{3,2,1,0:T(8,128)(2,1)S(1)}, bf16[1,8,96,192]{3,2,1,0:T(8,128)(2,1)}, u32[]{:S(2)}, u32[]{:S(2)}) %collective-permute-start.10) | collective-permute-done | bytes 294944 | tf_op jit(solution)/shard_map/ppermute | solution.py:268
  145.2 11.2 %attend.1 = (bf16[1024,768]{1,0:T(8,128)(2,1)S(1)}, f32[1,6,8,1024]{3,2,1,0:T(8,128)S(1)}) custom-call(s32[1]{0:T(128)S(6)} %copy.398.kind_ref, bf16[1024,2304]{1,0:T(8,128)(2,1)S(1)} %convolution_convert_fusion.query_ref.key_ref.value_ref, bf16[1024,2304]{1,0:T(8,128)(2,1)S(1)} %convolution_convert_fusion.query_ref.key_ref.value_ref, ...), custom_call_target="tpu_custom_call" | custom-call | tf_op jit(solution)/shard_map/attend/pallas_call | solution.py:126
  173.1 18.3 %all-to-all-start.3 = ((bf16[8,288,768]{2,1,0:T(8,128)(2,1)}), bf16[8,288,768]{2,1,0:T(8,128)(2,1)}, u32[]{:S(2)}, u32[]{:S(2)}) async-start(bf16[8,288,768]{2,1,0:T(8,128)(2,1)} %bitcast.530), calls=%async_computation.3 | async-start | bytes 7077888 | tf_op jit(solution)/shard_map/all_to_all | solution.py:446
  203.0 42.1 %collective-permute-done.21 = bf16[4,384,192]{1,2,0:T(8,128)(2,1)S(1)} collective-permute-done((bf16[4,384,192]{1,2,0:T(8,128)(2,1)S(1)}, bf16[4,384,192]{1,2,0:T(8,128)(2,1)S(1)}, u32[]{:S(2)}, u32[]{:S(2)}) %collective-permute-start.21) | collective-permute-done | bytes 589856 | tf_op jit(solution)/shard_map/ppermute | solution.py:265
  260.3 22.8 %collective-permute-done.22 = bf16[1,8,384,192]{2,3,1,0:T(8,128)(2,1)S(1)} collective-permute-done((bf16[1,8,384,192]{2,3,1,0:T(8,128)(2,1)S(1)}, bf16[1,8,384,192]{2,3,1,0:T(8,128)(2,1)S(1)}, u32[]{:S(2)}, u32[]{:S(2)}) %collective-permute-start.22) | collective-permute-done | bytes 1179680 | tf_op jit(solution)/shard_map/ppermute | solution.py:268
  289.9 13.3 %collective-permute-done.29 = bf16[768,768]{1,0:T(8,128)(2,1)} collective-permute-done((bf16[768,768]{1,0:T(8,128)(2,1)S(1)}, bf16[768,768]{1,0:T(8,128)(2,1)}, u32[]{:S(2)}, u32[]{:S(2)}) %collective-permute-start.29) | collective-permute-done | bytes 1179680 | tf_op jit(solution)/shard_map/ppermute | solution.py:262
  355.8 9.7 add_convert_fusion.2
  402.5 10.5 %fusion.169 = f32[1024,3072]{1,0:T(8,128)} fusion(bf16[1024,768]{1,0:T(8,128)(2,1)S(1)} %bitcast.499, bf16[768,3072]{0,1:T(8,128)(2,1)} %bitcast.508), kind=kOutput, calls=%fused_computation.374 | convolution fusion | flops 4831838208 | bytes 18874368 | tf_op jit(solution)/shard_map/dot_general | solution.py:57
  419.5 9.4 multiply_reduce_fusion.6
  464.5 12.7 %fusion.14 = bf16[1024,3072]{1,0:T(8,128)(2,1)S(1)} fusion(f32[1024,3072]{1,0:T(8,128)} %fusion.169, bf16[1024,768]{1,0:T(8,128)(2,1)S(1)} %copy-done.48, bf16[3072,768]{0,1:T(8,128)(2,1)S(1)} %bitcast.515), kind=kOutput, calls=%fused_computation.21 | convolution fusion | flops 4891607040 | bytes 25165824 | tf_op jit(solution)/shard_map/dot_general | solution.py:57
  486.8 9.7 reshape.585
  521.2 15.7 %multiply_reduce_fusion = (bf16[4,768]{1,0:T(4,128)(2,1)}, f32[1024,768]{1,0:T(8,128)}, f32[1024,768]{1,0:T(8,128)}) fusion(bf16[1024,768]{1,0:T(8,128)(2,1)} %param.17, f32[1024,768]{1,0:T(8,128)} %copy-done.97, f32[1024]{0:T(1024)S(1)} %bitcast.577, f32[1024,768]{1,0:T(8,128)} %get-tuple-element.76, f32[1024]{0:T(1024)S(1)} %bitcast.576, ...), kind=kOutput, calls=%fused_computation.140 | convolution fusion | flops 4865651712 | bytes 31471616 | tf_op jit(solution)/shard_map/dot_general | solution.py:57
  571.6 9.1 fusion.153
  580.7 9.2 fusion.150
  628.8 9.4 fusion.73
  681.9 18.8 %collective-permute-done.46 = bf16[4,96,768]{2,1,0:T(8,128)(2,1)} collective-permute-done((bf16[4,96,768]{2,1,0:T(8,128)(2,1)}, bf16[4,96,768]{2,1,0:T(8,128)(2,1)}, u32[]{:S(2)}, u32[]{:S(2)}) %collective-permute-start.46) | collective-permute-done | bytes 589856 | tf_op jit(solution)/shard_map/ppermute | solution.py:265
  721.6 47.0 %collective-permute-done.54 = bf16[384,192]{0,1:T(8,128)(2,1)S(1)} collective-permute-done((bf16[384,192]{0,1:T(8,128)(2,1)S(1)}, bf16[384,192]{0,1:T(8,128)(2,1)S(1)}, u32[]{:S(2)}, u32[]{:S(2)}) %collective-permute-start.54) | collective-permute-done | bytes 147488 | tf_op jit(solution)/shard_map/ppermute | solution.py:262
  807.2 17.1 %attend_back.1 = bf16[3,1024,768]{2,1,0:T(8,128)(2,1)S(1)} custom-call(s32[1]{0:T(128)S(6)} %copy.398.kind_ref, bf16[1024,2304]{1,0:T(8,128)(2,1)S(1)} %bitcast.477, bf16[1024,2304]{1,0:T(8,128)(2,1)S(1)} %bitcast.477, bf16[1024,2304]{1,0:T(8,128)(2,1)S(1)} %bitcast.477, bf16[1024,768]{1,0:T(8,128)(2,1)S(1)} %copy-done.4, ...), custom_call_target="tpu_custom_call" | custom-call | tf_op jit(solution)/shard_map/attend_back/pallas_call | solution.py:226
  846.4 12.3 %collective-permute-start.38 = (bf16[2,8,96,192]{3,2,1,0:T(8,128)(2,1)}, bf16[2,8,96,192]{3,2,1,0:T(8,128)(2,1)}, u32[]{:S(2)}, u32[]{:S(2)}) collective-permute-start(bf16[2,8,96,192]{3,2,1,0:T(8,128)(2,1)} %dynamic-slice_bitcast_fusion.3), channel_id=1, source_target_pairs={{0,8},{8,0},{16,24},{24,16},{1,9},{9,1},{17,25},{25,17},{2,10},{10... | collective-permute-start | bytes 1769480 | tf_op jit(solution)/shard_map/ppermute | solution.py:268
  882.1 13.1 %reshape.649 = bf16[4,256,2304]{2,1,0:T(8,128)(2,1)} reshape(bf16[1024,3,768]{2,1,0:T(4,128)(2,1)} %copy.356) | data formatting | bytes 9437184 | tf_op jit(solution)/shard_map/dot_general | solution.py:57
  895.2 9.6 multiply_reduce_fusion.9
  905.8 13.2 %all-to-all-start.7 = ((bf16[32,4,1152]{2,1,0:T(4,128)(2,1)}), bf16[32,4,1152]{2,1,0:T(4,128)(2,1)S(1)}, u32[]{:S(2)}, u32[]{:S(2)}) async-start(bf16[32,4,1152]{2,1,0:T(4,128)(2,1)} %bitcast.115), calls=%async_computation.7 | async-start | bytes 589824 | tf_op jit(solution)/shard_map/all_to_all | solution.py:568
  942.1 13.5 %all-to-all-done.8 = f32[32,4,96]{2,1,0:T(4,128)S(1)} async-done(((f32[32,4,96]{2,1,0:T(4,128)}), f32[32,4,96]{2,1,0:T(4,128)S(1)}, u32[]{:S(2)}, u32[]{:S(2)}) %all-to-all-start.8) | async-done | bytes 49184 | tf_op jit(solution)/shard_map/all_to_all | solution.py:573
  968.6 16.4 %collective-permute-done.33 = bf16[1,8,96,576]{3,2,1,0:T(8,128)(2,1)S(1)} collective-permute-done((bf16[1,8,96,576]{3,2,1,0:T(8,128)(2,1)S(1)}, bf16[1,8,96,576]{3,2,1,0:T(8,128)(2,1)S(1)}, u32[]{:S(2)}, u32[]{:S(2)}) %collective-permute-start.33) | collective-permute-done | bytes 884768 | tf_op jit(solution)/shard_map/ppermute | solution.py:268
  (627 shorter events, 631.0 us)
Async XLA Ops:
  6.8 56.1 %all-to-all-start = ((bf16[32,4,96]{2,1,0:T(4,128)(2,1)}), bf16[32,4,96]{2,1,0:T(4,128)(2,1)S(1)}, u32[]{:S(2)}, u32[]{:S(2)}) async-start(bf16[32,4,96]{2,1,0:T(4,128)(2,1)} %bitcast.2), calls=%async_computation | async-start | bytes 65536 | tf_op jit(solution)/shard_map/all_to_all | solution.py:361
  13.7 181.1 %collective-permute-start.24 = (bf16[768,384]{1,0:T(8,128)(2,1)}, bf16[768,384]{1,0:T(8,128)(2,1)}, u32[]{:S(2)}, u32[]{:S(2)}) collective-permute-start(bf16[768,384]{1,0:T(8,128)(2,1)} %get-tuple-element.55), channel_id=1, source_target_pairs={{0,1},{1,0},{2,3},{3,2},{4,5},{5,4},{6,7},{7,6},{8,9},{9,8},{10,11... | collective-permute-start | bytes 1769480 | tf_op jit(solution)/shard_map/ppermute | solution.py:265
  64.3 60.0 %all-to-all-start.1 = ((f32[32,4,1152]{2,1,0:T(4,128)}), f32[32,4,1152]{2,1,0:T(4,128)}, u32[]{:S(2)}, u32[]{:S(2)}) async-start(f32[32,4,1152]{2,1,0:T(4,128)} %copy.314), calls=%async_computation.1 | async-start | bytes 1179648 | tf_op jit(solution)/shard_map/all_to_all | solution.py:365
  100.0 98.9 %collective-permute-start.26 = (bf16[384,768]{1,0:T(8,128)(2,1)}, bf16[384,768]{1,0:T(8,128)(2,1)}, u32[]{:S(2)}, u32[]{:S(2)}) collective-permute-start(bf16[384,768]{1,0:T(8,128)(2,1)} %get-tuple-element.57), channel_id=1, source_target_pairs={{0,1},{1,0},{2,3},{3,2},{4,5},{5,4},{6,7},{7,6},{8,9},{9,8},{10,11... | collective-permute-start | bytes 1769480 | tf_op jit(solution)/shard_map/ppermute | solution.py:265
  108.8 91.3 %collective-permute-start.15 = (bf16[4,96,768]{2,1,0:T(8,128)(2,1)}, bf16[4,96,768]{2,1,0:T(8,128)(2,1)}, u32[]{:S(2)}, u32[]{:S(2)}) collective-permute-start(bf16[4,96,768]{2,1,0:T(8,128)(2,1)} %broadcast_select_fusion.1), channel_id=1, source_target_pairs={{0,1},{1,0},{2,3},{3,2},{4,5},{5,4},{6,7},{7,6},{8,9},{9,8},{10,11... | collective-permute-start | bytes 1769480 | tf_op jit(solution)/shard_map/ppermute | solution.py:265
  173.1 132.0 %all-to-all-start.3 = ((bf16[8,288,768]{2,1,0:T(8,128)(2,1)}), bf16[8,288,768]{2,1,0:T(8,128)(2,1)}, u32[]{:S(2)}, u32[]{:S(2)}) async-start(bf16[8,288,768]{2,1,0:T(8,128)(2,1)} %bitcast.530), calls=%async_computation.3 | async-start | bytes 7077888 | tf_op jit(solution)/shard_map/all_to_all | solution.py:446
  201.5 56.8 %collective-permute-start.16 = (bf16[1,8,96,768]{3,2,1,0:T(8,128)(2,1)S(1)}, bf16[1,8,96,768]{3,2,1,0:T(8,128)(2,1)S(1)}, u32[]{:S(2)}, u32[]{:S(2)}) collective-permute-start(bf16[1,8,96,768]{3,2,1,0:T(8,128)(2,1)S(1)} %bitcast.504), channel_id=1, source_target_pairs={{0,16},{8,24},{16,0},{24,8},{1,17},{9,25},{17,1},{25,9},{2,18},{10... | collective-permute-start | bytes 3538952 | tf_op jit(solution)/shard_map/ppermute | solution.py:268
  260.3 113.6 %collective-permute-start.17 = (bf16[2,8,96,768]{3,2,1,0:T(8,128)(2,1)}, bf16[2,8,96,768]{3,2,1,0:T(8,128)(2,1)}, u32[]{:S(2)}, u32[]{:S(2)}) collective-permute-start(bf16[2,8,96,768]{3,2,1,0:T(8,128)(2,1)} %maximum_bitcast_fusion), channel_id=1, source_target_pairs={{0,8},{8,0},{16,24},{24,16},{1,9},{9,1},{17,25},{25,17},{2,10},{10... | collective-permute-start | bytes 7077896 | tf_op jit(solution)/shard_map/ppermute | solution.py:268
  286.0 100.1 %collective-permute-start.23 = (bf16[2,8,384,192]{2,3,1,0:T(8,128)(2,1)}, bf16[2,8,384,192]{2,3,1,0:T(8,128)(2,1)}, u32[]{:S(2)}, u32[]{:S(2)}) collective-permute-start(bf16[2,8,384,192]{2,3,1,0:T(8,128)(2,1)} %maximum_bitcast_fusion.1), channel_id=1, source_target_pairs={{0,8},{8,0},{16,24},{24,16},{1,9},{9,1},{17,25},{25,17},{2,10},{10... | collective-permute-start | bytes 7077896 | tf_op jit(solution)/shard_map/ppermute | solution.py:268
  286.0 58.0 %collective-permute-start.30 = (bf16[768,768]{1,0:T(8,128)(2,1)}, bf16[768,768]{1,0:T(8,128)(2,1)}, u32[]{:S(2)}, u32[]{:S(2)}) collective-permute-start(bf16[768,768]{1,0:T(8,128)(2,1)} %collective-permute-done.28), channel_id=1, source_target_pairs={{0,2},{2,4},{4,6},{6,0},{1,3},{3,5},{5,7},{7,1},{8,10},{10,12},{12... | collective-permute-start | bytes 3538952 | tf_op jit(solution)/shard_map/ppermute | solution.py:262
  305.7 59.8 %all-to-all-start.2 = ((bf16[32,96,2]{1,2,0:T(2,128)(2,1)}), bf16[32,96,2]{1,2,0:T(2,128)(2,1)S(1)}, u32[]{:S(2)}, u32[]{:S(2)}) async-start(bf16[32,96,2]{1,2,0:T(2,128)(2,1)} %broadcast_in_dim.86), calls=%async_computation.2 | async-start | bytes 32768 | tf_op jit(solution)/shard_map/all_to_all | solution.py:373
  464.0 82.3 %collective-permute-start.50 = (bf16[2,8,384,192]{2,3,1,0:T(8,128)(2,1)}, bf16[2,8,384,192]{2,3,1,0:T(8,128)(2,1)}, u32[]{:S(2)}, u32[]{:S(2)}) collective-permute-start(bf16[2,8,384,192]{2,3,1,0:T(8,128)(2,1)} %dynamic-slice_bitcast_fusion), channel_id=1, source_target_pairs={{0,8},{8,0},{16,24},{24,16},{1,9},{9,1},{17,25},{25,17},{2,10},{10... | collective-permute-start | bytes 7077896 | tf_op jit(solution)/shard_map/ppermute | solution.py:268
  550.7 109.5 %collective-permute-start.51 = (bf16[1,8,384,192]{2,3,1,0:T(8,128)(2,1)}, bf16[1,8,384,192]{2,3,1,0:T(8,128)(2,1)}, u32[]{:S(2)}, u32[]{:S(2)}) collective-permute-start(bf16[1,8,384,192]{2,3,1,0:T(8,128)(2,1)} %constant_dynamic-slice_fusion), channel_id=1, source_target_pairs={{0,16},{8,24},{16,0},{24,8},{1,17},{9,25},{17,1},{25,9},{2,18},{10... | collective-permute-start | bytes 3538952 | tf_op jit(solution)/shard_map/ppermute | solution.py:268
  557.6 106.0 %collective-permute-start.45 = (bf16[1,8,96,768]{3,2,1,0:T(8,128)(2,1)}, bf16[1,8,96,768]{3,2,1,0:T(8,128)(2,1)}, u32[]{:S(2)}, u32[]{:S(2)}) collective-permute-start(bf16[1,8,96,768]{3,2,1,0:T(8,128)(2,1)} %constant_dynamic-slice_fusion.1), channel_id=1, source_target_pairs={{0,16},{8,24},{16,0},{24,8},{1,17},{9,25},{17,1},{25,9},{2,18},{10... | collective-permute-start | bytes 3538952 | tf_op jit(solution)/shard_map/ppermute | solution.py:268
  589.9 113.1 %collective-permute-start.60 = (bf16[768,768]{1,0:T(8,128)(2,1)}, bf16[768,768]{1,0:T(8,128)(2,1)}, u32[]{:S(2)}, u32[]{:S(2)}) collective-permute-start(bf16[768,768]{1,0:T(8,128)(2,1)} %convolution_convert_fusion.6), channel_id=1, source_target_pairs={{0,2},{2,4},{4,6},{6,0},{1,3},{3,5},{5,7},{7,1},{8,10},{10,12},{12... | collective-permute-start | bytes 3538952 | tf_op jit(solution)/shard_map/ppermute | solution.py:262
  605.6 108.1 %collective-permute-start.56 = (bf16[768,768]{1,0:T(8,128)(2,1)}, bf16[768,768]{1,0:T(8,128)(2,1)}, u32[]{:S(2)}, u32[]{:S(2)}) collective-permute-start(bf16[768,768]{1,0:T(8,128)(2,1)} %convolution_convert_fusion.7), channel_id=1, source_target_pairs={{0,2},{2,4},{4,6},{6,0},{1,3},{3,5},{5,7},{7,1},{8,10},{10,12},{12... | collective-permute-start | bytes 3538952 | tf_op jit(solution)/shard_map/ppermute | solution.py:262
  675.3 108.9 %all-to-all-start.6 = ((bf16[8,288,768]{2,1,0:T(8,128)(2,1)}), bf16[8,288,768]{2,1,0:T(8,128)(2,1)}, u32[]{:S(2)}, u32[]{:S(2)}) async-start(bf16[8,288,768]{2,1,0:T(8,128)(2,1)} %bitcast.495), calls=%async_computation.6 | async-start | bytes 7077888 | tf_op jit(solution)/shard_map/all_to_all | solution.py:483
  710.9 69.0 %collective-permute-start.61 = (bf16[768,768]{1,0:T(8,128)(2,1)S(1)}, bf16[768,768]{1,0:T(8,128)(2,1)S(1)}, u32[]{:S(2)}, u32[]{:S(2)}) collective-permute-start(bf16[768,768]{1,0:T(8,128)(2,1)S(1)} %add_convert_fusion.6), channel_id=1, source_target_pairs={{0,2},{2,4},{4,6},{6,0},{1,3},{3,5},{5,7},{7,1},{8,10},{10,12},{12... | collective-permute-start | bytes 3538952 | tf_op jit(solution)/shard_map/ppermute | solution.py:262
  719.1 62.1 %collective-permute-start.57 = (bf16[768,768]{1,0:T(8,128)(2,1)S(1)}, bf16[768,768]{1,0:T(8,128)(2,1)S(1)}, u32[]{:S(2)}, u32[]{:S(2)}) collective-permute-start(bf16[768,768]{1,0:T(8,128)(2,1)S(1)} %add_convert_fusion.8), channel_id=1, source_target_pairs={{0,2},{2,4},{4,6},{6,0},{1,3},{3,5},{5,7},{7,1},{8,10},{10,12},{12... | collective-permute-start | bytes 3538952 | tf_op jit(solution)/shard_map/ppermute | solution.py:262
  781.2 142.6 %collective-permute-start.62 = (bf16[768,768]{1,0:T(8,128)(2,1)}, bf16[768,768]{1,0:T(8,128)(2,1)}, u32[]{:S(2)}, u32[]{:S(2)}) collective-permute-start(bf16[768,768]{1,0:T(8,128)(2,1)} %add_convert_fusion.5), channel_id=1, source_target_pairs={{0,2},{2,4},{4,6},{6,0},{1,3},{3,5},{5,7},{7,1},{8,10},{10,12},{12... | collective-permute-start | bytes 3538952 | tf_op jit(solution)/shard_map/ppermute | solution.py:262
  782.5 145.6 %collective-permute-start.58 = (bf16[768,768]{1,0:T(8,128)(2,1)}, bf16[768,768]{1,0:T(8,128)(2,1)}, u32[]{:S(2)}, u32[]{:S(2)}) collective-permute-start(bf16[768,768]{1,0:T(8,128)(2,1)} %add_convert_fusion.7), channel_id=1, source_target_pairs={{0,2},{2,4},{4,6},{6,0},{1,3},{3,5},{5,7},{7,1},{8,10},{10,12},{12... | collective-permute-start | bytes 3538952 | tf_op jit(solution)/shard_map/ppermute | solution.py:262
  846.4 84.5 %collective-permute-start.38 = (bf16[2,8,96,192]{3,2,1,0:T(8,128)(2,1)}, bf16[2,8,96,192]{3,2,1,0:T(8,128)(2,1)}, u32[]{:S(2)}, u32[]{:S(2)}) collective-permute-start(bf16[2,8,96,192]{3,2,1,0:T(8,128)(2,1)} %dynamic-slice_bitcast_fusion.3), channel_id=1, source_target_pairs={{0,8},{8,0},{16,24},{24,16},{1,9},{9,1},{17,25},{25,17},{2,10},{10... | collective-permute-start | bytes 1769480 | tf_op jit(solution)/shard_map/ppermute | solution.py:268
  881.2 77.5 %collective-permute-start.32 = (bf16[2,8,96,576]{3,2,1,0:T(8,128)(2,1)}, bf16[2,8,96,576]{3,2,1,0:T(8,128)(2,1)}, u32[]{:S(2)}, u32[]{:S(2)}) collective-permute-start(bf16[2,8,96,576]{3,2,1,0:T(8,128)(2,1)} %dynamic-slice_bitcast_fusion.2), channel_id=1, source_target_pairs={{0,8},{8,0},{16,24},{24,16},{1,9},{9,1},{17,25},{25,17},{2,10},{10... | collective-permute-start | bytes 5308424 | tf_op jit(solution)/shard_map/ppermute | solution.py:268
  930.5 55.3 %collective-permute-start.59 = (bf16[768,384]{1,0:T(8,128)(2,1)}, bf16[768,384]{1,0:T(8,128)(2,1)}, u32[]{:S(2)}, u32[]{:S(2)}) collective-permute-start(bf16[768,384]{1,0:T(8,128)(2,1)} %slice.141), channel_id=1, source_target_pairs={{0,1},{1,0},{2,3},{3,2},{4,5},{5,4},{6,7},{7,6},{8,9},{9,8},{10,11... | collective-permute-start | bytes 1769480 | tf_op jit(solution)/shard_map/ppermute | solution.py:265
  (175 other events, 2760.4 us)

commit v2 on v1

v2 whole, which is shorter than its diff:
```python
import functools

import jax
import jax.numpy as jnp
from jax import lax
from jax.experimental import pallas as pl
from jax.experimental.pallas import tpu as pltpu
from jax.sharding import Mesh
from jax.sharding import PartitionSpec as P

H = 12
HD = 64
E = 8
TOPK = 2
SHORT = 256
GROUP = 1024
CAP = 288

F32 = jnp.float32
BF16 = jnp.bfloat16

eps_norm = 1e-06
tanh_gain = 0.7978845608028654
ALL = ("exp", "zi", "yi")
FSDP = ("zi", "yi")

PIECES = 4
STRIPS = 8
LANES = 128
OUT_LANES = 2 * LANES


def layer_norm(values):
    centered = values - jnp.mean(values, axis=-1, keepdims=True)
    inverse = lax.rsqrt(jnp.mean(centered * centered, axis=-1, keepdims=True) + eps_norm)
    return (centered * inverse, inverse)


def norm_back(grad, normed, inverse):
    return inverse * (
        grad
        - jnp.mean(grad, axis=-1, keepdims=True)
        - normed * jnp.mean(grad * normed, axis=-1, keepdims=True)
    )


def silu_slope(values):
    sigma = jax.nn.sigmoid(values)
    return sigma * (1.0 + values * (1.0 - sigma))


def dot(left, right, dims):
    return lax.dot_general(left, right, (dims, ((), ())), preferred_element_type=F32)


def mm(left, right):
    return dot(left, right, ((1,), (0,)))


def mm_rt(left, right):
    return dot(left, right, ((1,), (1,)))


def mm_lt(left, right):
    return dot(left, right, ((0,), (0,)))


def slot_table(expert_ids):
    flat = expert_ids.reshape(-1)
    onehot = (flat[:, None] == jnp.arange(E, dtype=jnp.int32)[None, :]).astype(jnp.int32)
    before = jnp.cumsum(onehot, axis=0) - onehot
    return jnp.sum(before * onehot, axis=1).reshape(expert_ids.shape)


def cost(flops, moved):
    return pl.CostEstimate(flops=flops, transcendentals=0, bytes_accessed=moved)


def fixed(shape):
    return pl.BlockSpec(shape, lambda *_: (0,) * len(shape), pipeline_mode=pl.Buffered(1))


LOG2E = 1.4426950408889634
SCORE = HD ** (-0.5)


def attend_kernel(kind_ref, query_ref, key_ref, value_ref, mixed_ref, logsum_ref):
    left = lax.broadcasted_iota(jnp.int32, (GROUP, 2 * HD), 1) < HD
    keys = key_ref[...]
    zero = jnp.zeros_like(keys)
    split_keys = (jnp.where(left, keys, zero), jnp.where(left, zero, keys))

    def rows_of(part, first, count):
        rows = pl.ds(part * SHORT, SHORT)
        query = query_ref[rows, :]
        value = value_ref[pl.ds(first, count), :]
        halves = []
        for half in range(2):
            scores = mm_rt(query, split_keys[half][first : first + count])
            peak = jnp.max(scores, axis=1, keepdims=True)
            weights = jnp.exp2((scores - peak) * (SCORE * LOG2E))
            total = jnp.sum(weights, axis=1, keepdims=True)
            halves.append(mm(weights.astype(BF16), value) / total)
            logsum = peak * (SCORE * LOG2E) + jnp.log2(total)
            logsum_ref[0, 0, half, rows] = jnp.transpose(
                jnp.broadcast_to(logsum, (SHORT, 2 * HD))
            )[0]
        mixed_ref[rows, :] = jnp.where(left[:SHORT], halves[0], halves[1]).astype(BF16)

    is_long = kind_ref[pl.program_id(0)] == 1

    @pl.when(is_long)
    def _():
        for part in range(GROUP // SHORT):
            rows_of(part, 0, GROUP)

    @pl.when(jnp.logical_not(is_long))
    def _():
        for part in range(GROUP // SHORT):
            rows_of(part, part * SHORT, SHORT)


def attend(triple, image_kind):
    groups = triple.shape[0] // GROUP
    pairs = H // 2

    def part(offset):
        return pl.BlockSpec((GROUP, 2 * HD), lambda g, i, kind: (g, offset + i))

    return pl.pallas_call(
        attend_kernel,
        out_shape=(
            jax.ShapeDtypeStruct((triple.shape[0], H * HD), BF16),
            jax.ShapeDtypeStruct((groups, pairs, 8, GROUP), F32),
        ),
        grid_spec=pltpu.PrefetchScalarGridSpec(
            num_scalar_prefetch=1,
            grid=(groups, pairs),
            in_specs=[part(0), part(pairs), part(2 * pairs)],
            out_specs=(
                part(0),
                pl.BlockSpec((1, 1, 8, GROUP), lambda g, i, kind: (g, i, 0, 0)),
            ),
        ),
        compiler_params=pltpu.CompilerParams(vmem_limit_bytes=32 << 20),
        cost_estimate=cost(16 * triple.shape[0] * GROUP * H * HD, 8 * triple.size),
        name="attend",
    )(image_kind, triple, triple, triple)


def attend_back_kernel(
    kind_ref,
    query_ref,
    key_ref,
    value_ref,
    mixed_ref,
    grad_ref,
    logsum_ref,
    grads_ref,
    key_sum,
    value_sum,
):
    left = lax.broadcasted_iota(jnp.int32, (GROUP, 2 * HD), 1) < HD

    def split(values):
        zero = jnp.zeros_like(values)
        return (jnp.where(left, values, zero), jnp.where(left, zero, values))

    split_query = split(query_ref[...])
    split_keys = split(key_ref[...])
    split_values = split(value_ref[...])
    split_grad = split(grad_ref[...])
    outer = jnp.transpose(mixed_ref[...].astype(F32) * grad_ref[...].astype(F32))
    inner = (
        jnp.sum(outer[:HD], axis=0, keepdims=True),
        jnp.sum(outer[HD:], axis=0, keepdims=True),
    )

    def rows_of(part, first, count, fresh):
        low, high = part * SHORT, (part + 1) * SHORT
        keys_at = pl.ds(first, count)
        query = query_ref[pl.ds(low, SHORT), :]
        grad = grad_ref[pl.ds(low, SHORT), :]
        key_part = value_part = query_part = None
        for half in range(2):
            keys = split_keys[half][first : first + count]
            scores = mm_rt(keys, query)
            logsum = logsum_ref[0, 0, half : half + 1, low:high]
            attention = jnp.exp2(scores * (SCORE * LOG2E) - logsum)
            moved = mm_rt(split_values[half][first : first + count], grad)
            grad_scores = (attention * (moved - inner[half][:, low:high])).astype(BF16)
            value_add = mm(attention.astype(BF16), split_grad[half][low:high])
            key_add = mm(grad_scores, split_query[half][low:high])
            query_add = mm_lt(grad_scores, keys)
            if half == 0:
                key_part, value_part, query_part = key_add, value_add, query_add
            else:
                key_part, value_part = key_part + key_add, value_part + value_add
                query_part = query_part + query_add
        grads_ref[0, pl.ds(low, SHORT), :] = (query_part * SCORE).astype(BF16)
        if fresh:
            key_sum[keys_at, :] = key_part
            value_sum[keys_at, :] = value_part
        else:
            key_sum[keys_at, :] += key_part
            value_sum[keys_at, :] += value_part

    is_long = kind_ref[pl.program_id(0)] == 1

    @pl.when(is_long)
    def _():
        for part in range(GROUP // SHORT):
            rows_of(part, 0, GROUP, part == 0)

    @pl.when(jnp.logical_not(is_long))
    def _():
        for part in range(GROUP // SHORT):
            rows_of(part, part * SHORT, SHORT, True)

    grads_ref[1, :, :] = (key_sum[...] * SCORE).astype(BF16)
    grads_ref[2, :, :] = value_sum[...].astype(BF16)


def attend_back(triple, attended, logsum, grad_attended, image_kind):
    groups = triple.shape[0] // GROUP
    pairs = H // 2

    def part(offset):
        return pl.BlockSpec((GROUP, 2 * HD), lambda g, i, kind: (g, offset + i))

    return pl.pallas_call(
        attend_back_kernel,
        out_shape=jax.ShapeDtypeStruct((3, triple.shape[0], H * HD), BF16),
        grid_spec=pltpu.PrefetchScalarGridSpec(
            num_scalar_prefetch=1,
            grid=(groups, pairs),
            in_specs=[
                part(0),
                part(pairs),
                part(2 * pairs),
                part(0),
                part(0),
                pl.BlockSpec((1, 1, 8, GROUP), lambda g, i, kind: (g, i, 0, 0)),
            ],
            out_specs=pl.BlockSpec((3, GROUP, 2 * HD), lambda g, i, kind: (0, g, i)),
            scratch_shapes=[pltpu.VMEM((GROUP, 2 * HD), F32)] * 2,
        ),
        compiler_params=pltpu.CompilerParams(vmem_limit_bytes=32 << 20),
        cost_estimate=cost(40 * triple.shape[0] * GROUP * H * HD, 12 * triple.size),
        name="attend_back",
    )(image_kind, triple, triple, triple, attended, grad_attended, logsum)


def gelu_both(values):
    square = values * values
    side = tanh_gain * 0.044715 * square
    half = 0.5 + 0.5 * jnp.tanh(values * (tanh_gain + side))
    slope = half + 2.0 * values * (tanh_gain + 3.0 * side) * (half * (1.0 - half))
    return values * half, slope


def way(me, piece, strip):
    sx, other = (piece >> 1) ^ me[1], (piece & 1) ^ me[0]
    sy, k = (strip & 1) ^ me[2], (me[3] - (strip >> 1)) & 3
    return other, sx, sy, k


def on_side(other, own_ref, other_ref, action):
    @pl.when(other == 0)
    def _():
        action(own_ref)

    @pl.when(other == 1)
    def _():
        action(other_ref)


def normalize(values):
    mean = jnp.mean(values, axis=1, keepdims=True)
    centered = values - mean
    return centered * lax.rsqrt(jnp.mean(centered * centered, axis=1, keepdims=True) + eps_norm)


def triple_kernel(me, x_ref, shift_ref, scale_ref, q1a, q1b, q2a, q2b, in_ref, out_ref, weight_ref):
    rows, cols = q1a.shape[3], q1a.shape[4] - OUT_LANES

    @pl.when(pl.program_id(0) == 0)
    def _():
        for piece in range(PIECES):
            for strip in range(STRIPS):
                other, sx, sy, k = way(me, piece, strip)
                low, at = strip * 2 * rows, slice(piece * cols, (piece + 1) * cols)

                def first(ref):
                    weight_ref[low : low + rows, at] = ref[sx, sy, k, :, OUT_LANES:]

                def second(ref):
                    weight_ref[low + rows : low + 2 * rows, at] = ref[sy, sx, k, :, OUT_LANES:]

                on_side(other, q1a, q1b, first)
                on_side(other, q2a, q2b, second)

    normed = normalize(x_ref[...].astype(F32))
    attend_in = (normed * (1.0 + scale_ref[0]) + shift_ref[0]).astype(BF16)
    in_ref[...] = attend_in
    out_ref[...] = mm(attend_in, weight_ref[...]).astype(BF16)


def make_triple(me, patches, shift, scale, weights):
    tok_count, width = patches.shape
    hidden = PIECES * (weights[0].shape[4] - OUT_LANES)
    rows = pl.BlockSpec((SHORT, width), lambda i, me: (i, 0))
    each = pl.BlockSpec((1, 1, width), lambda i, me: (i, 0, 0))
    return pl.pallas_call(
        triple_kernel,
        out_shape=(
            jax.ShapeDtypeStruct((tok_count, width), BF16),
            jax.ShapeDtypeStruct((tok_count, hidden), BF16),
            jax.ShapeDtypeStruct((width, hidden), BF16),
        ),
        grid_spec=pltpu.PrefetchScalarGridSpec(
            num_scalar_prefetch=1,
            grid=(tok_count // SHORT,),
            in_specs=[rows, each, each] + [fixed(w.shape) for w in weights],
            out_specs=(
                rows,
                pl.BlockSpec((SHORT, hidden), lambda i, me: (i, 0)),
                fixed((width, hidden)),
            ),
        ),
        compiler_params=pltpu.CompilerParams(vmem_limit_bytes=40 << 20),
        cost_estimate=cost(2 * tok_count * width * hidden, 8 * tok_count * width),
        name="triple",
    )(me, patches, shift, scale, *weights)


def project_kernel(
    me,
    attended_ref,
    x_ref,
    gate_ref,
    shift_ref,
    scale_ref,
    q1a,
    q1b,
    q2a,
    q2b,
    projected_ref,
    residual_ref,
    branch_ref,
    logits_ref,
    weight_ref,
    router_ref,
):
    width = x_ref.shape[1]
    rows, cols, experts = q1a.shape[3], width // PIECES, E // PIECES

    @pl.when(pl.program_id(0) == 0)
    def _():
        router_ref[...] = jnp.zeros_like(router_ref)
        for piece in range(PIECES):
            for strip in range(STRIPS):
                other, sx, sy, k = way(me, piece, strip)

                def place(block, low):
                    weight_ref[low : low + rows, piece * cols : (piece + 1) * cols] = block[
                        :, :cols
                    ]
                    router_ref[
                        low : low + rows, piece * experts : (piece + 1) * experts
                    ] = block[:, cols : cols + experts]

                def first(ref):
                    place(ref[sx, sy, k], strip * 2 * rows)

                def second(ref):
                    place(ref[sy, sx, k], strip * 2 * rows + rows)

                on_side(other, q1a, q1b, first)
                on_side(other, q2a, q2b, second)

    projected = mm(attended_ref[...], weight_ref[...])
    projected_ref[...] = projected
    residual = x_ref[...].astype(F32) + gate_ref[0] * projected
    residual_ref[...] = residual
    branch = (normalize(residual) * (1.0 + scale_ref[0]) + shift_ref[0]).astype(BF16)
    branch_ref[...] = branch
    logits_ref[...] = mm(branch, router_ref[...])


def make_branch(me, attended, patches, gate, shift, scale, weights):
    tok_count, width = patches.shape
    rows = pl.BlockSpec((SHORT, width), lambda i, me: (i, 0))
    each = pl.BlockSpec((1, 1, width), lambda i, me: (i, 0, 0))
    outs = fixed(weights[0].shape[:4] + (OUT_LANES,))
    return pl.pallas_call(
        project_kernel,
        out_shape=(
            jax.ShapeDtypeStruct((tok_count, width), F32),
            jax.ShapeDtypeStruct((tok_count, width), F32),
            jax.ShapeDtypeStruct((tok_count, width), BF16),
            jax.ShapeDtypeStruct((tok_count, LANES), F32),
            jax.ShapeDtypeStruct((width, width), BF16),
            jax.ShapeDtypeStruct((width, LANES), BF16),
        ),
        grid_spec=pltpu.PrefetchScalarGridSpec(
            num_scalar_prefetch=1,
            grid=(tok_count // SHORT,),
            in_specs=[rows, rows, each, each, each, outs, outs, outs, outs],
            out_specs=(
                rows,
                rows,
                rows,
                pl.BlockSpec((SHORT, LANES), lambda i, me: (i, 0)),
                fixed((width, width)),
                fixed((width, LANES)),
            ),
        ),
        compiler_params=pltpu.CompilerParams(vmem_limit_bytes=32 << 20),
        cost_estimate=cost(2 * tok_count * width * width, 16 * tok_count * width),
        name="project",
    )(me, attended, patches, gate, shift, scale, *weights)


def shared_kernel(
    x_ref,
    grad_ref,
    in_ref,
    out_ref,
    res_ref,
    x_grad_ref,
    weight_grad_ref,
    weight_out,
    x_turned,
    grad_turned,
):
    step = pl.program_id(0)
    width = x_ref.shape[1]
    rows, half = width // STRIPS, width // 2

    @pl.when(step == 0)
    def _():
        x_turned[...] = jnp.transpose(x_ref[...])
        grad_turned[...] = jnp.transpose(grad_ref[...])

    halves = [slice(0, half), slice(half, width)]
    for piece in range(PIECES):
        for strip in range(2):
            for part in range(2):
                low = (2 * piece + part) * rows
                weight_out[low : low + rows, halves[strip]] = out_ref[piece, strip, :, halves[part]]
    weight_in = in_ref[...].reshape(width, width)
    act, slope = gelu_both(mm(x_ref[...], weight_in))
    act = act.astype(BF16)
    grad_pre = (mm(grad_ref[...], weight_out[...]) * slope).astype(BF16)
    res = mm_rt(act, weight_out[...])
    x_grad = mm_rt(grad_pre, weight_in)

    @pl.when(step == 0)
    def _():
        res_ref[...] = res
        x_grad_ref[...] = x_grad

    @pl.when(step != 0)
    def _():
        res_ref[...] += res
        x_grad_ref[...] += x_grad

    in_grad = mm(x_turned[...], grad_pre).astype(BF16)
    out_grad = mm(grad_turned[...], act).astype(BF16)
    weight_grad_ref[step, :, :rows, :] = in_grad.reshape(STRIPS, rows, width)
    for piece in range(PIECES):
        for strip in range(2):
            for part in range(2):
                low = (2 * piece + part) * rows
                weight_grad_ref[piece, 2 * step + strip, rows:, halves[part]] = out_grad[
                    low : low + rows, halves[strip]
                ]


def shared_expert(x, grad, weights):
    tok_count, width = x.shape
    rows = width // STRIPS
    whole = fixed((tok_count, width))
    return pl.pallas_call(
        shared_kernel,
        out_shape=(
            jax.ShapeDtypeStruct((tok_count, width), F32),
            jax.ShapeDtypeStruct((tok_count, width), F32),
            jax.ShapeDtypeStruct(weights.shape, BF16),
        ),
        grid=(PIECES,),
        in_specs=[
            whole,
            whole,
            pl.BlockSpec((1, STRIPS, rows, width), lambda j: (j, 0, 0, 0)),
            pl.BlockSpec((PIECES, 2, rows, width), lambda j: (0, j, 1, 0)),
        ],
        out_specs=(whole, whole, fixed(weights.shape)),
        scratch_shapes=[pltpu.VMEM((width, width), BF16)]
        + [pltpu.VMEM((width, tok_count), BF16)] * 2,
        compiler_params=pltpu.CompilerParams(vmem_limit_bytes=56 << 20),
        cost_estimate=cost(12 * tok_count * width * 4 * width, 16 * tok_count * width),
        name="shared_expert",
    )(x, grad, weights, weights)


def project_back_kernel(
    attended_ref, grad_ref, branch_ref, logits_ref, weight_ref, back_ref, out_grad_ref, router_ref
):
    back_ref[...] = mm_rt(grad_ref[...], weight_ref[...]).astype(BF16)
    out_grad_ref[...] = mm_lt(attended_ref[...], grad_ref[...]).astype(BF16)
    router_ref[...] = mm_lt(branch_ref[...], logits_ref[...]).astype(BF16)


def project_back(attended, grad, branch, grad_logits, weight):
    tok_count, width = attended.shape
    whole = fixed((tok_count, width))
    return pl.pallas_call(
        project_back_kernel,
        out_shape=(
            jax.ShapeDtypeStruct((tok_count, width), BF16),
            jax.ShapeDtypeStruct((width, width), BF16),
            jax.ShapeDtypeStruct((width, LANES), BF16),
        ),
        grid=(1,),
        in_specs=[whole, whole, whole, fixed((tok_count, LANES)), fixed((width, width))],
        out_specs=(whole, fixed((width, width)), fixed((width, LANES))),
        compiler_params=pltpu.CompilerParams(vmem_limit_bytes=32 << 20),
        cost_estimate=cost(4 * tok_count * width * width, 8 * tok_count * width),
        name="project_back",
    )(attended, grad, branch, grad_logits, weight)


def triple_back_kernel(
    me,
    grad_ref,
    in_ref,
    weight_ref,
    out_grad_ref,
    router_ref,
    back_ref,
    q1a,
    q1b,
    q2a,
    q2b,
    in_turned,
    weight_grad,
):
    step = pl.program_id(0)
    rows, cols = q1a.shape[3], q1a.shape[4] - OUT_LANES
    width = in_ref.shape[1]
    outs, experts = width // PIECES, E // PIECES

    @pl.when(step == 0)
    def _():
        in_turned[...] = jnp.transpose(in_ref[...])

    grad = grad_ref[0]
    at = pl.ds(pl.multiple_of(step * width, LANES), width)
    weight_grad[:, at] = mm(in_turned[...], grad).astype(BF16)
    back = mm_rt(grad, weight_ref[...])

    @pl.when(step == 0)
    def _():
        back_ref[...] = back

    @pl.when(step != 0)
    def _():
        back_ref[...] += back

    @pl.when(step == 2)
    def _():
        for piece in range(PIECES):
            for strip in range(STRIPS):
                other, sx, sy, k = way(me, piece, strip)

                def place(ref, where, low):
                    at = slice(low, low + rows)
                    ref[where + (slice(None), slice(0, outs))] = out_grad_ref[
                        at, piece * outs : (piece + 1) * outs
                    ]
                    ref[where + (slice(None), slice(outs, outs + experts))] = router_ref[
                        at, piece * experts : (piece + 1) * experts
                    ]
                    ref[where + (slice(None), slice(outs + experts, OUT_LANES))] = jnp.zeros(
                        (rows, OUT_LANES - outs - experts), BF16
                    )
                    ref[where + (slice(None), slice(OUT_LANES, None))] = weight_grad[
                        at, piece * cols : (piece + 1) * cols
                    ]

                def first(ref):
                    place(ref, (sx, sy, k), strip * 2 * rows)

                def second(ref):
                    place(ref, (sy, sx, k), strip * 2 * rows + rows)

                on_side(other, q1a, q1b, first)
                on_side(other, q2a, q2b, second)


def triple_back(me, grads, attend_in, weight, out_grad, router_grad):
    tok_count, width = attend_in.shape
    hidden = weight.shape[1]
    block = (2, 2, 4, width // STRIPS // 2, OUT_LANES + hidden // PIECES)
    block = jax.ShapeDtypeStruct(block, BF16)
    return pl.pallas_call(
        triple_back_kernel,
        out_shape=(jax.ShapeDtypeStruct((tok_count, width), F32),) + (block,) * 4,
        grid_spec=pltpu.PrefetchScalarGridSpec(
            num_scalar_prefetch=1,
            grid=(3,),
            in_specs=[
                pl.BlockSpec((1, tok_count, width), lambda p, me: (p, 0, 0)),
                fixed((tok_count, width)),
                pl.BlockSpec((width, width), lambda p, me: (0, p)),
                fixed((width, width)),
                fixed((width, LANES)),
            ],
            out_specs=(fixed((tok_count, width)),) + (fixed(block.shape),) * 4,
            scratch_shapes=[
                pltpu.VMEM((width, tok_count), BF16),
                pltpu.VMEM((width, hidden), BF16),
            ],
        ),
        compiler_params=pltpu.CompilerParams(vmem_limit_bytes=40 << 20),
        cost_estimate=cost(4 * tok_count * width * hidden, 12 * tok_count * width),
        name="triple_back",
    )(me, grads, attend_in, weight, out_grad, router_grad)


ROW_TILE = 576


def expert_kernel(parts, x_ref, *refs):
    weights, (res_ref, act_ref, slope_ref) = refs[:parts], refs[parts:]
    x = x_ref[...]
    total = None
    for part in range(parts):
        width = weights[part].shape[1]
        at = pl.ds(part * width, width)
        act, slope = gelu_both(mm(x, weights[part][:width, :]))
        act = act.astype(BF16)
        act_ref[:, at] = act
        slope_ref[:, at] = slope.astype(BF16)
        res = mm(act, weights[part][width:, :])
        total = res if total is None else total + res
    res_ref[...] = total.astype(BF16)


def expert_back_kernel(parts, grad_ref, slope_ref, *refs):
    weights, (rows_ref, pre_ref) = refs[:parts], refs[parts:]
    grad = grad_ref[...]
    total = None
    for part in range(parts):
        width = weights[part].shape[1]
        at = pl.ds(part * width, width)
        grad_pre = mm_rt(grad, weights[part][width:, :]) * slope_ref[:, at].astype(F32)
        grad_pre = grad_pre.astype(BF16)
        pre_ref[:, at] = grad_pre
        rows = mm_rt(grad_pre, weights[part][:width, :])
        total = rows if total is None else total + rows
    rows_ref[...] = total.astype(BF16)


def expert_call(kernel, name, rows_in, wide_in, weights, n_wide):
    rows, width = rows_in.shape
    hidden = len(weights) * width
    narrow = pl.BlockSpec((ROW_TILE, width), lambda i: (i, 0))
    wide = pl.BlockSpec((ROW_TILE, hidden), lambda i: (i, 0))
    fixed = pl.BlockSpec((2 * width, width), lambda i: (0, 0), pipeline_mode=pl.Buffered(1))
    return pl.pallas_call(
        functools.partial(kernel, len(weights)),
        out_shape=(jax.ShapeDtypeStruct((rows, width), BF16),)
        + (jax.ShapeDtypeStruct((rows, hidden), BF16),) * n_wide,
        grid=(rows // ROW_TILE,),
        in_specs=[narrow] + [wide] * len(wide_in) + [fixed] * len(weights),
        out_specs=(narrow,) + (wide,) * n_wide,
        compiler_params=pltpu.CompilerParams(vmem_limit_bytes=48 << 20),
        cost_estimate=cost(8 * rows * hidden * width, 2 * rows * hidden * (1 + n_wide)),
        name=name,
    )(rows_in, *wide_in, *weights)


def by_way(blocks, y_outer):
    rows, cols = blocks.shape[2:]
    blocks = blocks.reshape(2, 2, 4, 2, rows, cols)[:, :, jnp.array([0, 3, 2, 1])]
    blocks = blocks.transpose((1, 3, 0, 2, 4, 5) if y_outer else (1, 0, 3, 2, 4, 5))
    return blocks[0], blocks[1]


def by_place(own, other, y_outer):
    blocks = jnp.stack((own, other))
    blocks = blocks.transpose((2, 0, 3, 1, 4, 5) if y_outer else (1, 0, 3, 2, 4, 5))
    rows, cols = blocks.shape[4:]
    return blocks[:, :, jnp.array([0, 3, 2, 1])].reshape(PIECES, STRIPS, rows, cols)


def to_blocks(whole):
    rows, cols = whole.shape
    return whole.reshape(STRIPS, rows // STRIPS, PIECES, cols // PIECES).transpose(2, 0, 1, 3)


def to_whole(blocks):
    rows, cols = blocks.shape[2:]
    return blocks.transpose(1, 2, 0, 3).reshape(STRIPS * rows, PIECES * cols)


def turn(block):
    block = block.T
    half = block.shape[0] // 2
    return jnp.concatenate((block[:half], block[half:]), axis=1)


def turn_back(block):
    half = block.shape[1] // 2
    return jnp.concatenate((block[:, :half], block[:, half:]), axis=0).T


def shared_bundle(up, down):
    down = to_blocks(down).swapaxes(2, 3)
    half = down.shape[2] // 2
    return jnp.concatenate(
        (to_blocks(up), jnp.concatenate((down[:, :, :half], down[:, :, half:]), axis=3)), axis=2
    )


def shared_unbundle(grads):
    rows, half = grads.shape[2] // 2, grads.shape[3] // 2
    down = grads[:, :, rows:]
    down = jnp.concatenate((down[..., :half], down[..., half:]), axis=2).swapaxes(2, 3)
    return to_whole(grads[:, :, :rows]), to_whole(down)


class Ring:
    def __init__(self, mesh):
        self.n_exp = mesh.shape["exp"]
        self.n_ring = mesh.shape["zi"]
        self.n_pair = mesh.shape["yi"]
        self.direct = (self.n_exp, self.n_ring, self.n_pair) == (PIECES, 4, 2)

    def step(self, value, by=1):
        n = self.n_ring
        return lax.ppermute(value, "zi", [(i, (i + by) % n) for i in range(n)])

    def over_y(self, value):
        return lax.ppermute(value, "yi", [(0, 1), (1, 0)])

    def over_x(self, value):
        return lax.ppermute(value, "exp", [(i, i ^ 2) for i in range(4)])

    def over_core(self, value):
        return lax.ppermute(value, "exp", [(i, i ^ 1) for i in range(4)])

    def near(self, block):
        return jnp.stack([block] + [self.step(block, k) for k in range(1, 4)])

    def second(self, held, y_outer):
        return jnp.stack((held, (self.over_x if y_outer else self.over_y)(held)))

    def third(self, held, y_outer):
        return jnp.stack((held, (self.over_y if y_outer else self.over_x)(held)))

    def outer(self, value, y_outer):
        return (self.over_y if y_outer else self.over_x)(value)

    def inner(self, value, y_outer):
        return (self.over_x if y_outer else self.over_y)(value)

    def line(self, held):
        return tuple(self.step(held[k], -k) for k in range(1, 4))


def add_both(keep, got):
    return add(keep[0], got[0]), add(keep[1], got[1])


def add_line(held, got):
    total = held.astype(F32)
    for part in got:
        total = total + part.astype(F32)
    return total


def add(left, right):
    return (left.astype(F32) + right.astype(F32)).astype(BF16)


def tie(*values):
    return lax.optimization_barrier(values)


def after(value, *others):
    return lax.optimization_barrier((value,) + others)[0]


def picked_experts(ring, y, expert_in, expert_out):
    own_in = jnp.where(y == 0, expert_in[0], expert_in[1])
    give_in = jnp.where(y == 0, expert_in[1], expert_in[0])
    own_out = jnp.where(y == 0, expert_out[0], expert_out[1])
    give_out = jnp.where(y == 0, expert_out[1], expert_out[0])
    ups = jnp.concatenate((own_in, ring.over_y(give_in)), axis=1)
    downs = jnp.concatenate((own_out, ring.over_y(give_out)), axis=0)
    return jnp.concatenate((ups, downs), axis=0)


def local(
    ring,
    patches,
    cond_embed,
    image_kind,
    expert_ids,
    out_grad,
    modulate_weight,
    attend_weight,
    output_weight,
    router_weight,
    shared_in,
    shared_out,
    expert_in,
    expert_out,
):
    tok_count, width = patches.shape
    blocks = tok_count // SHORT
    n_exp, n_ring, n_pair = ring.n_exp, ring.n_ring, ring.n_pair
    n_fsdp = n_ring * n_pair
    n_all = n_exp * n_fsdp
    e, z, y = (lax.axis_index(name) for name in ("exp", "zi", "yi"))
    mod_rows, mod_cols = modulate_weight.shape
    half = width // STRIPS // 2
    if ring.direct:
        me = jnp.stack((e & 1, e >> 1, y, z)).astype(jnp.int32)
    else:
        me = jnp.zeros((4,), jnp.int32)

    cond_float = cond_embed.astype(F32)
    cond_act = jax.nn.silu(cond_float).astype(BF16)
    cond_send = cond_act.reshape(blocks, n_fsdp, mod_rows).transpose(1, 0, 2)
    cond_send = jnp.broadcast_to(cond_send[None], (n_exp, n_fsdp, blocks, mod_rows))
    cond_all = lax.all_to_all(
        cond_send.reshape(n_all, blocks, mod_rows), ALL, 0, 0, tiled=True
    ).reshape(n_all * blocks, mod_rows)
    mod_part = mm(cond_all, modulate_weight).reshape(n_all, blocks, mod_cols)
    mod_early = mod_part
    mod_part = lax.all_to_all(mod_part, ALL, 0, 0, tiled=True)
    modulation = jnp.sum(mod_part.reshape(n_exp, n_fsdp, blocks, mod_cols), axis=1)
    modulation = modulation.transpose(1, 0, 2).reshape(blocks, 1, 6, width)

    if ring.direct:
        spare = OUT_LANES - output_weight.shape[1] - router_weight.shape[1]
        block = jnp.concatenate(
            (
                output_weight,
                router_weight,
                jnp.zeros((router_weight.shape[0], spare), BF16),
                attend_weight,
            ),
            axis=1,
        )
        bundle = jnp.concatenate((shared_in, turn(shared_out)), axis=0)
        shared_weights = lax.all_gather(bundle, ALL, axis=0, tiled=False)
        shared_weights = shared_weights.reshape((PIECES, STRIPS) + bundle.shape)
        expert_block = picked_experts(ring, y, expert_in, expert_out)
        held = after(ring.near(block), mod_early)
        held_1 = ring.second(held[:, :half], False)
        held_2 = ring.second(held[:, half:], True)
        held_1 = ring.third(after(held_1, expert_block), False)
        held_2 = ring.third(after(held_2, expert_block), True)
        dense_weights = (held_1, ring.over_core(held_1), held_2, ring.over_core(held_2))
        expert_block = after(expert_block, modulation)
        expert_weights = [expert_block, ring.step(expert_block)]
    else:
        wholes = [
            lax.all_gather(
                lax.all_gather(w, FSDP, axis=0, tiled=True), "exp", axis=1, tiled=True
            )
            for w in (attend_weight, output_weight, router_weight, shared_in, shared_out)
        ]
        attend_all, output_all, router_all = map(to_blocks, wholes[:3])
        up_all, down_all = wholes[3:]
        spare = jnp.zeros((PIECES, STRIPS, 2 * half, OUT_LANES - (width + E) // PIECES), BF16)
        dense_all = jnp.concatenate((output_all, router_all, spare, attend_all), axis=3)
        dense_weights = by_way(dense_all[:, :, :half], False)
        dense_weights += by_way(dense_all[:, :, half:], True)
        shared_weights = shared_bundle(up_all, down_all)
        up_all = lax.all_gather(expert_in[0], FSDP, axis=1, tiled=True)
        down_all = lax.all_gather(expert_out[0], FSDP, axis=0, tiled=True)
        expert_weights = [
            jnp.concatenate((up_all[:, at : at + width], down_all[at : at + width]), axis=0)
            for at in range(0, up_all.shape[1], width)
        ]

    shift_first = modulation[:, :, 0]
    scale_first = modulation[:, :, 1]
    gate_first = modulation[:, :, 2]
    shift_second = modulation[:, :, 3]
    scale_second = modulation[:, :, 4]
    gate_second = modulation[:, :, 5]
    attend_in, triple, triple_weight = make_triple(
        me, patches, shift_first, scale_first, dense_weights
    )
    attended, logsum = attend(triple, image_kind)
    projected, residual, branch_in, logits, output_weight_all, router_all = make_branch(
        me, attended, patches, gate_first, shift_second, scale_second, dense_weights
    )
    if ring.direct:
        branch_in = after(branch_in, expert_weights[1])
        expert_weights.append(ring.step(expert_weights[1]))
    choose = expert_ids[:, :, None] == jnp.arange(E, dtype=jnp.int32)[None, None, :]
    choose = choose.astype(F32)
    gates = jax.nn.softmax(jnp.sum(choose * logits[:, None, :E], axis=-1), axis=-1)

    grad_out = out_grad.astype(F32).reshape(blocks, SHORT, width)
    grad_branch = (gate_second * grad_out).astype(BF16).reshape(tok_count, width)
    grad_branch_wide = grad_branch.astype(F32)

    slots = slot_table(expert_ids)
    target = expert_ids * CAP + slots
    row_of = jnp.arange(E * CAP, dtype=jnp.int32)[:, None]
    pick0 = (row_of == target[None, :, 0]).astype(BF16)
    pick1 = (row_of == target[None, :, 1]).astype(BF16)
    send_rows = mm(pick0 + pick1, branch_in).astype(BF16).reshape(E, CAP, width)
    grad_picked = (gates[:, :, None] * grad_branch_wide[:, None, :]).astype(BF16)
    grad_send = mm(pick0, grad_picked[:, 0]) + mm(pick1, grad_picked[:, 1])
    grad_send = grad_send.astype(BF16).reshape(E, CAP, width)
    shared_x = after(branch_in, send_rows, grad_send)

    def exchange(rows):
        return lax.all_to_all(rows, ("exp", "yi"), 0, 0, tiled=True)

    received = exchange(send_rows)

    shared_res, grad_branch_in, shared_grads = shared_expert(shared_x, grad_branch, shared_weights)

    received = after(received, shared_res)
    if ring.direct:
        expert_weights[2] = after(expert_weights[2], shared_res)
        expert_weights.append(ring.step(expert_weights[2]))
        expert_weights = expert_weights[1:] + expert_weights[:1]
    received = received.reshape(-1, width)
    grad_received = exchange(after(grad_send, received))
    expert_res, expert_act, expert_slope = expert_call(
        expert_kernel, "experts", received, (), expert_weights, 2
    )
    grad_received = grad_received.reshape(-1, width)
    expert_res = after(expert_res, grad_received)
    returned = exchange(expert_res.reshape(E, CAP, width))
    grad_rows, grad_pre = expert_call(
        expert_back_kernel, "experts_back", grad_received, (expert_slope,), expert_weights, 1
    )
    returned = returned.reshape(-1, width)
    grad_rows = after(grad_rows, returned)
    grad_returned = exchange(grad_rows.reshape(E, CAP, width)).reshape(-1, width)

    def expert_grads(part):
        at = slice(part * width, (part + 1) * width)
        return jnp.concatenate(
            (
                mm_lt(received, grad_pre[:, at]).astype(BF16),
                mm_lt(expert_act[:, at], grad_received).astype(BF16),
            ),
            axis=0,
        )

    grad_blocks = [expert_grads(part) for part in range(len(expert_weights))]
    returned = after(returned, *grad_blocks)
    if ring.direct:
        moved = ring.step(grad_blocks[0])

    picked0 = mm_lt(pick0, returned)
    picked1 = mm_lt(pick1, returned)
    mixture = gates[:, 0:1] * picked0 + gates[:, 1:2] * picked1
    branch_out = (shared_res + mixture).reshape(blocks, SHORT, width)
    projected = projected.reshape(blocks, SHORT, width)
    residual = residual.reshape(blocks, SHORT, width)
    normed_second, inverse_second = layer_norm(residual)
    block_out = (residual + gate_second * branch_out).reshape(tok_count, width).astype(BF16)
    grad_gate_second = jnp.sum(grad_out * branch_out, axis=1)
    grad_gates = jnp.stack(
        (
            jnp.sum(grad_branch_wide * picked0, axis=-1),
            jnp.sum(grad_branch_wide * picked1, axis=-1),
        ),
        axis=1,
    )
    grad_chosen = gates * (grad_gates - jnp.sum(gates * grad_gates, axis=-1, keepdims=True))
    grad_logits = jnp.sum(choose * grad_chosen[:, :, None], axis=1).astype(BF16)
    grad_logits = jnp.concatenate((grad_logits, jnp.zeros((tok_count, LANES - E), BF16)), axis=1)
    grad_branch_in = (
        grad_branch_in
        + mm_lt(pick0 + pick1, grad_returned)
        + mm_rt(grad_logits, router_all)
    )
    grad_norm_in = grad_branch_in.reshape(blocks, SHORT, width)
    grad_shift_second = jnp.sum(grad_norm_in, axis=1)
    grad_scale_second = jnp.sum(grad_norm_in * normed_second, axis=1)
    grad_residual = grad_out + norm_back(
        grad_norm_in * (1.0 + scale_second), normed_second, inverse_second
    )
    grad_gate_first = jnp.sum(grad_residual * projected, axis=1)
    grad_projected = (gate_first * grad_residual).astype(BF16).reshape(tok_count, width)
    grad_attended, out_grad_all, router_grad_all = project_back(
        attended, grad_projected, branch_in, grad_logits, output_weight_all
    )
    if ring.direct:
        grad_attended, moved = tie(grad_attended, moved)
        moved = ring.step(add(moved, grad_blocks[1]))
    grad_triple = attend_back(triple, attended, logsum, grad_attended, image_kind)
    if ring.direct:
        grad_triple, moved = tie(grad_triple, moved)
        moved = ring.step(add(moved, grad_blocks[2]))
    grad_attend_in, *dense_grads = triple_back(
        me, grad_triple, attend_in, triple_weight, out_grad_all, router_grad_all
    )
    if ring.direct:
        own_1, give_1, own_2, give_2 = dense_grads
        sum_1, give_1 = add_both(own_1, ring.over_core(give_1))
        sum_2, give_2 = add_both(own_2, ring.over_core(give_2))
        got_1, got_2 = ring.outer(give_1, False), ring.outer(give_2, True)
    inputs = patches.astype(F32).reshape(blocks, SHORT, width)
    normed_first, inverse_first = layer_norm(inputs)
    grad_attend_in = grad_attend_in.reshape(blocks, SHORT, width)
    grad_shift_first = jnp.sum(grad_attend_in, axis=1)
    grad_scale_first = jnp.sum(grad_attend_in * normed_first, axis=1)
    patches_grad = grad_residual + norm_back(
        grad_attend_in * (1.0 + scale_first), normed_first, inverse_first
    )
    patches_grad = patches_grad.reshape(tok_count, width)

    grad_modulation = jnp.stack(
        (
            grad_shift_first,
            grad_scale_first,
            grad_gate_first,
            grad_shift_second,
            grad_scale_second,
            grad_gate_second,
        ),
        axis=1,
    )
    grad_modulation = grad_modulation.reshape(blocks, n_exp, mod_cols).astype(BF16)
    mod_send = jnp.broadcast_to(
        grad_modulation.transpose(1, 0, 2)[:, None], (n_exp, n_fsdp, blocks, mod_cols)
    )
    mod_all = lax.all_to_all(
        mod_send.reshape(n_all, blocks, mod_cols), ALL, 0, 0, tiled=True
    ).reshape(n_all * blocks, mod_cols)
    modulate_grad = mm_lt(cond_all, mod_all)
    cond_part = mm_rt(mod_all, modulate_weight).reshape(n_all, blocks, mod_rows)
    if ring.direct:
        mod_all = after(mod_all, got_1, got_2)
        sum_1, give_1 = add_both(sum_1, got_1)
        sum_2, give_2 = add_both(sum_2, got_2)
        sum_1 = add(sum_1, ring.inner(give_1, False))
        sum_2 = add(sum_2, ring.inner(give_2, True))
        cond_part = after(cond_part, sum_1, sum_2)
    cond_part = lax.all_to_all(cond_part, ALL, 0, 0, tiled=True)
    cond_grad = jnp.sum(cond_part.reshape(n_exp, n_fsdp, blocks, mod_rows), axis=0)
    cond_grad = cond_grad.transpose(1, 0, 2).reshape(blocks, width) * silu_slope(cond_float)

    if ring.direct:
        cols, experts = width // PIECES, E // PIECES
        summed = jnp.concatenate(
            (add_line(sum_1[0], ring.line(sum_1)), add_line(sum_2[0], ring.line(sum_2))), axis=0
        )
        output_grad, router_grad = summed[:, :cols], summed[:, cols : cols + experts]
        attend_grad = summed[:, OUT_LANES:]
        summed = lax.psum_scatter(
            shared_grads.reshape((n_all,) + bundle.shape), ALL, scatter_dimension=0
        ).astype(F32)
        shared_in_grad = summed[: 2 * half]
        shared_out_grad = turn_back(summed[2 * half :])
        moved = moved.astype(F32) + grad_blocks[3].astype(F32)
        up_sum, down_sum = moved[:width], moved[width:]
        split = width // 2
        got_up = ring.over_y(up_sum[:, split:].astype(BF16)).astype(F32)
        got_down = ring.over_y(down_sum[split:].astype(BF16)).astype(F32)
        own_up, own_down = up_sum[:, :split], down_sum[:split]
        expert_in_grad = jnp.stack(
            (jnp.where(y == 0, own_up, got_up), jnp.where(y == 0, got_up, own_up))
        )
        expert_out_grad = jnp.stack(
            (jnp.where(y == 0, own_down, got_down), jnp.where(y == 0, got_down, own_down))
        )
    else:

        def spread(grad):
            part = lax.psum_scatter(grad, "exp", scatter_dimension=1, tiled=True)
            return lax.psum_scatter(part, FSDP, scatter_dimension=0, tiled=True).astype(F32)

        dense_all = jnp.concatenate(
            (by_place(*dense_grads[:2], False), by_place(*dense_grads[2:], True)), axis=2
        )
        cols, experts = width // PIECES, E // PIECES
        attend_grad = spread(to_whole(dense_all[..., OUT_LANES:]))
        output_grad = spread(to_whole(dense_all[..., :cols]))
        router_grad = spread(to_whole(dense_all[..., cols : cols + experts]))
        shared_in_grad, shared_out_grad = map(spread, shared_unbundle(shared_grads))
        up_sum = jnp.concatenate([b[:width] for b in grad_blocks], axis=1)
        down_sum = jnp.concatenate([b[width:] for b in grad_blocks], axis=0)
        expert_in_grad = lax.psum_scatter(up_sum, FSDP, scatter_dimension=1, tiled=True)
        expert_out_grad = lax.psum_scatter(down_sum, FSDP, scatter_dimension=0, tiled=True)
        expert_in_grad = expert_in_grad.astype(F32)[None]
        expert_out_grad = expert_out_grad.astype(F32)[None]
    return (
        block_out,
        patches_grad,
        cond_grad,
        modulate_grad,
        attend_grad,
        output_grad,
        router_grad,
        shared_in_grad,
        shared_out_grad,
        expert_in_grad,
        expert_out_grad,
    )


def solution(mesh):
    n_exp, n_fsdp = mesh.shape["exp"], mesh.shape["fsdp"]
    n_pair = E // n_exp
    if n_pair not in (1, 2) or n_fsdp % n_pair:
        raise ValueError("unsupported mesh")
    fine = Mesh(mesh.devices.reshape(n_exp, n_fsdp // n_pair, n_pair), ALL)
    ring = Ring(fine)
    in_specs = (
        P(ALL, None),
        P(ALL, None),
        P(ALL),
        P(ALL, None),
        P(ALL, None),
        P(FSDP, "exp"),
        P(FSDP, "exp"),
        P(FSDP, "exp"),
        P(FSDP, "exp"),
        P(FSDP, "exp"),
        P(FSDP, "exp"),
        P("exp", None, FSDP),
        P("exp", FSDP, None),
    )
    out_specs = (
        P(ALL, None),
        P(ALL, None),
        P(ALL, None),
        P(FSDP, "exp"),
        P(FSDP, "exp"),
        P(FSDP, "exp"),
        P(FSDP, "exp"),
        P(FSDP, "exp"),
        P(FSDP, "exp"),
        P("exp", None, FSDP),
        P("exp", FSDP, None),
    )

    def step(*args):
        return local(ring, *args)

    return jax.shard_map(step, mesh=fine, in_specs=in_specs, out_specs=out_specs, check_vma=False)
```

time: 1030 us -> 740 us (0.72)
  matrix products: 308 us -> 99.4 us
  Pallas kernels: 28.4 us -> 183 us
  local copies, waits for them, and re-layouts: 159 us -> 35.4 us
  waiting for transfers between devices: 265 us -> 183 us
  other arithmetic: 102 us -> 73.7 us
  between operations: 3.88 us -> 16.5 us
    dot_general x48 -> x18, matrix products: 308 us -> 99.4 us  [dot(): lax.dot_general(left, right, (dims, ((), ())), preferred_element_type=F32)]
    pallas_call x0 -> x7, Pallas kernels: none -> 155 us  [the longest x2 69.5 us: expert_call(): pl.pallas_call(functools.partial(kernel, len(weights)), out_shape=(jax.Sh...]
    ppermute x64 -> x31, waiting for transfers between devices: 242 us -> 157 us  [the longest x15 94.6 us: step(): return lax.ppermute(value, 'zi', [(i, (i + by) % n) for i in range(n)])]
    reshape x9 -> x0, local copies, waits for them, and re-layouts: 29.4 us -> none  [the longest x6 28.6 us: dense(): grad.reshape(n_fsdp, rows, n_exp, cols).transpose(2, 0, 1, 3).astype(BF16)]
    another operation x6 -> x1, local copies, waits for them, and re-layouts: 24.7 us -> 0.1 us  [second(): return jnp.stack((held, (self.over_x if y_outer else self.over_y)(held)))]
    dot_general x6 -> x1, local copies, waits for them, and re-layouts: 25.7 us -> 2.45 us  [dot(): lax.dot_general(left, right, (dims, ((), ())), preferred_element_type=F32)]
    transpose x6 -> x1, local copies, waits for them, and re-layouts: 20.8 us -> 0.02 us  [local(): modulation = modulation.transpose(1, 0, 2).reshape(blocks, 1, 6, width)]
    another operation x26 -> x9, other arithmetic: 26 us -> 6.81 us  [the longest x2 2.79 us: third(): return jnp.stack((held, (self.over_y if y_outer else self.over_x)(held)))]
  transfers between devices with their start and end apart: 74 -> 41, of which waited for: 27 -> 17; matrix products, arithmetic and copies ran while one was open for 49% -> 25% of each run, Pallas kernels for 3% -> 25%
where the time goes in v2:
time: 740 us; the launch traced here: 735 us
  waiting for transfers between devices  183 us (25%)
  Pallas kernels  183 us (25%)
  starting transfers between devices  144 us (19%)
  matrix products  99.4 us (13%)
  other arithmetic  73.7 us (10%)
  local copies, waits for them, and re-layouts  35.4 us (5%)
  between operations  16.5 us (2%)
    dot_general x18, matrix products, dot(): lax.dot_general(left, right, (dims, ((), ())), preferred_element_type=F32)  99.4 us
    ppermute x15, waiting for transfers between devices, step(): return lax.ppermute(value, 'zi', [(i, (i + by) % n) for i in range(n)])  94.6 us
    ppermute x8, starting transfers between devices, over_y(): return lax.ppermute(value, 'yi', [(0, 1), (1, 0)])  71.6 us
    pallas_call x2, Pallas kernels, expert_call(): pl.pallas_call(functools.partial(kernel, len(weights)), out_shape=(jax.Sh...  69.5 us
    ppermute x8, waiting for transfers between devices, over_y(): return lax.ppermute(value, 'yi', [(0, 1), (1, 0)])  41.9 us
    pallas_call x1, Pallas kernels, shared_expert(): pl.pallas_call(shared_kernel, out_shape=(jax.ShapeDtypeStruct((tok_count,...  41.8 us
    all_to_all x4, starting transfers between devices, exchange(): return lax.all_to_all(rows, ('exp', 'yi'), 0, 0, tiled=True)  33.5 us
    unnamed x167, local copies, waits for them, and re-layouts  20.5 us
  transfers between devices with their start and end apart: 41, of which 17 were waited for; matrix products, arithmetic and copies ran while one was open for 25% of the time, Pallas kernels for 25%

profile of v2, /device:TPU:0, one launch (start us, length us, event | category | flops | bytes accessed | tf_op | source)
XLA Modules:
  0.0 735.0 jit_solution(7224102182881405973)
XLA Ops:
  29.9 10.4 %all-to-all-done = bf16[32,4,96]{2,1,0:T(4,128)(2,1)S(1)} async-done(((bf16[32,4,96]{2,1,0:T(4,128)(2,1)}), bf16[32,4,96]{2,1,0:T(4,128)(2,1)S(1)}, u32[]{:S(2)}, u32[]{:S(2)}) %all-to-all-start) | async-done | bytes 24608 | tf_op jit(solution)/shard_map/all_to_all | solution.py:841
  44.1 15.4 %collective-permute-done.8 = bf16[4,48,832]{2,1,0:T(8,128)(2,1)S(1)} collective-permute-done((bf16[4,48,832]{2,1,0:T(8,128)(2,1)S(1)}, bf16[4,48,832]{2,1,0:T(8,128)(2,1)S(1)}, u32[]{:S(2)}, u32[]{:S(2)}) %collective-permute-start.8) | collective-permute-done | bytes 319520 | tf_op jit(solution)/shard_map/ppermute | solution.py:751
  79.8 12.9 %collective-permute-done.9 = bf16[2,4,48,832]{3,2,1,0:T(8,128)(2,1)S(1)} collective-permute-done((bf16[2,4,48,832]{3,2,1,0:T(8,128)(2,1)S(1)}, bf16[2,4,48,832]{3,2,1,0:T(8,128)(2,1)S(1)}, u32[]{:S(2)}, u32[]{:S(2)}) %collective-permute-start.9) | collective-permute-done | bytes 639008 | tf_op jit(solution)/shard_map/ppermute | solution.py:748
  113.5 12.2 %triple.1 = (bf16[1024,768]{1,0:T(8,128)(2,1)S(1)}, bf16[1024,2304]{1,0:T(8,128)(2,1)}, bf16[768,2304]{1,0:T(8,128)(2,1)S(1)}) custom-call(s32[4]{0:T(128)S(1)} %pad_add_fusion.me, bf16[1024,768]{1,0:T(8,128)(2,1)S(1)} %copy-done.1, f32[4,1,768]{2,1,0:T(1,128)S(1)} %get-tuple-element.243.shift_ref, f32[4,1,768]{2,1,0:T(1,128)S(1)} %get-tuple-element.242.scale_ref, ...), custom_call_target="tpu_custom_call" | custom-call | flops 3623878656 | bytes 6291456 | tf_op jit(solution)/shard_map/triple/pallas_call | solution.py:314
  131.2 11.0 %attend.1 = (bf16[1024,768]{1,0:T(8,128)(2,1)S(1)}, f32[1,6,8,1024]{3,2,1,0:T(8,128)S(1)}) custom-call(s32[1]{0:T(128)S(6)} %copy.161.kind_ref, bf16[1024,2304]{1,0:T(8,128)(2,1)S(1)} %copy-done.26, bf16[1024,2304]{1,0:T(8,128)(2,1)S(1)} %copy-done.26, bf16[1024,2304]{1,0:T(8,128)(2,1)S(1)} %copy-done.26), custom_call_target="tpu_custom_call" | custom-call | flops 12884901888 | bytes 18874368 | tf_op jit(solution)/shard_map/attend/pallas_call | solution.py:130
  142.9 11.5 %project.1 = (f32[1024,768]{1,0:T(8,128)S(1)}, f32[1024,768]{1,0:T(8,128)S(1)}, bf16[1024,768]{1,0:T(8,128)(2,1)S(1)}, f32[1024,128]{1,0:T(8,128)S(1)}, bf16[768...) custom-call(s32[4]{0:T(128)S(1)} %pad_add_fusion.me, bf16[1024,768]{1,0:T(8,128)(2,1)S(1)} %get-tuple-element.59.attended_ref.mixed_ref, ...), custom_call_target="tpu_custom_call" | custom-call | flops 1207959552 | bytes 12582912 | tf_op jit(solution)/shard_map/project/pallas_call | solution.py:396
  180.0 19.8 %all-to-all-start.2 = ((bf16[8,288,768]{2,1,0:T(8,128)(2,1)}), bf16[8,288,768]{2,1,0:T(8,128)(2,1)}, u32[]{:S(2)}, u32[]{:S(2)}) async-start(bf16[8,288,768]{2,1,0:T(8,128)(2,1)} %bitcast.265), calls=%async_computation.2 | async-start | bytes 7077888 | tf_op jit(solution)/shard_map/all_to_all | solution.py:930
  201.2 41.8 %shared_expert.1 = (f32[1024,768]{1,0:T(8,128)}, f32[1024,768]{1,0:T(8,128)}, bf16[4,8,192,768]{3,2,1,0:T(8,128)(2,1)}) custom-call(bf16[1024,768]{1,0:T(8,128)(2,1)} %copy-done.19, bf16[1024,768]{1,0:T(8,128)(2,1)} %get-tuple-element.203.grad_ref, bf16[4,8,192,768]{3,2,1,0:T(8,128)(2,1)} %bitcast.299, bf16[4,8,192,768]{3,2,1,0:T(8,128)(2,1)} %bitcast.300), custom_call_target="tpu_custom_call" | custom-call | flops 28991029248 | bytes 12582912 | tf_op jit(solution)/shard_map/shared_expert/pallas_call | solution.py:485
  243.0 13.0 %collective-permute-done.12.refs_1_ = bf16[1536,768]{1,0:T(8,128)(2,1)} collective-permute-done((bf16[1536,768]{1,0:T(8,128)(2,1)}, bf16[1536,768]{1,0:T(8,128)(2,1)}, u32[]{:S(2)}, u32[]{:S(2)}) %collective-permute-start.12) | collective-permute-done | bytes 2359328 | tf_op jit(solution)/shard_map/ppermute | solution.py:745
  265.7 45.5 %collective-permute-done.13.refs_2_ = bf16[1536,768]{1,0:T(8,128)(2,1)} collective-permute-done((bf16[1536,768]{1,0:T(8,128)(2,1)}, bf16[1536,768]{1,0:T(8,128)(2,1)}, u32[]{:S(2)}, u32[]{:S(2)}) %collective-permute-start.13) | collective-permute-done | bytes 2359328 | tf_op jit(solution)/shard_map/ppermute | solution.py:745
  311.2 37.8 %experts.1 = (bf16[2304,768]{1,0:T(8,128)(2,1)}, bf16[2304,3072]{1,0:T(8,128)(2,1)}, bf16[2304,3072]{1,0:T(8,128)(2,1)}) custom-call(bf16[2304,768]{1,0:T(8,128)(2,1)} %bitcast.41.x_ref, bf16[1536,768]{1,0:T(8,128)(2,1)} %collective-permute-done.11.refs_0_, bf16[1536,768]{1,0:T(8,128)(2,1)} %collective-permute-done.12.refs_1_, ...), custom_call_target="tpu_custom_call" | custom-call | flops 43486543872 | bytes 42467328 | tf_op jit(solution)/shard_map/experts/pallas_call | solution.py:673
  349.0 7.3 fusion.63
  356.3 7.3 fusion.57
  368.1 31.7 %experts_back.1 = (bf16[2304,768]{1,0:T(8,128)(2,1)}, bf16[2304,3072]{1,0:T(8,128)(2,1)}) custom-call(bf16[2304,768]{1,0:T(8,128)(2,1)} %bitcast.42.grad_ref, bf16[2304,3072]{1,0:T(8,128)(2,1)} %get-tuple-element.72.slope_ref, bf16[1536,768]{1,0:T(8,128)(2,1)} %collective-permute-done.11.refs_0_, bf16[1536,768]{1,0:T(8,128)(2,1)} %collective-permute-done.12.refs_1_, ...), custom_call_target="tpu_custom_call" | custom-call | flops 43486543872 | bytes 28311552 | tf_op jit(solution)/shard_map/experts_back/pallas_call | solution.py:673
  454.4 9.3 %multiply_reduce_fusion.6 = (f32[1024]{0:T(1024)S(1)}, f32[1024]{0:T(1024)S(1)}, f32[1024,768]{1,0:T(8,128)}) fusion(bf16[1024,768]{1,0:T(8,128)(2,1)S(1)} %copy-done.41, f32[1024,768]{1,0:T(8,128)S(1)} %fusion, bf16[2304,768]{1,0:T(8,128)(2,1)} %bitcast.44, s32[1024]{0:T(1024)S(1)} %bitcast.293), kind=kOutput, calls=%fused_computation.64 | convolution fusion | flops 3630168064 | bytes 11415552 | tf_op jit(solution)/shard_map/dot_general | solution.py:53
  466.3 12.4 %all-to-all-done.5 = bf16[8,288,768]{2,1,0:T(8,128)(2,1)} async-done(((bf16[8,288,768]{2,1,0:T(8,128)(2,1)}), bf16[8,288,768]{2,1,0:T(8,128)(2,1)}, u32[]{:S(2)}, u32[]{:S(2)}) %all-to-all-start.5) | async-done | bytes 3538976 | tf_op jit(solution)/shard_map/all_to_all | solution.py:930
  488.9 7.6 %fusion.38 = (bf16[4,768]{1,0:T(4,128)(2,1)S(1)}, bf16[4,768]{1,0:T(4,128)(2,1)S(1)}, bf16[4,768]{1,0:T(4,128)(2,1)S(1)}, bf16[4,768]{1,0:T(4,128)(2,1)S(1)}, f32[1024,768]{1,0:T(8,128)S(1)}) fusion(f32[1024,768]{1,0:T(8,128)} %get-tuple-element.249, f32[1024,768]{1,0:T(8,128)S(1)} %get-tuple-element.60, f32[4,256]{1,0:T(4,128)S(1)} %div.65, ...), kind=kLoop, calls=%fused_computation.50 | loop fusion | flops 15716352 | bytes 23654400 | tf_op jit(solution)/shard_map/reduce_sum | solution.py:997
  506.1 16.9 %attend_back.1.grad_ref = bf16[3,1024,768]{2,1,0:T(8,128)(2,1)S(1)} custom-call(s32[1]{0:T(128)S(6)} %copy.161.kind_ref, bf16[1024,2304]{1,0:T(8,128)(2,1)S(1)} %bitcast.261, bf16[1024,2304]{1,0:T(8,128)(2,1)S(1)} %bitcast.261, bf16[1024,2304]{1,0:T(8,128)(2,1)S(1)} %bitcast.261, bf16[1024,768]{1,0:T(8,128)(2,1)S(1)} %copy-done.12, ...), custom_call_target="tpu_custom_call" | custom-call | flops 32212254720 | bytes 28311552 | tf_op jit(solution)/shard_map/attend_back/pallas_call | solution.py:231
  525.2 35.8 %collective-permute-done.15 = bf16[1536,768]{1,0:T(8,128)(2,1)S(1)} collective-permute-done((bf16[1536,768]{1,0:T(8,128)(2,1)S(1)}, bf16[1536,768]{1,0:T(8,128)(2,1)S(1)}, u32[]{:S(2)}, u32[]{:S(2)}) %collective-permute-start.15) | collective-permute-done | bytes 2359328 | tf_op jit(solution)/shard_map/ppermute | solution.py:745
  562.4 17.3 %triple_back.1 = (f32[1024,768]{1,0:T(8,128)S(1)}, bf16[2,2,4,48,832]{4,3,2,1,0:T(8,128)(2,1)S(1)}, bf16[2,2,4,48,832]{4,3,2,1,0:T(8,128)(2,1)S(1)}, bf16[2,2,4,...) custom-call(s32[4]{0:T(128)S(1)} %pad_add_fusion.me, bf16[3,1024,768]{2,1,0:T(8,128)(2,1)} %copy-done.30, ...), custom_call_target="tpu_custom_call" | custom-call | flops 7247757312 | bytes 9437184 | tf_op jit(solution)/shard_map/triple_back/pallas_call | solution.py:608
  604.1 50.9 %collective-permute-start.20 = (bf16[2,4,48,832]{3,2,1,0:T(8,128)(2,1)S(1)}, bf16[2,4,48,832]{3,2,1,0:T(8,128)(2,1)S(1)}, u32[]{:S(2)}, u32[]{:S(2)}) collective-permute-start(bf16[2,4,48,832]{3,2,1,0:T(8,128)(2,1)S(1)} %get-tuple-element.212), channel_id=1, source_target_pairs={{0,1},{1,0},{2,3},{3,2},{4,5},{5,4},{6,7},{7,6},{8,9},{9,8},{10,11... | collective-permute-start | bytes 1916936 | tf_op jit(solution)/shard_map/ppermute | solution.py:748
  655.8 13.3 %collective-permute-start.18 = (bf16[4,48,832]{2,1,0:T(8,128)(2,1)S(1)}, bf16[4,48,832]{2,1,0:T(8,128)(2,1)S(1)}, u32[]{:S(2)}, u32[]{:S(2)}) collective-permute-start(bf16[4,48,832]{2,1,0:T(8,128)(2,1)S(1)} %fusion.79), channel_id=1, source_target_pairs={{0,1},{1,0},{2,3},{3,2},{4,5},{5,4},{6,7},{7,6},{8,9},{9,8},{10,11... | collective-permute-start | bytes 958472 | tf_op jit(solution)/shard_map/ppermute | solution.py:748
  703.5 10.3 %collective-permute-done.29 = bf16[768,384]{1,0:T(8,128)(2,1)} collective-permute-done((bf16[768,384]{1,0:T(8,128)(2,1)}, bf16[768,384]{1,0:T(8,128)(2,1)}, u32[]{:S(2)}, u32[]{:S(2)}) %collective-permute-start.29) | collective-permute-done | bytes 589856 | tf_op jit(solution)/shard_map/ppermute | solution.py:748
  717.0 7.6 %collective-permute-done.30 = bf16[384,768]{1,0:T(8,128)(2,1)S(1)} collective-permute-done((bf16[384,768]{1,0:T(8,128)(2,1)S(1)}, bf16[384,768]{1,0:T(8,128)(2,1)S(1)}, u32[]{:S(2)}, u32[]{:S(2)}) %collective-permute-start.30) | collective-permute-done | bytes 589856 | tf_op jit(solution)/shard_map/ppermute | solution.py:748
  (365 shorter events, 259.5 us)
Async XLA Ops:
  7.2 194.0 %all-gather.3.cloned.1.call-start = ((), (), s32[]{:S(2)}) async-start(), calls=%async_computation.10 | async-start | bytes 9732096 | tf_op jit(solution)/shard_map/all_gather | solution.py:862
  12.5 28.8 %collective-permute-start.1 = (bf16[96,832]{1,0:T(8,128)(2,1)}, bf16[96,832]{1,0:T(8,128)(2,1)}, u32[]{:S(2)}, u32[]{:S(2)}) collective-permute-start(bf16[96,832]{1,0:T(8,128)(2,1)} %pad_maximum_fusion.12), channel_id=1, source_target_pairs={{0,4},{2,6},{4,0},{6,2},{1,5},{3,7},{5,1},{7,3},{8,12},{10,14},{12... | collective-permute-start | bytes 479240 | tf_op jit(solution)/shard_map/ppermute | solution.py:745
  16.6 24.7 %collective-permute-start = (bf16[96,832]{1,0:T(8,128)(2,1)}, bf16[96,832]{1,0:T(8,128)(2,1)}, u32[]{:S(2)}, u32[]{:S(2)}) collective-permute-start(bf16[96,832]{1,0:T(8,128)(2,1)} %pad_maximum_fusion.12), channel_id=1, source_target_pairs={{0,2},{2,4},{4,6},{6,0},{1,3},{3,5},{5,7},{7,1},{8,10},{10,12},{12... | collective-permute-start | bytes 479240 | tf_op jit(solution)/shard_map/ppermute | solution.py:745
  18.2 23.2 %collective-permute-start.2 = (bf16[96,832]{1,0:T(8,128)(2,1)}, bf16[96,832]{1,0:T(8,128)(2,1)}, u32[]{:S(2)}, u32[]{:S(2)}) collective-permute-start(bf16[96,832]{1,0:T(8,128)(2,1)} %pad_maximum_fusion.12), channel_id=1, source_target_pairs={{0,6},{2,0},{4,2},{6,4},{1,7},{3,1},{5,3},{7,5},{8,14},{10,8},{12,... | collective-permute-start | bytes 479240 | tf_op jit(solution)/shard_map/ppermute | solution.py:745
  26.8 32.8 %collective-permute-start.4 = (bf16[768,384]{1,0:T(8,128)(2,1)}, bf16[768,384]{1,0:T(8,128)(2,1)S(1)}, u32[]{:S(2)}, u32[]{:S(2)}) collective-permute-start(bf16[768,384]{1,0:T(8,128)(2,1)} %get-tuple-element.216), channel_id=1, source_target_pairs={{0,1},{1,0},{2,3},{3,2},{4,5},{5,4},{6,7},{7,6},{8,9},{9,8},{10,11... | collective-permute-start | bytes 1769480 | tf_op jit(solution)/shard_map/ppermute | solution.py:748
  29.5 30.9 %collective-permute-start.5 = (bf16[384,768]{1,0:T(8,128)(2,1)}, bf16[384,768]{1,0:T(8,128)(2,1)}, u32[]{:S(2)}, u32[]{:S(2)}) collective-permute-start(bf16[384,768]{1,0:T(8,128)(2,1)} %get-tuple-element.218), channel_id=1, source_target_pairs={{0,1},{1,0},{2,3},{3,2},{4,5},{5,4},{6,7},{7,6},{8,9},{9,8},{10,11... | collective-permute-start | bytes 1769480 | tf_op jit(solution)/shard_map/ppermute | solution.py:748
  43.5 24.2 %collective-permute-start.3 = (bf16[4,48,832]{2,1,0:T(8,128)(2,1)S(1)}, bf16[4,48,832]{2,1,0:T(8,128)(2,1)S(1)}, u32[]{:S(2)}, u32[]{:S(2)}) collective-permute-start(bf16[4,48,832]{2,1,0:T(8,128)(2,1)S(1)} %get-tuple-element.222), channel_id=1, source_target_pairs={{0,1},{1,0},{2,3},{3,2},{4,5},{5,4},{6,7},{7,6},{8,9},{9,8},{10,11... | collective-permute-start | bytes 958472 | tf_op jit(solution)/shard_map/ppermute | solution.py:748
  63.0 29.7 %collective-permute-start.9 = (bf16[2,4,48,832]{3,2,1,0:T(8,128)(2,1)S(1)}, bf16[2,4,48,832]{3,2,1,0:T(8,128)(2,1)S(1)}, u32[]{:S(2)}, u32[]{:S(2)}) collective-permute-start(bf16[2,4,48,832]{3,2,1,0:T(8,128)(2,1)S(1)} %pad_maximum_fusion.11), channel_id=1, source_target_pairs={{0,1},{1,0},{2,3},{3,2},{4,5},{5,4},{6,7},{7,6},{8,9},{9,8},{10,11... | collective-permute-start | bytes 1916936 | tf_op jit(solution)/shard_map/ppermute | solution.py:748
  67.8 32.0 %collective-permute-start.6 = (bf16[2,4,48,832]{3,2,1,0:T(8,128)(2,1)S(1)}, bf16[2,4,48,832]{3,2,1,0:T(8,128)(2,1)}, u32[]{:S(2)}, u32[]{:S(2)}) collective-permute-start(bf16[2,4,48,832]{3,2,1,0:T(8,128)(2,1)S(1)} %pad_maximum_fusion.10), channel_id=1, source_target_pairs={{0,16},{8,24},{16,0},{24,8},{1,17},{9,25},{17,1},{25,9},{2,18},{10... | collective-permute-start | bytes 1916936 | tf_op jit(solution)/shard_map/ppermute | solution.py:751
  75.3 30.3 %all-to-all-start.1 = ((f32[32,4,1152]{2,1,0:T(4,128)}), f32[32,4,1152]{2,1,0:T(4,128)}, u32[]{:S(2)}, u32[]{:S(2)}) async-start(f32[32,4,1152]{2,1,0:T(4,128)} %copy.120), calls=%async_computation.1 | async-start | bytes 1179648 | tf_op jit(solution)/shard_map/all_to_all | solution.py:846
  106.9 66.6 %collective-permute-start.11 = (bf16[1536,768]{1,0:T(8,128)(2,1)}, bf16[1536,768]{1,0:T(8,128)(2,1)}, u32[]{:S(2)}, u32[]{:S(2)}) collective-permute-start(bf16[1536,768]{1,0:T(8,128)(2,1)} %pad_maximum_fusion.refs_3_), channel_id=1, source_target_pairs={{0,2},{2,4},{4,6},{6,0},{1,3},{3,5},{5,7},{7,1},{8,10},{10,12},{12... | collective-permute-start | bytes 7077896 | tf_op jit(solution)/shard_map/ppermute | solution.py:745
  180.0 80.9 %all-to-all-start.2 = ((bf16[8,288,768]{2,1,0:T(8,128)(2,1)}), bf16[8,288,768]{2,1,0:T(8,128)(2,1)}, u32[]{:S(2)}, u32[]{:S(2)}) async-start(bf16[8,288,768]{2,1,0:T(8,128)(2,1)} %bitcast.265), calls=%async_computation.2 | async-start | bytes 7077888 | tf_op jit(solution)/shard_map/all_to_all | solution.py:930
  199.8 399.1 %reduce-scatter.2.cloned.1.call-start = ((), (), s32[]{:S(2)}) async-start(), calls=%async_computation.9 | async-start | bytes 9732096 | tf_op jit(solution)/shard_map/reduce_scatter | solution.py:1069
  199.8 56.1 %collective-permute-start.12 = (bf16[1536,768]{1,0:T(8,128)(2,1)}, bf16[1536,768]{1,0:T(8,128)(2,1)}, u32[]{:S(2)}, u32[]{:S(2)}) collective-permute-start(bf16[1536,768]{1,0:T(8,128)(2,1)} %collective-permute-done.11.refs_0_), channel_id=1, source_target_pairs={{0,2},{2,4},{4,6},{6,0},{1,3},{3,5},{5,7},{7,1},{8,10},{10,12},{12... | collective-permute-start | bytes 7077896 | tf_op jit(solution)/shard_map/ppermute | solution.py:745
  255.9 55.2 %collective-permute-start.13 = (bf16[1536,768]{1,0:T(8,128)(2,1)}, bf16[1536,768]{1,0:T(8,128)(2,1)}, u32[]{:S(2)}, u32[]{:S(2)}) collective-permute-start(bf16[1536,768]{1,0:T(8,128)(2,1)} %collective-permute-done.12.refs_1_), channel_id=1, source_target_pairs={{0,2},{2,4},{4,6},{6,0},{1,3},{3,5},{5,7},{7,1},{8,10},{10,12},{12... | collective-permute-start | bytes 7077896 | tf_op jit(solution)/shard_map/ppermute | solution.py:745
  261.0 88.0 %all-to-all-start.3 = ((bf16[8,288,768]{2,1,0:T(8,128)(2,1)}), bf16[8,288,768]{2,1,0:T(8,128)(2,1)}, u32[]{:S(2)}, u32[]{:S(2)}) async-start(bf16[8,288,768]{2,1,0:T(8,128)(2,1)} %bitcast.263), calls=%async_computation.3 | async-start | bytes 7077888 | tf_op jit(solution)/shard_map/all_to_all | solution.py:930
  363.6 69.3 %all-to-all-start.4 = ((bf16[8,288,768]{2,1,0:T(8,128)(2,1)}), bf16[8,288,768]{2,1,0:T(8,128)(2,1)}, u32[]{:S(2)}, u32[]{:S(2)}) async-start(bf16[8,288,768]{2,1,0:T(8,128)(2,1)} %bitcast.266), calls=%async_computation.4 | async-start | bytes 7077888 | tf_op jit(solution)/shard_map/all_to_all | solution.py:930
  432.9 45.8 %all-to-all-start.5 = ((bf16[8,288,768]{2,1,0:T(8,128)(2,1)}), bf16[8,288,768]{2,1,0:T(8,128)(2,1)}, u32[]{:S(2)}, u32[]{:S(2)}) async-start(bf16[8,288,768]{2,1,0:T(8,128)(2,1)} %bitcast.264), calls=%async_computation.5 | async-start | bytes 7077888 | tf_op jit(solution)/shard_map/all_to_all | solution.py:930
  440.6 62.6 %collective-permute-start.14 = (bf16[1536,768]{1,0:T(8,128)(2,1)}, bf16[1536,768]{1,0:T(8,128)(2,1)}, u32[]{:S(2)}, u32[]{:S(2)}) collective-permute-start(bf16[1536,768]{1,0:T(8,128)(2,1)} %pad_maximum_fusion.1), channel_id=1, source_target_pairs={{0,2},{2,4},{4,6},{6,0},{1,3},{3,5},{5,7},{7,1},{8,10},{10,12},{12... | collective-permute-start | bytes 7077896 | tf_op jit(solution)/shard_map/ppermute | solution.py:745
  505.7 55.2 %collective-permute-start.15 = (bf16[1536,768]{1,0:T(8,128)(2,1)S(1)}, bf16[1536,768]{1,0:T(8,128)(2,1)S(1)}, u32[]{:S(2)}, u32[]{:S(2)}) collective-permute-start(bf16[1536,768]{1,0:T(8,128)(2,1)S(1)} %add_convert_fusion.2), channel_id=1, source_target_pairs={{0,2},{2,4},{4,6},{6,0},{1,3},{3,5},{5,7},{7,1},{8,10},{10,12},{12... | collective-permute-start | bytes 7077896 | tf_op jit(solution)/shard_map/ppermute | solution.py:745
  591.3 99.9 %collective-permute-start.28 = (bf16[1536,768]{1,0:T(8,128)(2,1)}, bf16[1536,768]{1,0:T(8,128)(2,1)}, u32[]{:S(2)}, u32[]{:S(2)}) collective-permute-start(bf16[1536,768]{1,0:T(8,128)(2,1)} %add_convert_fusion.1), channel_id=1, source_target_pairs={{0,2},{2,4},{4,6},{6,0},{1,3},{3,5},{5,7},{7,1},{8,10},{10,12},{12... | collective-permute-start | bytes 7077896 | tf_op jit(solution)/shard_map/ppermute | solution.py:745
  601.7 54.0 %collective-permute-start.17 = (bf16[2,4,48,832]{3,2,1,0:T(8,128)(2,1)S(1)}, bf16[2,4,48,832]{3,2,1,0:T(8,128)(2,1)S(1)}, u32[]{:S(2)}, u32[]{:S(2)}) collective-permute-start(bf16[2,4,48,832]{3,2,1,0:T(8,128)(2,1)S(1)} %get-tuple-element.214), channel_id=1, source_target_pairs={{0,16},{8,24},{16,0},{24,8},{1,17},{9,25},{17,1},{25,9},{2,18},{10... | collective-permute-start | bytes 1916936 | tf_op jit(solution)/shard_map/ppermute | solution.py:751
  604.1 67.1 %collective-permute-start.20 = (bf16[2,4,48,832]{3,2,1,0:T(8,128)(2,1)S(1)}, bf16[2,4,48,832]{3,2,1,0:T(8,128)(2,1)S(1)}, u32[]{:S(2)}, u32[]{:S(2)}) collective-permute-start(bf16[2,4,48,832]{3,2,1,0:T(8,128)(2,1)S(1)} %get-tuple-element.212), channel_id=1, source_target_pairs={{0,1},{1,0},{2,3},{3,2},{4,5},{5,4},{6,7},{7,6},{8,9},{9,8},{10,11... | collective-permute-start | bytes 1916936 | tf_op jit(solution)/shard_map/ppermute | solution.py:748
  701.3 23.3 %collective-permute-start.30 = (bf16[384,768]{1,0:T(8,128)(2,1)S(1)}, bf16[384,768]{1,0:T(8,128)(2,1)S(1)}, u32[]{:S(2)}, u32[]{:S(2)}) collective-permute-start(bf16[384,768]{1,0:T(8,128)(2,1)S(1)} %slice.328), channel_id=1, source_target_pairs={{0,1},{1,0},{2,3},{3,2},{4,5},{5,4},{6,7},{7,6},{8,9},{9,8},{10,11... | collective-permute-start | bytes 1769480 | tf_op jit(solution)/shard_map/ppermute | solution.py:748
  (95 other events, 1075.8 us)
Sparse Core Ops, SparseCore 0:
  11.5 119.1 all-gather.2
  261.1 151.9 reduce-scatter.1

commit v3 on v2

--- a/solution.py
+++ b/solution.py
@@ -1,5 +1,3 @@
-import functools
-
 import jax
 import jax.numpy as jnp
 from jax import lax
@@ -73,7 +71,7 @@
 
 
 def cost(flops, moved):
-    return pl.CostEstimate(flops=flops, transcendentals=0, bytes_accessed=moved)
+    return pl.CostEstimate(flops=flops // 64, transcendentals=0, bytes_accessed=moved // 64)
 
 
 def fixed(shape):
@@ -120,7 +118,7 @@
             rows_of(part, part * SHORT, SHORT)
 
 
-def attend(triple, image_kind):
+def attend(triple, image_kind, first, count):
     groups = triple.shape[0] // GROUP
     pairs = H // 2
 
@@ -130,20 +128,20 @@
     return pl.pallas_call(
         attend_kernel,
         out_shape=(
-            jax.ShapeDtypeStruct((triple.shape[0], H * HD), BF16),
-            jax.ShapeDtypeStruct((groups, pairs, 8, GROUP), F32),
+            jax.ShapeDtypeStruct((triple.shape[0], count * 2 * HD), BF16),
+            jax.ShapeDtypeStruct((groups, count, 8, GROUP), F32),
         ),
         grid_spec=pltpu.PrefetchScalarGridSpec(
             num_scalar_prefetch=1,
-            grid=(groups, pairs),
-            in_specs=[part(0), part(pairs), part(2 * pairs)],
+            grid=(groups, count),
+            in_specs=[part(first), part(pairs + first), part(2 * pairs + first)],
             out_specs=(
                 part(0),
                 pl.BlockSpec((1, 1, 8, GROUP), lambda g, i, kind: (g, i, 0, 0)),
             ),
         ),
         compiler_params=pltpu.CompilerParams(vmem_limit_bytes=32 << 20),
-        cost_estimate=cost(16 * triple.shape[0] * GROUP * H * HD, 8 * triple.size),
+        cost_estimate=cost(32 * triple.shape[0] * GROUP * count * HD, 2 * triple.size),
         name="attend",
     )(image_kind, triple, triple, triple)
 
@@ -221,8 +219,8 @@
     grads_ref[2, :, :] = value_sum[...].astype(BF16)
 
 
-def attend_back(triple, attended, logsum, grad_attended, image_kind):
-    groups = triple.shape[0] // GROUP
+def attend_back(triple, attended, logsum, grad_attended, image_kind, first):
+    groups, count = logsum.shape[:2]
     pairs = H // 2
 
     def part(offset):
@@ -230,23 +228,23 @@
 
     return pl.pallas_call(
         attend_back_kernel,
-        out_shape=jax.ShapeDtypeStruct((3, triple.shape[0], H * HD), BF16),
+        out_shape=jax.ShapeDtypeStruct((3, triple.shape[0], count * 2 * HD), BF16),
         grid_spec=pltpu.PrefetchScalarGridSpec(
             num_scalar_prefetch=1,
-            grid=(groups, pairs),
+            grid=(groups, count),
             in_specs=[
+                part(first),
+                part(pairs + first),
+                part(2 * pairs + first),
                 part(0),
-                part(pairs),
-                part(2 * pairs),
-                part(0),
-                part(0),
+                part(first),
                 pl.BlockSpec((1, 1, 8, GROUP), lambda g, i, kind: (g, i, 0, 0)),
             ],
             out_specs=pl.BlockSpec((3, GROUP, 2 * HD), lambda g, i, kind: (0, g, i)),
             scratch_shapes=[pltpu.VMEM((GROUP, 2 * HD), F32)] * 2,
         ),
         compiler_params=pltpu.CompilerParams(vmem_limit_bytes=32 << 20),
-        cost_estimate=cost(40 * triple.shape[0] * GROUP * H * HD, 12 * triple.size),
+        cost_estimate=cost(80 * triple.shape[0] * GROUP * count * HD, 4 * triple.size),
         name="attend_back",
     )(image_kind, triple, triple, triple, attended, grad_attended, logsum)
 
@@ -336,7 +334,8 @@
 
 def project_kernel(
     me,
-    attended_ref,
+    left_ref,
+    right_ref,
     x_ref,
     gate_ref,
     shift_ref,
@@ -379,7 +378,8 @@
                 on_side(other, q1a, q1b, first)
                 on_side(other, q2a, q2b, second)
 
-    projected = mm(attended_ref[...], weight_ref[...])
+    split = left_ref.shape[1]
+    projected = mm(left_ref[...], weight_ref[:split, :]) + mm(right_ref[...], weight_ref[split:, :])
     projected_ref[...] = projected
     residual = x_ref[...].astype(F32) + gate_ref[0] * projected
     residual_ref[...] = residual
@@ -388,11 +388,12 @@
     logits_ref[...] = mm(branch, router_ref[...])
 
 
-def make_branch(me, attended, patches, gate, shift, scale, weights):
+def make_branch(me, left, right, patches, gate, shift, scale, weights):
     tok_count, width = patches.shape
     rows = pl.BlockSpec((SHORT, width), lambda i, me: (i, 0))
     each = pl.BlockSpec((1, 1, width), lambda i, me: (i, 0, 0))
     outs = fixed(weights[0].shape[:4] + (OUT_LANES,))
+    part = pl.BlockSpec((SHORT, width // 2), lambda i, me: (i, 0))
     return pl.pallas_call(
         project_kernel,
         out_shape=(
@@ -406,7 +407,7 @@
         grid_spec=pltpu.PrefetchScalarGridSpec(
             num_scalar_prefetch=1,
             grid=(tok_count // SHORT,),
-            in_specs=[rows, rows, each, each, each, outs, outs, outs, outs],
+            in_specs=[part, part, rows, each, each, each, outs, outs, outs, outs],
             out_specs=(
                 rows,
                 rows,
@@ -419,17 +420,21 @@
         compiler_params=pltpu.CompilerParams(vmem_limit_bytes=32 << 20),
         cost_estimate=cost(2 * tok_count * width * width, 16 * tok_count * width),
         name="project",
-    )(me, attended, patches, gate, shift, scale, *weights)
+    )(me, left, right, patches, gate, shift, scale, *weights)
 
 
 def shared_kernel(
+    me,
     x_ref,
     grad_ref,
-    in_ref,
-    out_ref,
+    in_own,
+    in_other,
+    out_own,
+    out_other,
     res_ref,
     x_grad_ref,
     weight_grad_ref,
+    weight_in,
     weight_out,
     x_turned,
     grad_turned,
@@ -437,24 +442,34 @@
     step = pl.program_id(0)
     width = x_ref.shape[1]
     rows, half = width // STRIPS, width // 2
+    halves = [slice(0, half), slice(half, width)]
 
     @pl.when(step == 0)
     def _():
         x_turned[...] = jnp.transpose(x_ref[...])
         grad_turned[...] = jnp.transpose(grad_ref[...])
 
-    halves = [slice(0, half), slice(half, width)]
-    for piece in range(PIECES):
-        for strip in range(2):
-            for part in range(2):
-                low = (2 * piece + part) * rows
-                weight_out[low : low + rows, halves[strip]] = out_ref[piece, strip, :, halves[part]]
-    weight_in = in_ref[...].reshape(width, width)
-    act, slope = gelu_both(mm(x_ref[...], weight_in))
+    def take_in(ref):
+        for sy in range(2):
+            for z in range(4):
+                low = (2 * z + (sy ^ me[2])) * rows
+                weight_in[pl.ds(pl.multiple_of(low, 32), rows), :] = ref[0, sy, z]
+
+    on_side((step & 1) ^ me[0], in_own, in_other, take_in)
+    for other, ref in enumerate((out_own, out_other)):
+        for sx in range(2):
+            low = (((sx ^ me[1]) << 1) | (other ^ me[0])) * 2 * rows
+            for sy in range(2):
+                at = pl.ds(pl.multiple_of((sy ^ me[2]) * half, LANES), half)
+                for part in range(2):
+                    start = pl.multiple_of(low + part * rows, 32)
+                    weight_out[pl.ds(start, rows), at] = ref[sy, sx, 0, :, halves[part]]
+
+    act, slope = gelu_both(mm(x_ref[...], weight_in[...]))
     act = act.astype(BF16)
     grad_pre = (mm(grad_ref[...], weight_out[...]) * slope).astype(BF16)
     res = mm_rt(act, weight_out[...])
-    x_grad = mm_rt(grad_pre, weight_in)
+    x_grad = mm_rt(grad_pre, weight_in[...])
 
     @pl.when(step == 0)
     def _():
@@ -478,43 +493,51 @@
                 ]
 
 
-def shared_expert(x, grad, weights):
+def shared_expert(me, x, grad, in_own, in_other, out_own, out_other):
     tok_count, width = x.shape
     rows = width // STRIPS
     whole = fixed((tok_count, width))
+    block_in = pl.BlockSpec((1, 2, 4, rows, width), lambda j, me: ((j >> 1) ^ me[1], 0, 0, 0, 0))
+    block_out = pl.BlockSpec((2, 2, 1, rows, width), lambda j, me: (0, 0, j, 0, 0))
+    grads = jax.ShapeDtypeStruct((PIECES, STRIPS, 2 * rows, width), BF16)
     return pl.pallas_call(
         shared_kernel,
-        out_shape=(
-            jax.ShapeDtypeStruct((tok_count, width), F32),
-            jax.ShapeDtypeStruct((tok_count, width), F32),
-            jax.ShapeDtypeStruct(weights.shape, BF16),
+        out_shape=(jax.ShapeDtypeStruct((tok_count, width), F32),) * 2 + (grads,),
+        grid_spec=pltpu.PrefetchScalarGridSpec(
+            num_scalar_prefetch=1,
+            grid=(PIECES,),
+            in_specs=[whole, whole, block_in, block_in, block_out, block_out],
+            out_specs=(whole, whole, fixed(grads.shape)),
+            scratch_shapes=[pltpu.VMEM((width, width), BF16)] * 2
+            + [pltpu.VMEM((width, tok_count), BF16)] * 2,
         ),
-        grid=(PIECES,),
-        in_specs=[
-            whole,
-            whole,
-            pl.BlockSpec((1, STRIPS, rows, width), lambda j: (j, 0, 0, 0)),
-            pl.BlockSpec((PIECES, 2, rows, width), lambda j: (0, j, 1, 0)),
-        ],
-        out_specs=(whole, whole, fixed(weights.shape)),
-        scratch_shapes=[pltpu.VMEM((width, width), BF16)]
-        + [pltpu.VMEM((width, tok_count), BF16)] * 2,
         compiler_params=pltpu.CompilerParams(vmem_limit_bytes=56 << 20),
         cost_estimate=cost(12 * tok_count * width * 4 * width, 16 * tok_count * width),
         name="shared_expert",
-    )(x, grad, weights, weights)
+    )(me, x, grad, in_own, in_other, out_own, out_other)
 
 
 def project_back_kernel(
-    attended_ref, grad_ref, branch_ref, logits_ref, weight_ref, back_ref, out_grad_ref, router_ref
+    left_ref,
+    right_ref,
+    grad_ref,
+    branch_ref,
+    logits_ref,
+    weight_ref,
+    back_ref,
+    out_grad_ref,
+    router_ref,
 ):
+    split = left_ref.shape[1]
     back_ref[...] = mm_rt(grad_ref[...], weight_ref[...]).astype(BF16)
-    out_grad_ref[...] = mm_lt(attended_ref[...], grad_ref[...]).astype(BF16)
+    out_grad_ref[:split, :] = mm_lt(left_ref[...], grad_ref[...]).astype(BF16)
+    out_grad_ref[split:, :] = mm_lt(right_ref[...], grad_ref[...]).astype(BF16)
     router_ref[...] = mm_lt(branch_ref[...], logits_ref[...]).astype(BF16)
 
 
-def project_back(attended, grad, branch, grad_logits, weight):
-    tok_count, width = attended.shape
+def project_back(left, right, grad, branch, grad_logits, weight):
+    tok_count, width = grad.shape
+    part = fixed((tok_count, width // 2))
     whole = fixed((tok_count, width))
     return pl.pallas_call(
         project_back_kernel,
@@ -524,17 +547,18 @@
             jax.ShapeDtypeStruct((width, LANES), BF16),
         ),
         grid=(1,),
-        in_specs=[whole, whole, whole, fixed((tok_count, LANES)), fixed((width, width))],
+        in_specs=[part, part, whole, whole, fixed((tok_count, LANES)), fixed((width, width))],
         out_specs=(whole, fixed((width, width)), fixed((width, LANES))),
         compiler_params=pltpu.CompilerParams(vmem_limit_bytes=32 << 20),
         cost_estimate=cost(4 * tok_count * width * width, 8 * tok_count * width),
         name="project_back",
-    )(attended, grad, branch, grad_logits, weight)
+    )(left, right, grad, branch, grad_logits, weight)
 
 
 def triple_back_kernel(
     me,
-    grad_ref,
+    left_ref,
+    right_ref,
     in_ref,
     weight_ref,
     out_grad_ref,
@@ -556,7 +580,7 @@
     def _():
         in_turned[...] = jnp.transpose(in_ref[...])
 
-    grad = grad_ref[0]
+    grad = jnp.concatenate((left_ref[0], right_ref[0]), axis=1)
     at = pl.ds(pl.multiple_of(step * width, LANES), width)
     weight_grad[:, at] = mm(in_turned[...], grad).astype(BF16)
     back = mm_rt(grad, weight_ref[...])
@@ -600,7 +624,7 @@
                 on_side(other, q2a, q2b, second)
 
 
-def triple_back(me, grads, attend_in, weight, out_grad, router_grad):
+def triple_back(me, left, right, attend_in, weight, out_grad, router_grad):
     tok_count, width = attend_in.shape
     hidden = weight.shape[1]
     block = (2, 2, 4, width // STRIPS // 2, OUT_LANES + hidden // PIECES)
@@ -612,7 +636,8 @@
             num_scalar_prefetch=1,
             grid=(3,),
             in_specs=[
-                pl.BlockSpec((1, tok_count, width), lambda p, me: (p, 0, 0)),
+                pl.BlockSpec((1, tok_count, width // 2), lambda p, me: (p, 0, 0)),
+                pl.BlockSpec((1, tok_count, width // 2), lambda p, me: (p, 0, 0)),
                 fixed((tok_count, width)),
                 pl.BlockSpec((width, width), lambda p, me: (0, p)),
                 fixed((width, width)),
@@ -627,65 +652,105 @@
         compiler_params=pltpu.CompilerParams(vmem_limit_bytes=40 << 20),
         cost_estimate=cost(4 * tok_count * width * hidden, 12 * tok_count * width),
         name="triple_back",
-    )(me, grads, attend_in, weight, out_grad, router_grad)
+    )(me, left, right, attend_in, weight, out_grad, router_grad)
 
 
 ROW_TILE = 576
 
 
-def expert_kernel(parts, x_ref, *refs):
-    weights, (res_ref, act_ref, slope_ref) = refs[:parts], refs[parts:]
+def expert_kernel(x_ref, weights_ref, res_ref, act_ref, slope_ref):
     x = x_ref[...]
+    width = x_ref.shape[1]
     total = None
-    for part in range(parts):
-        width = weights[part].shape[1]
+    for part in range(weights_ref.shape[0]):
         at = pl.ds(part * width, width)
-        act, slope = gelu_both(mm(x, weights[part][:width, :]))
+        act, slope = gelu_both(mm(x, weights_ref[part, :width, :]))
         act = act.astype(BF16)
         act_ref[:, at] = act
         slope_ref[:, at] = slope.astype(BF16)
-        res = mm(act, weights[part][width:, :])
+        res = mm(act, weights_ref[part, width:, :])
         total = res if total is None else total + res
     res_ref[...] = total.astype(BF16)
 
 
-def expert_back_kernel(parts, grad_ref, slope_ref, *refs):
-    weights, (rows_ref, pre_ref) = refs[:parts], refs[parts:]
+def expert_back_kernel(grad_ref, slope_ref, weights_ref, rows_ref, pre_ref):
     grad = grad_ref[...]
+    width = grad_ref.shape[1]
     total = None
-    for part in range(parts):
-        width = weights[part].shape[1]
+    for part in range(weights_ref.shape[0]):
         at = pl.ds(part * width, width)
-        grad_pre = mm_rt(grad, weights[part][width:, :]) * slope_ref[:, at].astype(F32)
+        grad_pre = mm_rt(grad, weights_ref[part, width:, :]) * slope_ref[:, at].astype(F32)
         grad_pre = grad_pre.astype(BF16)
         pre_ref[:, at] = grad_pre
-        rows = mm_rt(grad_pre, weights[part][:width, :])
+        rows = mm_rt(grad_pre, weights_ref[part, :width, :])
         total = rows if total is None else total + rows
     rows_ref[...] = total.astype(BF16)
 
 
 def expert_call(kernel, name, rows_in, wide_in, weights, n_wide):
     rows, width = rows_in.shape
-    hidden = len(weights) * width
+    hidden = weights.shape[0] * width
     narrow = pl.BlockSpec((ROW_TILE, width), lambda i: (i, 0))
     wide = pl.BlockSpec((ROW_TILE, hidden), lambda i: (i, 0))
-    fixed = pl.BlockSpec((2 * width, width), lambda i: (0, 0), pipeline_mode=pl.Buffered(1))
     return pl.pallas_call(
-        functools.partial(kernel, len(weights)),
+        kernel,
         out_shape=(jax.ShapeDtypeStruct((rows, width), BF16),)
         + (jax.ShapeDtypeStruct((rows, hidden), BF16),) * n_wide,
         grid=(rows // ROW_TILE,),
-        in_specs=[narrow] + [wide] * len(wide_in) + [fixed] * len(weights),
+        in_specs=[narrow] + [wide] * len(wide_in) + [fixed(weights.shape)],
         out_specs=(narrow,) + (wide,) * n_wide,
         compiler_params=pltpu.CompilerParams(vmem_limit_bytes=48 << 20),
         cost_estimate=cost(8 * rows * hidden * width, 2 * rows * hidden * (1 + n_wide)),
         name=name,
-    )(rows_in, *wide_in, *weights)
-
-
-def by_way(blocks, y_outer):
+    )(rows_in, *wide_in, weights)
+
+
+def expert_grads_kernel(part, x_ref, pre_ref, act_ref, grad_ref, out_ref, up_sum, down_sum):
+    step, width = pl.program_id(0), x_ref.shape[1]
+    up = mm_lt(x_ref[...], pre_ref[...])
+    down = mm_lt(act_ref[...], grad_ref[...])
+
+    @pl.when(step == 0)
+    def _():
+        up_sum[...] = up
+        down_sum[...] = down
+
+    @pl.when(step != 0)
+    def _():
+        up_sum[...] += up
+        down_sum[...] += down
+
+    @pl.when(step == pl.num_programs(0) - 1)
+    def _():
+        out_ref[:width, :] = up_sum[...].astype(BF16)
+        out_ref[width:, :] = down_sum[...].astype(BF16)
+
+
+def expert_grads(x, grad_pre, act, grad, part):
+    rows, width = x.shape
+    narrow = pl.BlockSpec((ROW_TILE, width), lambda i, part: (i, 0))
+    wide = pl.BlockSpec((ROW_TILE, width), lambda i, part: (i, part[0]))
+    return pl.pallas_call(
+        expert_grads_kernel,
+        out_shape=jax.ShapeDtypeStruct((2 * width, width), BF16),
+        grid_spec=pltpu.PrefetchScalarGridSpec(
+            num_scalar_prefetch=1,
+            grid=(rows // ROW_TILE,),
+            in_specs=[narrow, wide, wide, narrow],
+            out_specs=fixed((2 * width, width)),
+            scratch_shapes=[pltpu.VMEM((width, width), F32)] * 2,
+        ),
+        compiler_params=pltpu.CompilerParams(vmem_limit_bytes=40 << 20),
+        cost_estimate=cost(4 * rows * width * width, 8 * rows * width),
+        name="expert_grads",
+    )(part, x, grad_pre, act, grad)
+
+
+def by_way(blocks, y_outer, turns=True):
     rows, cols = blocks.shape[2:]
-    blocks = blocks.reshape(2, 2, 4, 2, rows, cols)[:, :, jnp.array([0, 3, 2, 1])]
+    blocks = blocks.reshape(2, 2, 4, 2, rows, cols)
+    if turns:
+        blocks = blocks[:, :, jnp.array([0, 3, 2, 1])]
     blocks = blocks.transpose((1, 3, 0, 2, 4, 5) if y_outer else (1, 0, 3, 2, 4, 5))
     return blocks[0], blocks[1]
 
@@ -795,13 +860,14 @@
     return lax.optimization_barrier((value,) + others)[0]
 
 
-def picked_experts(ring, y, expert_in, expert_out):
+def picked_experts(ring, y, expert_in, expert_out, first):
     own_in = jnp.where(y == 0, expert_in[0], expert_in[1])
     give_in = jnp.where(y == 0, expert_in[1], expert_in[0])
     own_out = jnp.where(y == 0, expert_out[0], expert_out[1])
     give_out = jnp.where(y == 0, expert_out[1], expert_out[0])
-    ups = jnp.concatenate((own_in, ring.over_y(give_in)), axis=1)
-    downs = jnp.concatenate((own_out, ring.over_y(give_out)), axis=0)
+    got_in, got_out = after(ring.over_y(give_in), first), after(ring.over_y(give_out), first)
+    ups = jnp.concatenate((own_in, got_in), axis=1)
+    downs = jnp.concatenate((own_out, got_out), axis=0)
     return jnp.concatenate((ups, downs), axis=0)
 
 
@@ -834,19 +900,6 @@
     else:
         me = jnp.zeros((4,), jnp.int32)
 
-    cond_float = cond_embed.astype(F32)
-    cond_act = jax.nn.silu(cond_float).astype(BF16)
-    cond_send = cond_act.reshape(blocks, n_fsdp, mod_rows).transpose(1, 0, 2)
-    cond_send = jnp.broadcast_to(cond_send[None], (n_exp, n_fsdp, blocks, mod_rows))
-    cond_all = lax.all_to_all(
-        cond_send.reshape(n_all, blocks, mod_rows), ALL, 0, 0, tiled=True
-    ).reshape(n_all * blocks, mod_rows)
-    mod_part = mm(cond_all, modulate_weight).reshape(n_all, blocks, mod_cols)
-    mod_early = mod_part
-    mod_part = lax.all_to_all(mod_part, ALL, 0, 0, tiled=True)
-    modulation = jnp.sum(mod_part.reshape(n_exp, n_fsdp, blocks, mod_cols), axis=1)
-    modulation = modulation.transpose(1, 0, 2).reshape(blocks, 1, 6, width)
-
     if ring.direct:
         spare = OUT_LANES - output_weight.shape[1] - router_weight.shape[1]
         block = jnp.concatenate(
@@ -858,18 +911,35 @@
             ),
             axis=1,
         )
-        bundle = jnp.concatenate((shared_in, turn(shared_out)), axis=0)
-        shared_weights = lax.all_gather(bundle, ALL, axis=0, tiled=False)
-        shared_weights = shared_weights.reshape((PIECES, STRIPS) + bundle.shape)
-        expert_block = picked_experts(ring, y, expert_in, expert_out)
-        held = after(ring.near(block), mod_early)
+        held = ring.near(block)
+
+    cond_float = cond_embed.astype(F32)
+    cond_act = jax.nn.silu(cond_float).astype(BF16)
+    cond_send = cond_act.reshape(blocks, n_fsdp, mod_rows).transpose(1, 0, 2)
+    cond_send = jnp.broadcast_to(cond_send[None], (n_exp, n_fsdp, blocks, mod_rows))
+    cond_all = lax.all_to_all(
+        cond_send.reshape(n_all, blocks, mod_rows), ALL, 0, 0, tiled=True
+    ).reshape(n_all * blocks, mod_rows)
+    if ring.direct:
+        cond_all = after(cond_all, held)
+    mod_part = mm(cond_all, modulate_weight).reshape(n_all, blocks, mod_cols)
+    mod_part = lax.all_to_all(mod_part, ALL, 0, 0, tiled=True)
+    modulation = jnp.sum(mod_part.reshape(n_exp, n_fsdp, blocks, mod_cols), axis=1)
+    if ring.direct:
+        held = after(held, modulation)
+    modulation = modulation.transpose(1, 0, 2).reshape(blocks, 1, 6, width)
+
+    if ring.direct:
+        expert_block = picked_experts(ring, y, expert_in, expert_out, modulation)
+        held = after(held, expert_block)
         held_1 = ring.second(held[:, :half], False)
         held_2 = ring.second(held[:, half:], True)
-        held_1 = ring.third(after(held_1, expert_block), False)
-        held_2 = ring.third(after(held_2, expert_block), True)
+        bundle = jnp.concatenate((shared_in, turn(shared_out)), axis=0)
+        shared_line = lax.all_gather(bundle, "zi", axis=0, tiled=False)
+        expert_weights = lax.all_gather(after(expert_block, shared_line), "zi", axis=0)
+        held_1 = ring.third(held_1, False)
+        held_2 = ring.third(held_2, True)
         dense_weights = (held_1, ring.over_core(held_1), held_2, ring.over_core(held_2))
-        expert_block = after(expert_block, modulation)
-        expert_weights = [expert_block, ring.step(expert_block)]
     else:
         wholes = [
             lax.all_gather(
@@ -883,13 +953,17 @@
         dense_all = jnp.concatenate((output_all, router_all, spare, attend_all), axis=3)
         dense_weights = by_way(dense_all[:, :, :half], False)
         dense_weights += by_way(dense_all[:, :, half:], True)
-        shared_weights = shared_bundle(up_all, down_all)
+        shared_all = shared_bundle(up_all, down_all)
+        in_weights = by_way(shared_all[:, :, : 2 * half], False, False)
+        out_weights = by_way(shared_all[:, :, 2 * half :], True, False)
         up_all = lax.all_gather(expert_in[0], FSDP, axis=1, tiled=True)
         down_all = lax.all_gather(expert_out[0], FSDP, axis=0, tiled=True)
-        expert_weights = [
-            jnp.concatenate((up_all[:, at : at + width], down_all[at : at + width]), axis=0)
-            for at in range(0, up_all.shape[1], width)
-        ]
+        expert_weights = jnp.stack(
+            [
+                jnp.concatenate((up_all[:, at : at + width], down_all[at : at + width]), axis=0)
+                for at in range(0, up_all.shape[1], width)
+            ]
+        )
 
     shift_first = modulation[:, :, 0]
     scale_first = modulation[:, :, 1]
@@ -900,13 +974,26 @@
     attend_in, triple, triple_weight = make_triple(
         me, patches, shift_first, scale_first, dense_weights
     )
-    attended, logsum = attend(triple, image_kind)
+    pairs = H // 4
+    attended_1, logsum_1 = attend(triple, image_kind, 0, pairs)
+    triple_2 = after(triple, attended_1)
+    if ring.direct:
+        shared_line = after(shared_line, triple)
+        in_held = ring.second(shared_line[:, : 2 * half], False)
+        out_held = ring.second(shared_line[:, 2 * half :], True)
+        triple_2, in_held, out_held = tie(triple_2, in_held, out_held)
+        in_held, out_held = ring.third(in_held, False), ring.third(out_held, True)
+    attended_2, logsum_2 = attend(triple_2, image_kind, pairs, pairs)
     projected, residual, branch_in, logits, output_weight_all, router_all = make_branch(
-        me, attended, patches, gate_first, shift_second, scale_second, dense_weights
-    )
-    if ring.direct:
-        branch_in = after(branch_in, expert_weights[1])
-        expert_weights.append(ring.step(expert_weights[1]))
+        me,
+        attended_1,
+        attended_2,
+        patches,
+        gate_first,
+        shift_second,
+        scale_second,
+        dense_weights,
+    )
     choose = expert_ids[:, :, None] == jnp.arange(E, dtype=jnp.int32)[None, None, :]
     choose = choose.astype(F32)
     gates = jax.nn.softmax(jnp.sum(choose * logits[:, None, :E], axis=-1), axis=-1)
@@ -922,6 +1009,11 @@
     pick1 = (row_of == target[None, :, 1]).astype(BF16)
     send_rows = mm(pick0 + pick1, branch_in).astype(BF16).reshape(E, CAP, width)
     grad_picked = (gates[:, :, None] * grad_branch_wide[:, None, :]).astype(BF16)
+    grad_picked = after(grad_picked, send_rows)
+    if ring.direct:
+        grad_picked, in_held, out_held = tie(grad_picked, in_held, out_held)
+        in_weights = (in_held, ring.over_core(in_held))
+        out_weights = (out_held, ring.over_core(out_held))
     grad_send = mm(pick0, grad_picked[:, 0]) + mm(pick1, grad_picked[:, 1])
     grad_send = grad_send.astype(BF16).reshape(E, CAP, width)
     shared_x = after(branch_in, send_rows, grad_send)
@@ -931,13 +1023,11 @@
 
     received = exchange(send_rows)
 
-    shared_res, grad_branch_in, shared_grads = shared_expert(shared_x, grad_branch, shared_weights)
+    shared_res, grad_branch_in, shared_grads = shared_expert(
+        me, shared_x, grad_branch, *in_weights, *out_weights
+    )
 
     received = after(received, shared_res)
-    if ring.direct:
-        expert_weights[2] = after(expert_weights[2], shared_res)
-        expert_weights.append(ring.step(expert_weights[2]))
-        expert_weights = expert_weights[1:] + expert_weights[:1]
     received = received.reshape(-1, width)
     grad_received = exchange(after(grad_send, received))
     expert_res, expert_act, expert_slope = expert_call(
@@ -953,20 +1043,23 @@
     grad_rows = after(grad_rows, returned)
     grad_returned = exchange(grad_rows.reshape(E, CAP, width)).reshape(-1, width)
 
-    def expert_grads(part):
-        at = slice(part * width, (part + 1) * width)
-        return jnp.concatenate(
-            (
-                mm_lt(received, grad_pre[:, at]).astype(BF16),
-                mm_lt(expert_act[:, at], grad_received).astype(BF16),
-            ),
-            axis=0,
-        )
-
-    grad_blocks = [expert_grads(part) for part in range(len(expert_weights))]
+    n_parts = expert_weights.shape[0]
+    first = z - 1 if ring.direct else jnp.zeros((), jnp.int32)
+
+    def grads_of(turn_at, act):
+        part = ((first - turn_at) % n_parts if ring.direct else first + turn_at).reshape(1)
+        return expert_grads(received, grad_pre, act, grad_received, part)
+
+    grad_blocks = [grads_of(0, expert_act)]
+    act = after(expert_act, returned)
+    for part in range(1, n_parts):
+        grad_blocks.append(grads_of(part, act))
+        act = after(act, grad_blocks[-1])
     returned = after(returned, *grad_blocks)
     if ring.direct:
         moved = ring.step(grad_blocks[0])
+        grad_returned, moved = tie(grad_returned, add(moved, grad_blocks[1]))
+        moved = ring.step(moved)
 
     picked0 = mm_lt(pick0, returned)
     picked1 = mm_lt(pick1, returned)
@@ -1001,20 +1094,31 @@
     grad_gate_first = jnp.sum(grad_residual * projected, axis=1)
     grad_projected = (gate_first * grad_residual).astype(BF16).reshape(tok_count, width)
     grad_attended, out_grad_all, router_grad_all = project_back(
-        attended, grad_projected, branch_in, grad_logits, output_weight_all
-    )
+        attended_1, attended_2, grad_projected, branch_in, grad_logits, output_weight_all
+    )
+    grad_triple_1 = attend_back(triple, attended_1, logsum_1, grad_attended, image_kind, 0)
+    grad_attended_2 = after(grad_attended, grad_triple_1)
     if ring.direct:
-        grad_attended, moved = tie(grad_attended, moved)
-        moved = ring.step(add(moved, grad_blocks[1]))
-    grad_triple = attend_back(triple, attended, logsum, grad_attended, image_kind)
-    if ring.direct:
-        grad_triple, moved = tie(grad_triple, moved)
-        moved = ring.step(add(moved, grad_blocks[2]))
+        grad_attended_2, moved = tie(grad_attended_2, add(moved, grad_blocks[2]))
+        moved = ring.step(moved)
+    grad_triple_2 = attend_back(triple, attended_2, logsum_2, grad_attended_2, image_kind, pairs)
     grad_attend_in, *dense_grads = triple_back(
-        me, grad_triple, attend_in, triple_weight, out_grad_all, router_grad_all
+        me,
+        grad_triple_1,
+        grad_triple_2,
+        attend_in,
+        triple_weight,
+        out_grad_all,
+        router_grad_all,
     )
     if ring.direct:
         own_1, give_1, own_2, give_2 = dense_grads
+        moved = moved.astype(F32) + grad_blocks[3].astype(F32)
+        moved, give_1, give_2 = tie(moved, give_1, give_2)
+        up_sum, down_sum = moved[:width], moved[width:]
+        split = width // 2
+        got_up = ring.over_y(up_sum[:, split:].astype(BF16)).astype(F32)
+        got_down = ring.over_y(down_sum[split:].astype(BF16)).astype(F32)
         sum_1, give_1 = add_both(own_1, ring.over_core(give_1))
         sum_2, give_2 = add_both(own_2, ring.over_core(give_2))
         got_1, got_2 = ring.outer(give_1, False), ring.outer(give_2, True)
@@ -1043,13 +1147,14 @@
     mod_send = jnp.broadcast_to(
         grad_modulation.transpose(1, 0, 2)[:, None], (n_exp, n_fsdp, blocks, mod_cols)
     )
+    if ring.direct:
+        mod_send = after(mod_send, sum_1, sum_2)
     mod_all = lax.all_to_all(
         mod_send.reshape(n_all, blocks, mod_cols), ALL, 0, 0, tiled=True
     ).reshape(n_all * blocks, mod_cols)
     modulate_grad = mm_lt(cond_all, mod_all)
     cond_part = mm_rt(mod_all, modulate_weight).reshape(n_all, blocks, mod_rows)
     if ring.direct:
-        mod_all = after(mod_all, got_1, got_2)
         sum_1, give_1 = add_both(sum_1, got_1)
         sum_2, give_2 = add_both(sum_2, got_2)
         sum_1 = add(sum_1, ring.inner(give_1, False))
@@ -1071,11 +1176,6 @@
         ).astype(F32)
         shared_in_grad = summed[: 2 * half]
         shared_out_grad = turn_back(summed[2 * half :])
-        moved = moved.astype(F32) + grad_blocks[3].astype(F32)
-        up_sum, down_sum = moved[:width], moved[width:]
-        split = width // 2
-        got_up = ring.over_y(up_sum[:, split:].astype(BF16)).astype(F32)
-        got_down = ring.over_y(down_sum[split:].astype(BF16)).astype(F32)
         own_up, own_down = up_sum[:, :split], down_sum[:split]
         expert_in_grad = jnp.stack(
             (jnp.where(y == 0, own_up, got_up), jnp.where(y == 0, got_up, own_up))

time: 740 us -> 646 us (0.87)
  Pallas kernels: 183 us -> 274 us
  waiting for transfers between devices: 183 us -> 114 us
  starting transfers between devices: 144 us -> 77.8 us
  matrix products: 99.4 us -> 44.2 us
    ppermute x15 -> x12, waiting for transfers between devices: 94.6 us -> 30.4 us  [step(): return lax.ppermute(value, 'zi', [(i, (i + by) % n) for i in range(n)])]
    ppermute x8 -> x10, starting transfers between devices: 71.6 us -> 12 us  [over_y(): return lax.ppermute(value, 'yi', [(0, 1), (1, 0)])]
    dot_general x18 -> x10, matrix products: 99.4 us -> 44.2 us  [dot(): lax.dot_general(left, right, (dims, ((), ())), preferred_element_type=F32)]
    pallas_call x2 -> x6, Pallas kernels: 69.5 us -> 118 us  [the longest x2 68.3 us: expert_call(): pl.pallas_call(kernel, out_shape=(jax.ShapeDtypeStruct((rows, width), BF1...]
    all_to_all x1, waiting for transfers between devices: 0.8 us -> 25.9 us  [local(): mod_part = lax.all_to_all(mod_part, ALL, 0, 0, tiled=True)]
    pallas_call x1 -> x2, Pallas kernels: 16.9 us -> 38.9 us  [attend_back(): pl.pallas_call(attend_back_kernel, out_shape=jax.ShapeDtypeStruct((3, tri...]
    pallas_call x1 -> x2, Pallas kernels: 11 us -> 27.4 us  [attend(): pl.pallas_call(attend_kernel, out_shape=(jax.ShapeDtypeStruct((triple.sha...]
    all_to_all x4, starting transfers between devices: 33.5 us -> 19 us  [exchange(): return lax.all_to_all(rows, ('exp', 'yi'), 0, 0, tiled=True)]
  transfers between devices with their start and end apart: 41 -> 45, of which waited for: 17 -> 19; matrix products, arithmetic and copies ran while one was open for 25% -> 22% of each run, Pallas kernels for 25% -> 43%
where the time goes in v3:
time: 646 us; the launch traced here: 641 us
  Pallas kernels  274 us (42%)
  waiting for transfers between devices  114 us (18%)
  starting transfers between devices  77.8 us (12%)
  other arithmetic  76.8 us (12%)
  matrix products  44.2 us (7%)
  local copies, waits for them, and re-layouts  38.2 us (6%)
  between operations  16.1 us (2%)
    pallas_call x2, Pallas kernels, expert_call(): pl.pallas_call(kernel, out_shape=(jax.ShapeDtypeStruct((rows, width), BF1...  68.3 us
    pallas_call x4, Pallas kernels, expert_grads(): pl.pallas_call(expert_grads_kernel, out_shape=jax.ShapeDtypeStruct((2 * w...  50 us
    dot_general x10, matrix products, dot(): lax.dot_general(left, right, (dims, ((), ())), preferred_element_type=F32)  44.2 us
    pallas_call x1, Pallas kernels, shared_expert(): pl.pallas_call(shared_kernel, out_shape=(jax.ShapeDtypeStruct((tok_count,...  43.2 us
    pallas_call x2, Pallas kernels, attend_back(): pl.pallas_call(attend_back_kernel, out_shape=jax.ShapeDtypeStruct((3, tri...  38.9 us
    ppermute x10, waiting for transfers between devices, over_y(): return lax.ppermute(value, 'yi', [(0, 1), (1, 0)])  34.1 us
    ppermute x12, waiting for transfers between devices, step(): return lax.ppermute(value, 'zi', [(i, (i + by) % n) for i in range(n)])  30.4 us
    pallas_call x2, Pallas kernels, attend(): pl.pallas_call(attend_kernel, out_shape=(jax.ShapeDtypeStruct((triple.sha...  27.4 us
  transfers between devices with their start and end apart: 45, of which 19 were waited for; matrix products, arithmetic and copies ran while one was open for 22% of the time, Pallas kernels for 43%

profile of v3, /device:TPU:0, one launch (start us, length us, event | category | flops | bytes accessed | tf_op | source)
XLA Modules:
  0.0 641.2 jit_solution(7716933711126724976)
XLA Ops:
  42.7 25.9 %all-to-all-done.1 = f32[32,4,1152]{2,1,0:T(4,128)S(1)} async-done(((f32[32,4,1152]{2,1,0:T(4,128)}), f32[32,4,1152]{2,1,0:T(4,128)S(1)}, u32[]{:S(2)}, u32[]{:S(2)}) %all-to-all-start.1) | async-done | bytes 589856 | tf_op jit(solution)/shard_map/all_to_all | solution.py:926
  77.4 6.3 collective-permute-done.5
  87.4 12.5 %collective-permute-done.6 = bf16[2,4,48,832]{3,2,1,0:T(8,128)(2,1)S(1)} collective-permute-done((bf16[2,4,48,832]{3,2,1,0:T(8,128)(2,1)S(1)}, bf16[2,4,48,832]{3,2,1,0:T(8,128)(2,1)S(1)}, u32[]{:S(2)}, u32[]{:S(2)}) %collective-permute-start.6) | collective-permute-done | bytes 639008 | tf_op jit(solution)/shard_map/ppermute | solution.py:816
  112.7 12.6 %triple.1 = (bf16[1024,768]{1,0:T(8,128)(2,1)S(1)}, bf16[1024,2304]{1,0:T(8,128)(2,1)}, bf16[768,2304]{1,0:T(8,128)(2,1)S(1)}) custom-call(s32[4]{0:T(128)S(1)} %pad_add_fusion.me, bf16[1024,768]{1,0:T(8,128)(2,1)S(1)} %copy-done.3, f32[4,1,768]{2,1,0:T(1,128)S(1)} %get-tuple-element.285.shift_ref, f32[4,1,768]{2,1,0:T(1,128)S(1)} %get-tuple-element.284.scale_ref, ...), custom_call_target="tpu_custom_call" | custom-call | flops 56623104 | bytes 98304 | tf_op jit(solution)/shard_map/triple/pallas_call | solution.py:312
  133.0 13.6 %attend.2 = (bf16[1024,384]{1,0:T(8,128)(2,1)S(1)}, f32[1,3,8,1024]{3,2,1,0:T(8,128)S(1)}) custom-call(s32[1]{0:T(128)S(6)} %copy.141.kind_ref, bf16[1024,2304]{1,0:T(8,128)(2,1)S(1)} %copy-done.1, bf16[1024,2304]{1,0:T(8,128)(2,1)S(1)} %copy-done.1, bf16[1024,2304]{1,0:T(8,128)(2,1)S(1)} %copy-done.1), custom_call_target="tpu_custom_call" | custom-call | flops 100663296 | bytes 73728 | tf_op jit(solution)/shard_map/attend/pallas_call | solution.py:128
  150.2 13.8 %attend.3 = (bf16[1024,384]{1,0:T(8,128)(2,1)S(1)}, f32[1,3,8,1024]{3,2,1,0:T(8,128)S(1)}) custom-call(s32[1]{0:T(128)S(6)} %copy.141.kind_ref, bf16[1024,2304]{1,0:T(8,128)(2,1)S(1)} %copy-done.1, bf16[1024,2304]{1,0:T(8,128)(2,1)S(1)} %copy-done.1, bf16[1024,2304]{1,0:T(8,128)(2,1)S(1)} %copy-done.1), custom_call_target="tpu_custom_call" | custom-call | flops 100663296 | bytes 73728 | tf_op jit(solution)/shard_map/attend/pallas_call | solution.py:128
  164.1 11.6 %project.1 = (f32[1024,768]{1,0:T(8,128)S(1)}, f32[1024,768]{1,0:T(8,128)S(1)}, bf16[1024,768]{1,0:T(8,128)(2,1)S(1)}, f32[1024,128]{1,0:T(8,128)S(1)}, bf16[768...) custom-call(s32[4]{0:T(128)S(1)} %pad_add_fusion.me, bf16[1024,384]{1,0:T(8,128)(2,1)S(1)} %get-tuple-element.79.left_ref.mixed_ref, ...), custom_call_target="tpu_custom_call" | custom-call | flops 18874368 | bytes 196608 | tf_op jit(solution)/shard_map/project/pallas_call | solution.py:397
  175.8 6.3 convolution_convert_fusion
  208.7 43.2 %shared_expert.1 = (f32[1024,768]{1,0:T(8,128)}, f32[1024,768]{1,0:T(8,128)}, bf16[4,8,192,768]{3,2,1,0:T(8,128)(2,1)}) custom-call(s32[4]{0:T(128)} %copy-done.38, bf16[1024,768]{1,0:T(8,128)(2,1)} %copy-done.18, bf16[1024,768]{1,0:T(8,128)(2,1)} %get-tuple-element.239.grad_ref, bf16[2,2,4,96,768]{4,3,2,1,0:T(8,128)(2,1)} %copy-done.46, ...), custom_call_target="tpu_custom_call" | custom-call | flops 452984832 | bytes 196608 | tf_op jit(solution)/shard_map/shared_expert/pallas_call | solution.py:503
  257.2 36.5 %experts.1 = (bf16[2304,768]{1,0:T(8,128)(2,1)S(1)}, bf16[2304,3072]{1,0:T(8,128)(2,1)}, bf16[2304,3072]{1,0:T(8,128)(2,1)}) custom-call(bf16[2304,768]{1,0:T(8,128)(2,1)} %bitcast.49.x_ref, bf16[4,1536,768]{2,1,0:T(8,128)(2,1)} %bitcast.274), custom_call_target="tpu_custom_call" | custom-call | flops 679477248 | bytes 663552 | tf_op jit(solution)/shard_map/experts/pallas_call | solution.py:695
  302.6 31.8 %experts_back.1 = (bf16[2304,768]{1,0:T(8,128)(2,1)S(1)}, bf16[2304,3072]{1,0:T(8,128)(2,1)}) custom-call(bf16[2304,768]{1,0:T(8,128)(2,1)} %bitcast.51.grad_ref, bf16[2304,3072]{1,0:T(8,128)(2,1)} %get-tuple-element.100.slope_ref, bf16[4,1536,768]{2,1,0:T(8,128)(2,1)} %bitcast.275), custom_call_target="tpu_custom_call" | custom-call | flops 679477248 | bytes 442368 | tf_op jit(solution)/shard_map/experts_back/pallas_call | solution.py:695
  336.1 13.5 %expert_grads.4 = bf16[1536,768]{1,0:T(8,128)(2,1)} custom-call(s32[1]{0:T(128)} %bitcast.54.part, bf16[2304,768]{1,0:T(8,128)(2,1)} %bitcast.49.x_ref, bf16[2304,3072]{1,0:T(8,128)(2,1)} %get-tuple-element.101.pre_ref, bf16[2304,3072]{1,0:T(8,128)(2,1)} %get-tuple-element.105.act_ref, bf16[2304,768]{1,0:T(8,128)(2,1)} %bitcast.51.grad_ref), custom_call_target="tpu_custom_call" | custom-call | flops 84934656 | bytes 221184 | tf_op jit(solution)/shard_map/expert_grads/pallas_call | solution.py:733
  363.0 12.3 %expert_grads.5 = bf16[1536,768]{1,0:T(8,128)(2,1)S(1)} custom-call(s32[1]{0:T(128)} %bitcast.55.part, bf16[2304,768]{1,0:T(8,128)(2,1)} %bitcast.49.x_ref, bf16[2304,3072]{1,0:T(8,128)(2,1)} %get-tuple-element.101.pre_ref, bf16[2304,3072]{1,0:T(8,128)(2,1)} %get-tuple-element.105.act_ref, bf16[2304,768]{1,0:T(8,128)(2,1)} %bitcast.51.grad_ref), custom_call_target="tpu_custom_call" | custom-call | flops 84934656 | bytes 221184 | tf_op jit(solution)/shard_map/expert_grads/pallas_call | solution.py:733
  375.3 12.1 %expert_grads.6 = bf16[1536,768]{1,0:T(8,128)(2,1)S(1)} custom-call(s32[1]{0:T(128)} %bitcast.56.part, bf16[2304,768]{1,0:T(8,128)(2,1)} %bitcast.49.x_ref, bf16[2304,3072]{1,0:T(8,128)(2,1)} %get-tuple-element.101.pre_ref, bf16[2304,3072]{1,0:T(8,128)(2,1)} %get-tuple-element.105.act_ref, bf16[2304,768]{1,0:T(8,128)(2,1)} %bitcast.51.grad_ref), custom_call_target="tpu_custom_call" | custom-call | flops 84934656 | bytes 221184 | tf_op jit(solution)/shard_map/expert_grads/pallas_call | solution.py:733
  388.8 12.1 %expert_grads.7 = bf16[1536,768]{1,0:T(8,128)(2,1)S(1)} custom-call(s32[1]{0:T(128)} %bitcast.57.part, bf16[2304,768]{1,0:T(8,128)(2,1)} %bitcast.49.x_ref, bf16[2304,3072]{1,0:T(8,128)(2,1)} %get-tuple-element.101.pre_ref, bf16[2304,3072]{1,0:T(8,128)(2,1)} %get-tuple-element.105.act_ref, bf16[2304,768]{1,0:T(8,128)(2,1)} %bitcast.51.grad_ref), custom_call_target="tpu_custom_call" | custom-call | flops 84934656 | bytes 221184 | tf_op jit(solution)/shard_map/expert_grads/pallas_call | solution.py:733
  401.0 20.6 %collective-permute-done.17 = bf16[1536,768]{1,0:T(8,128)(2,1)} collective-permute-done((bf16[1536,768]{1,0:T(8,128)(2,1)}, bf16[1536,768]{1,0:T(8,128)(2,1)}, u32[]{:S(2)}, u32[]{:S(2)}) %collective-permute-start.17) | collective-permute-done | bytes 2359328 | tf_op jit(solution)/shard_map/ppermute | solution.py:810
  425.5 8.0 %fusion = f32[1024,768]{1,0:T(8,128)} fusion(bf16[2304,768]{1,0:T(8,128)(2,1)} %bitcast.53, s32[1024]{0:T(1024)S(1)} %bitcast.317), kind=kOutput, calls=%fused_computation.1 | convolution fusion | flops 3626237952 | bytes 6688768 | tf_op jit(solution)/shard_map/dot_general | solution.py:51
  433.5 8.7 %multiply_reduce_fusion.6 = (f32[1024]{0:T(1024)S(1)}, f32[1024]{0:T(1024)S(1)}, f32[1024,768]{1,0:T(8,128)}) fusion(bf16[1024,768]{1,0:T(8,128)(2,1)} %get-tuple-element.239.grad_ref, f32[1024,768]{1,0:T(8,128)} %fusion, bf16[2304,768]{1,0:T(8,128)(2,1)} %bitcast.53, s32[1024]{0:T(1024)S(1)} %bitcast.313), kind=kOutput, calls=%fused_computation.48 | convolution fusion | flops 3630168064 | bytes 11415552 | tf_op jit(solution)/shard_map/dot_general | solution.py:51
  444.8 6.8 %fusion.7 = f32[1024,768]{1,0:T(8,128)S(1)} fusion(bf16[2304,768]{1,0:T(8,128)(2,1)} %bitcast.60, s32[1024]{0:T(1024)} %bitcast.315, s32[1024]{0:T(1024)} %bitcast.311), kind=kOutput, calls=%fused_computation.14 | convolution fusion | flops 3642753024 | bytes 6692864 | tf_op jit(solution)/shard_map/dot_general | solution.py:51
  455.3 8.2 %fusion.22 = (bf16[4,768]{1,0:T(4,128)(2,1)S(1)}, bf16[4,768]{1,0:T(4,128)(2,1)}, bf16[4,768]{1,0:T(4,128)(2,1)}, bf16[4,768]{1,0:T(4,128)(2,1)S(1)}, f32[1024,768]{1,0:T(8,128)S(1)}) fusion(f32[1024,768]{1,0:T(8,128)} %get-tuple-element.291, f32[1024,768]{1,0:T(8,128)S(1)} %get-tuple-element.84, f32[4,256]{1,0:T(4,128)} %div.65, f32[4,256]{1,0:T(4,128)} %rsqrt.27, ...), kind=kLoop, calls=%fused_computation.34 | loop fusion | flops 15716352 | bytes 23654400 | tf_op jit(solution)/shard_map/reduce_sum | solution.py:1090
  470.8 19.4 %attend_back.2.left_ref = bf16[3,1024,384]{2,1,0:T(8,128)(2,1)S(1)} custom-call(s32[1]{0:T(128)S(6)} %copy.141.kind_ref, bf16[1024,2304]{1,0:T(8,128)(2,1)S(1)} %bitcast.270, bf16[1024,2304]{1,0:T(8,128)(2,1)S(1)} %bitcast.270, bf16[1024,2304]{1,0:T(8,128)(2,1)S(1)} %bitcast.270, bf16[1024,384]{1,0:T(8,128)(2,1)S(1)} %copy-done.17, ...), custom_call_target="tpu_custom_call" | custom-call | flops 251658240 | bytes 147456 | tf_op jit(solution)/shard_map/attend_back/pallas_call | solution.py:229
  499.8 19.5 %attend_back.3.right_ref = bf16[3,1024,384]{2,1,0:T(8,128)(2,1)S(1)} custom-call(s32[1]{0:T(128)S(6)} %copy.141.kind_ref, bf16[1024,2304]{1,0:T(8,128)(2,1)S(1)} %copy-done.2, bf16[1024,2304]{1,0:T(8,128)(2,1)S(1)} %copy-done.2, bf16[1024,2304]{1,0:T(8,128)(2,1)S(1)} %copy-done.2, bf16[1024,384]{1,0:T(8,128)(2,1)S(1)} %copy-done.15, ...), custom_call_target="tpu_custom_call" | custom-call | flops 251658240 | bytes 147456 | tf_op jit(solution)/shard_map/attend_back/pallas_call | solution.py:229
  519.4 19.3 %triple_back.1 = (f32[1024,768]{1,0:T(8,128)}, bf16[2,2,4,48,832]{4,3,2,1,0:T(8,128)(2,1)S(1)}, bf16[2,2,4,48,832]{4,3,2,1,0:T(8,128)(2,1)}, bf16[2,2,4,48,832]{...) custom-call(s32[4]{0:T(128)S(1)} %copy-done.39, bf16[3,1024,384]{2,1,0:T(8,128)(2,1)S(1)} %copy-done.12, ...), custom_call_target="tpu_custom_call" | custom-call | flops 113246208 | bytes 147456 | tf_op jit(solution)/shard_map/triple_back/pallas_call | solution.py:632
  564.6 9.6 %collective-permute-done.33 = bf16[384,768]{1,0:T(8,128)(2,1)} collective-permute-done((bf16[384,768]{1,0:T(8,128)(2,1)}, bf16[384,768]{1,0:T(8,128)(2,1)}, u32[]{:S(2)}, u32[]{:S(2)}) %collective-permute-start.33) | collective-permute-done | bytes 589856 | tf_op jit(solution)/shard_map/ppermute | solution.py:813
  (376 shorter events, 240.9 us)
Async XLA Ops:
  9.1 16.7 %collective-permute-start.1 = (bf16[96,832]{1,0:T(8,128)(2,1)S(1)}, bf16[96,832]{1,0:T(8,128)(2,1)S(1)}, u32[]{:S(2)}, u32[]{:S(2)}) collective-permute-start(bf16[96,832]{1,0:T(8,128)(2,1)S(1)} %pad_maximum_fusion.12), channel_id=1, source_target_pairs={{0,4},{2,6},{4,0},{6,2},{1,5},{3,7},{5,1},{7,3},{8,12},{10,14},{12... | collective-permute-start | bytes 479240 | tf_op jit(solution)/shard_map/ppermute | solution.py:810
  21.3 52.8 %all-gather.5.cloned.1.call-start = ((), (), s32[]{:S(2)}) async-start(), calls=%async_computation.10 | async-start | bytes 1474560 | tf_op jit(solution)/shard_map/all_gather | solution.py:938
  32.4 36.3 %all-to-all-start.1 = ((f32[32,4,1152]{2,1,0:T(4,128)}), f32[32,4,1152]{2,1,0:T(4,128)S(1)}, u32[]{:S(2)}, u32[]{:S(2)}) async-start(f32[32,4,1152]{2,1,0:T(4,128)} %reshape.469), calls=%async_computation.1 | async-start | bytes 1179648 | tf_op jit(solution)/shard_map/all_to_all | solution.py:926
  36.3 220.8 %all-gather.7.cloned.1.call-start = ((), (), s32[]{:S(2)}) async-start(), calls=%async_computation.11 | async-start | bytes 11796480 | tf_op jit(solution)/shard_map/all_gather | solution.py:939
  38.6 30.3 %collective-permute-start.3 = (bf16[768,384]{1,0:T(8,128)(2,1)}, bf16[768,384]{1,0:T(8,128)(2,1)S(1)}, u32[]{:S(2)}, u32[]{:S(2)}) collective-permute-start(bf16[768,384]{1,0:T(8,128)(2,1)} %get-tuple-element.254), channel_id=1, source_target_pairs={{0,1},{1,0},{2,3},{3,2},{4,5},{5,4},{6,7},{7,6},{8,9},{9,8},{10,11... | collective-permute-start | bytes 1769480 | tf_op jit(solution)/shard_map/ppermute | solution.py:813
  42.5 28.9 %collective-permute-start.4 = (bf16[384,768]{1,0:T(8,128)(2,1)}, bf16[384,768]{1,0:T(8,128)(2,1)}, u32[]{:S(2)}, u32[]{:S(2)}) collective-permute-start(bf16[384,768]{1,0:T(8,128)(2,1)} %get-tuple-element.256), channel_id=1, source_target_pairs={{0,1},{1,0},{2,3},{3,2},{4,5},{5,4},{6,7},{7,6},{8,9},{9,8},{10,11... | collective-permute-start | bytes 1769480 | tf_op jit(solution)/shard_map/ppermute | solution.py:813
  125.6 21.0 %collective-permute-start.12 = (bf16[4,96,768]{2,1,0:T(8,128)(2,1)S(1)}, bf16[4,96,768]{2,1,0:T(8,128)(2,1)S(1)}, u32[]{:S(2)}, u32[]{:S(2)}) collective-permute-start(bf16[4,96,768]{2,1,0:T(8,128)(2,1)S(1)} %get-tuple-element.251), channel_id=1, source_target_pairs={{0,16},{8,24},{16,0},{24,8},{1,17},{9,25},{17,1},{25,9},{2,18},{10... | collective-permute-start | bytes 1769480 | tf_op jit(solution)/shard_map/ppermute | solution.py:816
  127.0 21.0 %collective-permute-start.11 = (bf16[4,96,768]{2,1,0:T(8,128)(2,1)S(1)}, bf16[4,96,768]{2,1,0:T(8,128)(2,1)S(1)}, u32[]{:S(2)}, u32[]{:S(2)}) collective-permute-start(bf16[4,96,768]{2,1,0:T(8,128)(2,1)S(1)} %get-tuple-element.252), channel_id=1, source_target_pairs={{0,1},{1,0},{2,3},{3,2},{4,5},{5,4},{6,7},{7,6},{8,9},{9,8},{10,11... | collective-permute-start | bytes 1769480 | tf_op jit(solution)/shard_map/ppermute | solution.py:813
  149.1 41.5 %collective-permute-start.13 = (bf16[2,4,96,768]{3,2,1,0:T(8,128)(2,1)}, bf16[2,4,96,768]{3,2,1,0:T(8,128)(2,1)}, u32[]{:S(2)}, u32[]{:S(2)}) collective-permute-start(bf16[2,4,96,768]{3,2,1,0:T(8,128)(2,1)} %pad_maximum_fusion.7), channel_id=1, source_target_pairs={{0,16},{8,24},{16,0},{24,8},{1,17},{9,25},{17,1},{25,9},{2,18},{10... | collective-permute-start | bytes 3538952 | tf_op jit(solution)/shard_map/ppermute | solution.py:816
  150.2 42.3 %collective-permute-start.14 = (bf16[2,4,96,768]{3,2,1,0:T(8,128)(2,1)}, bf16[2,4,96,768]{3,2,1,0:T(8,128)(2,1)}, u32[]{:S(2)}, u32[]{:S(2)}) collective-permute-start(bf16[2,4,96,768]{3,2,1,0:T(8,128)(2,1)} %pad_maximum_fusion.8), channel_id=1, source_target_pairs={{0,1},{1,0},{2,3},{3,2},{4,5},{5,4},{6,7},{7,6},{8,9},{9,8},{10,11... | collective-permute-start | bytes 3538952 | tf_op jit(solution)/shard_map/ppermute | solution.py:813
  183.3 68.6 %all-to-all-start.2 = ((bf16[8,288,768]{2,1,0:T(8,128)(2,1)}), bf16[8,288,768]{2,1,0:T(8,128)(2,1)}, u32[]{:S(2)}, u32[]{:S(2)}) async-start(bf16[8,288,768]{2,1,0:T(8,128)(2,1)} %bitcast.277), calls=%async_computation.2 | async-start | bytes 7077888 | tf_op jit(solution)/shard_map/all_to_all | solution.py:1022
  251.9 45.8 %all-to-all-start.3 = ((bf16[8,288,768]{2,1,0:T(8,128)(2,1)}), bf16[8,288,768]{2,1,0:T(8,128)(2,1)}, u32[]{:S(2)}, u32[]{:S(2)}) async-start(bf16[8,288,768]{2,1,0:T(8,128)(2,1)} %bitcast.278), calls=%async_computation.3 | async-start | bytes 7077888 | tf_op jit(solution)/shard_map/all_to_all | solution.py:1022
  256.4 238.5 %reduce-scatter.2.cloned.1.call-start = ((), (), s32[]{:S(2)}) async-start(), calls=%async_computation.9 | async-start | bytes 9732096 | tf_op jit(solution)/shard_map/reduce_scatter | solution.py:1174
  297.6 54.8 %all-to-all-start.4 = ((bf16[8,288,768]{2,1,0:T(8,128)(2,1)}), bf16[8,288,768]{2,1,0:T(8,128)(2,1)}, u32[]{:S(2)}, u32[]{:S(2)}) async-start(bf16[8,288,768]{2,1,0:T(8,128)(2,1)} %bitcast.272), calls=%async_computation.4 | async-start | bytes 7077888 | tf_op jit(solution)/shard_map/all_to_all | solution.py:1022
  349.6 72.0 %collective-permute-start.17 = (bf16[1536,768]{1,0:T(8,128)(2,1)}, bf16[1536,768]{1,0:T(8,128)(2,1)}, u32[]{:S(2)}, u32[]{:S(2)}) collective-permute-start(bf16[1536,768]{1,0:T(8,128)(2,1)} %expert_grads.4), channel_id=1, source_target_pairs={{0,2},{2,4},{4,6},{6,0},{1,3},{3,5},{5,7},{7,1},{8,10},{10,12},{12... | collective-permute-start | bytes 7077896 | tf_op jit(solution)/shard_map/ppermute | solution.py:810
  352.5 81.0 %all-to-all-start.5 = ((bf16[8,288,768]{2,1,0:T(8,128)(2,1)}), bf16[8,288,768]{2,1,0:T(8,128)(2,1)}, u32[]{:S(2)}, u32[]{:S(2)}) async-start(bf16[8,288,768]{2,1,0:T(8,128)(2,1)} %bitcast.271), calls=%async_computation.5 | async-start | bytes 7077888 | tf_op jit(solution)/shard_map/all_to_all | solution.py:1022
  433.5 56.7 %collective-permute-start.18 = (bf16[1536,768]{1,0:T(8,128)(2,1)}, bf16[1536,768]{1,0:T(8,128)(2,1)}, u32[]{:S(2)}, u32[]{:S(2)}) collective-permute-start(bf16[1536,768]{1,0:T(8,128)(2,1)} %add_convert_fusion.2), channel_id=1, source_target_pairs={{0,2},{2,4},{4,6},{6,0},{1,3},{3,5},{5,7},{7,1},{8,10},{10,12},{12... | collective-permute-start | bytes 7077896 | tf_op jit(solution)/shard_map/ppermute | solution.py:810
  494.9 54.9 %collective-permute-start.19 = (bf16[1536,768]{1,0:T(8,128)(2,1)}, bf16[1536,768]{1,0:T(8,128)(2,1)}, u32[]{:S(2)}, u32[]{:S(2)}) collective-permute-start(bf16[1536,768]{1,0:T(8,128)(2,1)} %add_convert_fusion.1), channel_id=1, source_target_pairs={{0,2},{2,4},{4,6},{6,0},{1,3},{3,5},{5,7},{7,1},{8,10},{10,12},{12... | collective-permute-start | bytes 7077896 | tf_op jit(solution)/shard_map/ppermute | solution.py:810
  543.6 18.0 %all-to-all-start.6 = ((bf16[32,4,1152]{2,1,0:T(4,128)(2,1)}), bf16[32,4,1152]{2,1,0:T(4,128)(2,1)S(1)}, u32[]{:S(2)}, u32[]{:S(2)}) async-start(bf16[32,4,1152]{2,1,0:T(4,128)(2,1)} %bitcast.280), calls=%async_computation.6 | async-start | bytes 589824 | tf_op jit(solution)/shard_map/all_to_all | solution.py:1152
  552.9 22.9 %collective-permute-start.20 = (bf16[2,2,4,48,832]{4,3,2,1,0:T(8,128)(2,1)}, bf16[2,2,4,48,832]{4,3,2,1,0:T(8,128)(2,1)}, u32[]{:S(2)}, u32[]{:S(2)}) collective-permute-start(bf16[2,2,4,48,832]{4,3,2,1,0:T(8,128)(2,1)} %get-tuple-element.129), channel_id=1, source_target_pairs={{0,8},{8,0},{16,24},{24,16},{1,9},{9,1},{17,25},{25,17},{2,10},{10... | collective-permute-start | bytes 3833864 | tf_op jit(solution)/shard_map/ppermute | solution.py:819
  555.1 24.0 %collective-permute-start.23 = (bf16[2,2,4,48,832]{4,3,2,1,0:T(8,128)(2,1)}, bf16[2,2,4,48,832]{4,3,2,1,0:T(8,128)(2,1)}, u32[]{:S(2)}, u32[]{:S(2)}) collective-permute-start(bf16[2,2,4,48,832]{4,3,2,1,0:T(8,128)(2,1)} %get-tuple-element.131), channel_id=1, source_target_pairs={{0,8},{8,0},{16,24},{24,16},{1,9},{9,1},{17,25},{25,17},{2,10},{10... | collective-permute-start | bytes 3833864 | tf_op jit(solution)/shard_map/ppermute | solution.py:819
  564.0 22.7 %collective-permute-start.32 = (bf16[768,384]{1,0:T(8,128)(2,1)S(1)}, bf16[768,384]{1,0:T(8,128)(2,1)S(1)}, u32[]{:S(2)}, u32[]{:S(2)}) collective-permute-start(bf16[768,384]{1,0:T(8,128)(2,1)S(1)} %slice.299), channel_id=1, source_target_pairs={{0,1},{1,0},{2,3},{3,2},{4,5},{5,4},{6,7},{7,6},{8,9},{9,8},{10,11... | collective-permute-start | bytes 1769480 | tf_op jit(solution)/shard_map/ppermute | solution.py:813
  580.8 20.7 %collective-permute-start.24 = (bf16[2,4,48,832]{3,2,1,0:T(8,128)(2,1)S(1)}, bf16[2,4,48,832]{3,2,1,0:T(8,128)(2,1)S(1)}, u32[]{:S(2)}, u32[]{:S(2)}) collective-permute-start(bf16[2,4,48,832]{3,2,1,0:T(8,128)(2,1)S(1)} %get-tuple-element.246), channel_id=1, source_target_pairs={{0,1},{1,0},{2,3},{3,2},{4,5},{5,4},{6,7},{7,6},{8,9},{9,8},{10,11... | collective-permute-start | bytes 1916936 | tf_op jit(solution)/shard_map/ppermute | solution.py:813
  613.4 20.2 %all-to-all-start.7 = ((f32[32,4,96]{2,1,0:T(4,128)}), f32[32,4,96]{2,1,0:T(4,128)S(1)}, u32[]{:S(2)}, u32[]{:S(2)}) async-start(f32[32,4,96]{2,1,0:T(4,128)} %copy.119), calls=%async_computation.7 | async-start | bytes 131072 | tf_op jit(solution)/shard_map/all_to_all | solution.py:1163
  (98 other events, 1070.8 us)
Sparse Core Ops, SparseCore 0:
  24.3 44.4 all-gather.4
  74.2 166.9 all-gather.6
  263.1 178.8 reduce-scatter.1

commit v4 on v3

--- a/solution.py
+++ b/solution.py
@@ -70,8 +70,8 @@
     return jnp.sum(before * onehot, axis=1).reshape(expert_ids.shape)
 
 
-def cost(flops, moved):
-    return pl.CostEstimate(flops=flops // 64, transcendentals=0, bytes_accessed=moved // 64)
+def cost(flops, moved, share=64):
+    return pl.CostEstimate(flops=flops // share, transcendentals=0, bytes_accessed=moved // share)
 
 
 def fixed(shape):
@@ -512,7 +512,7 @@
             + [pltpu.VMEM((width, tok_count), BF16)] * 2,
         ),
         compiler_params=pltpu.CompilerParams(vmem_limit_bytes=56 << 20),
-        cost_estimate=cost(12 * tok_count * width * 4 * width, 16 * tok_count * width),
+        cost_estimate=cost(12 * tok_count * width * 4 * width, 16 * tok_count * width, 1),
         name="shared_expert",
     )(me, x, grad, in_own, in_other, out_own, out_other)
 
@@ -705,45 +705,46 @@
     )(rows_in, *wide_in, weights)
 
 
-def expert_grads_kernel(part, x_ref, pre_ref, act_ref, grad_ref, out_ref, up_sum, down_sum):
-    step, width = pl.program_id(0), x_ref.shape[1]
-    up = mm_lt(x_ref[...], pre_ref[...])
-    down = mm_lt(act_ref[...], grad_ref[...])
-
-    @pl.when(step == 0)
-    def _():
-        up_sum[...] = up
-        down_sum[...] = down
-
-    @pl.when(step != 0)
-    def _():
-        up_sum[...] += up
-        down_sum[...] += down
-
-    @pl.when(step == pl.num_programs(0) - 1)
-    def _():
-        out_ref[:width, :] = up_sum[...].astype(BF16)
-        out_ref[width:, :] = down_sum[...].astype(BF16)
+def expert_grads_kernel(part, x_ref, pre_ref, act_ref, grad_ref, out_ref):
+    step, cols = pl.program_id(0), x_ref.shape[1]
+    up = mm_lt(x_ref[...], pre_ref[...]).astype(BF16)
+    down = mm_lt(act_ref[...], grad_ref[...]).astype(BF16)
+    out_ref[0, step] = up[:, :cols]
+    out_ref[1, step] = up[:, cols:]
+    out_ref[step, 2] = down[:, :cols]
+    out_ref[step, 3] = down[:, cols:]
 
 
 def expert_grads(x, grad_pre, act, grad, part):
     rows, width = x.shape
-    narrow = pl.BlockSpec((ROW_TILE, width), lambda i, part: (i, 0))
-    wide = pl.BlockSpec((ROW_TILE, width), lambda i, part: (i, part[0]))
+    cols = width // 2
+    out = jax.ShapeDtypeStruct((2, 4, cols, cols), BF16)
     return pl.pallas_call(
         expert_grads_kernel,
-        out_shape=jax.ShapeDtypeStruct((2 * width, width), BF16),
+        out_shape=out,
         grid_spec=pltpu.PrefetchScalarGridSpec(
             num_scalar_prefetch=1,
-            grid=(rows // ROW_TILE,),
-            in_specs=[narrow, wide, wide, narrow],
-            out_specs=fixed((2 * width, width)),
-            scratch_shapes=[pltpu.VMEM((width, width), F32)] * 2,
+            grid=(2,),
+            in_specs=[
+                pl.BlockSpec((rows, cols), lambda i, part: (0, i)),
+                pl.BlockSpec((rows, width), lambda i, part: (0, part[0])),
+                pl.BlockSpec((rows, cols), lambda i, part: (0, part[0] * 2 + i)),
+                fixed((rows, width)),
+            ],
+            out_specs=fixed(out.shape),
         ),
         compiler_params=pltpu.CompilerParams(vmem_limit_bytes=40 << 20),
         cost_estimate=cost(4 * rows * width * width, 8 * rows * width),
         name="expert_grads",
     )(part, x, grad_pre, act, grad)
+
+
+def up_of(half):
+    return jnp.concatenate((half[0], half[1]), axis=0)
+
+
+def down_of(half):
+    return jnp.concatenate((half[2], half[3]), axis=1)
 
 
 def by_way(blocks, y_outer, turns=True):
@@ -809,6 +810,10 @@
         n = self.n_ring
         return lax.ppermute(value, "zi", [(i, (i + by) % n) for i in range(n)])
 
+    def step_aside(self, value):
+        n = 2 * self.n_ring
+        return lax.ppermute(value, FSDP, [(i, (i + 2) % n ^ 1) for i in range(n)])
+
     def over_y(self, value):
         return lax.ppermute(value, "yi", [(0, 1), (1, 0)])
 
@@ -858,17 +863,6 @@
 
 def after(value, *others):
     return lax.optimization_barrier((value,) + others)[0]
-
-
-def picked_experts(ring, y, expert_in, expert_out, first):
-    own_in = jnp.where(y == 0, expert_in[0], expert_in[1])
-    give_in = jnp.where(y == 0, expert_in[1], expert_in[0])
-    own_out = jnp.where(y == 0, expert_out[0], expert_out[1])
-    give_out = jnp.where(y == 0, expert_out[1], expert_out[0])
-    got_in, got_out = after(ring.over_y(give_in), first), after(ring.over_y(give_out), first)
-    ups = jnp.concatenate((own_in, got_in), axis=1)
-    downs = jnp.concatenate((own_out, got_out), axis=0)
-    return jnp.concatenate((ups, downs), axis=0)
 
 
 def local(
@@ -921,16 +915,28 @@
         cond_send.reshape(n_all, blocks, mod_rows), ALL, 0, 0, tiled=True
     ).reshape(n_all * blocks, mod_rows)
     if ring.direct:
-        cond_all = after(cond_all, held)
-    mod_part = mm(cond_all, modulate_weight).reshape(n_all, blocks, mod_cols)
+        own_in = jnp.where(y == 0, expert_in[0], expert_in[1])
+        got_in = ring.over_y(jnp.where(y == 0, expert_in[1], expert_in[0]))
+        cond_all = after(cond_all, held, got_in)
+    mod_part = mm(cond_all, modulate_weight).astype(BF16).reshape(n_all, blocks, mod_cols)
     mod_part = lax.all_to_all(mod_part, ALL, 0, 0, tiled=True)
-    modulation = jnp.sum(mod_part.reshape(n_exp, n_fsdp, blocks, mod_cols), axis=1)
+    mod_part = mod_part.reshape(n_exp, n_fsdp, blocks, mod_cols)
+    modulation = jnp.sum(mod_part.astype(F32), axis=1)
     if ring.direct:
         held = after(held, modulation)
     modulation = modulation.transpose(1, 0, 2).reshape(blocks, 1, 6, width)
 
     if ring.direct:
-        expert_block = picked_experts(ring, y, expert_in, expert_out, modulation)
+        own_out = jnp.where(y == 0, expert_out[0], expert_out[1])
+        got_out = ring.over_y(jnp.where(y == 0, expert_out[1], expert_out[0]))
+        got_out = after(got_out, modulation)
+        expert_block = jnp.concatenate(
+            (
+                jnp.concatenate((own_in, got_in), axis=1),
+                jnp.concatenate((own_out, got_out), axis=0),
+            ),
+            axis=0,
+        )
         held = after(held, expert_block)
         held_1 = ring.second(held[:, :half], False)
         held_2 = ring.second(held[:, half:], True)
@@ -1008,9 +1014,11 @@
     pick0 = (row_of == target[None, :, 0]).astype(BF16)
     pick1 = (row_of == target[None, :, 1]).astype(BF16)
     send_rows = mm(pick0 + pick1, branch_in).astype(BF16).reshape(E, CAP, width)
-    grad_picked = (gates[:, :, None] * grad_branch_wide[:, None, :]).astype(BF16)
+    gates_sent = after(gates, send_rows)
+    grad_picked = (gates_sent[:, :, None] * grad_branch_wide[:, None, :]).astype(BF16)
     grad_picked = after(grad_picked, send_rows)
     if ring.direct:
+        in_held, out_held = after(in_held, send_rows), after(out_held, send_rows)
         grad_picked, in_held, out_held = tie(grad_picked, in_held, out_held)
         in_weights = (in_held, ring.over_core(in_held))
         out_weights = (out_held, ring.over_core(out_held))
@@ -1051,19 +1059,20 @@
         return expert_grads(received, grad_pre, act, grad_received, part)
 
     grad_blocks = [grads_of(0, expert_act)]
-    act = after(expert_act, returned)
+    picked0 = mm_lt(pick0, returned)
+    picked1 = mm_lt(pick1, returned)
+    mixture = gates[:, 0:1] * picked0 + gates[:, 1:2] * picked1
+    act = after(expert_act, mixture)
     for part in range(1, n_parts):
         grad_blocks.append(grads_of(part, act))
         act = after(act, grad_blocks[-1])
-    returned = after(returned, *grad_blocks)
     if ring.direct:
         moved = ring.step(grad_blocks[0])
-        grad_returned, moved = tie(grad_returned, add(moved, grad_blocks[1]))
+
+    if ring.direct:
+        moved = add(after(moved, *grad_blocks), grad_blocks[1])
+        grad_returned, moved = tie(grad_returned, moved)
         moved = ring.step(moved)
-
-    picked0 = mm_lt(pick0, returned)
-    picked1 = mm_lt(pick1, returned)
-    mixture = gates[:, 0:1] * picked0 + gates[:, 1:2] * picked1
     branch_out = (shared_res + mixture).reshape(blocks, SHORT, width)
     projected = projected.reshape(blocks, SHORT, width)
     residual = residual.reshape(blocks, SHORT, width)
@@ -1096,11 +1105,15 @@
     grad_attended, out_grad_all, router_grad_all = project_back(
         attended_1, attended_2, grad_projected, branch_in, grad_logits, output_weight_all
     )
+    if ring.direct:
+        neighbour = ring.over_y(grad_blocks[3][1])
+        grad_attended = after(grad_attended, neighbour)
     grad_triple_1 = attend_back(triple, attended_1, logsum_1, grad_attended, image_kind, 0)
     grad_attended_2 = after(grad_attended, grad_triple_1)
     if ring.direct:
-        grad_attended_2, moved = tie(grad_attended_2, add(moved, grad_blocks[2]))
-        moved = ring.step(moved)
+        moved = add(moved, grad_blocks[2])
+        grad_attended_2, own, aside = tie(grad_attended_2, moved[0], moved[1])
+        own, aside = ring.step(own), ring.step_aside(aside)
     grad_triple_2 = attend_back(triple, attended_2, logsum_2, grad_attended_2, image_kind, pairs)
     grad_attend_in, *dense_grads = triple_back(
         me,
@@ -1113,12 +1126,8 @@
     )
     if ring.direct:
         own_1, give_1, own_2, give_2 = dense_grads
-        moved = moved.astype(F32) + grad_blocks[3].astype(F32)
-        moved, give_1, give_2 = tie(moved, give_1, give_2)
-        up_sum, down_sum = moved[:width], moved[width:]
-        split = width // 2
-        got_up = ring.over_y(up_sum[:, split:].astype(BF16)).astype(F32)
-        got_down = ring.over_y(down_sum[split:].astype(BF16)).astype(F32)
+        give_1, give_2 = after(give_1, own, aside), after(give_2, own, aside)
+        grad_attend_in = after(grad_attend_in, own, aside)
         sum_1, give_1 = add_both(own_1, ring.over_core(give_1))
         sum_2, give_2 = add_both(own_2, ring.over_core(give_2))
         got_1, got_2 = ring.outer(give_1, False), ring.outer(give_2, True)
@@ -1157,18 +1166,17 @@
     if ring.direct:
         sum_1, give_1 = add_both(sum_1, got_1)
         sum_2, give_2 = add_both(sum_2, got_2)
-        sum_1 = add(sum_1, ring.inner(give_1, False))
-        sum_2 = add(sum_2, ring.inner(give_2, True))
-        cond_part = after(cond_part, sum_1, sum_2)
+        got_1, got_2 = ring.inner(give_1, False), ring.inner(give_2, True)
+        held = jnp.concatenate((add(sum_1, got_1), add(sum_2, got_2)), axis=1)
+        cond_part = after(cond_part, held)
+        got_line = ring.line(held)
     cond_part = lax.all_to_all(cond_part, ALL, 0, 0, tiled=True)
     cond_grad = jnp.sum(cond_part.reshape(n_exp, n_fsdp, blocks, mod_rows), axis=0)
     cond_grad = cond_grad.transpose(1, 0, 2).reshape(blocks, width) * silu_slope(cond_float)
 
     if ring.direct:
         cols, experts = width // PIECES, E // PIECES
-        summed = jnp.concatenate(
-            (add_line(sum_1[0], ring.line(sum_1)), add_line(sum_2[0], ring.line(sum_2))), axis=0
-        )
+        summed = add_line(held[0], got_line)
         output_grad, router_grad = summed[:, :cols], summed[:, cols : cols + experts]
         attend_grad = summed[:, OUT_LANES:]
         summed = lax.psum_scatter(
@@ -1176,13 +1184,11 @@
         ).astype(F32)
         shared_in_grad = summed[: 2 * half]
         shared_out_grad = turn_back(summed[2 * half :])
-        own_up, own_down = up_sum[:, :split], down_sum[:split]
-        expert_in_grad = jnp.stack(
-            (jnp.where(y == 0, own_up, got_up), jnp.where(y == 0, got_up, own_up))
-        )
-        expert_out_grad = jnp.stack(
-            (jnp.where(y == 0, own_down, got_down), jnp.where(y == 0, got_down, own_down))
-        )
+        own = own.astype(F32) + grad_blocks[3][0].astype(F32)
+        aside = aside.astype(F32) + neighbour.astype(F32)
+        first, second = jnp.where(y == 0, own, aside), jnp.where(y == 0, aside, own)
+        expert_in_grad = jnp.stack((up_of(first), up_of(second)))
+        expert_out_grad = jnp.stack((down_of(first), down_of(second)))
     else:
 
         def spread(grad):
@@ -1197,8 +1203,10 @@
         output_grad = spread(to_whole(dense_all[..., :cols]))
         router_grad = spread(to_whole(dense_all[..., cols : cols + experts]))
         shared_in_grad, shared_out_grad = map(spread, shared_unbundle(shared_grads))
-        up_sum = jnp.concatenate([b[:width] for b in grad_blocks], axis=1)
-        down_sum = jnp.concatenate([b[width:] for b in grad_blocks], axis=0)
+        up_sum = jnp.concatenate([up_of(half) for block in grad_blocks for half in block], axis=1)
+        down_sum = jnp.concatenate(
+            [down_of(half) for block in grad_blocks for half in block], axis=0
+        )
         expert_in_grad = lax.psum_scatter(up_sum, FSDP, scatter_dimension=1, tiled=True)
         expert_out_grad = lax.psum_scatter(down_sum, FSDP, scatter_dimension=0, tiled=True)
         expert_in_grad = expert_in_grad.astype(F32)[None]

time: 646 us -> 624 us (0.966)
  Pallas kernels: 274 us -> 228 us
  waiting for transfers between devices: 114 us -> 140 us
    pallas_call x2, Pallas kernels: 38.9 us -> 17.6 us  [attend_back(): pl.pallas_call(attend_back_kernel, out_shape=jax.ShapeDtypeStruct((3, tri...]
    ppermute x12 -> x9, waiting for transfers between devices: 30.4 us -> 51.5 us  [step(): return lax.ppermute(value, 'zi', [(i, (i + by) % n) for i in range(n)])]
    ppermute x0 -> x1, waiting for transfers between devices: none -> 20.1 us  [step_aside(): return lax.ppermute(value, FSDP, [(i, (i + 2) % n ^ 1) for i in range(n)])]
    ppermute x10 -> x9, waiting for transfers between devices: 34.1 us -> 15.9 us  [over_y(): return lax.ppermute(value, 'yi', [(0, 1), (1, 0)])]
    pallas_call x2, Pallas kernels: 27.4 us -> 11.3 us  [attend(): pl.pallas_call(attend_kernel, out_shape=(jax.ShapeDtypeStruct((triple.sha...]
    ppermute x6, waiting for transfers between devices: 16.1 us -> 26.4 us  [over_x(): return lax.ppermute(value, 'exp', [(i, i ^ 2) for i in range(4)])]
    all_to_all x1, waiting for transfers between devices: 25.9 us -> 16.5 us  [local(): mod_part = lax.all_to_all(mod_part, ALL, 0, 0, tiled=True)]
    pallas_call x4, Pallas kernels: 50 us -> 42.1 us  [expert_grads(): pl.pallas_call(expert_grads_kernel, out_shape=out, grid_spec=pltpu.Prefet...]
  transfers between devices with their start and end apart: 45 -> 42, of which waited for: 19 -> 18; matrix products, arithmetic and copies ran while one was open for 22% -> 21% of each run, Pallas kernels for 43% -> 37%
where the time goes in v4:
time: 624 us; the launch traced here: 617 us
  Pallas kernels  228 us (37%)
  waiting for transfers between devices  140 us (22%)
  starting transfers between devices  75.7 us (12%)
  other arithmetic  72.8 us (12%)
  matrix products  46.1 us (7%)
  local copies, waits for them, and re-layouts  39 us (6%)
  between operations  16 us (3%)
    pallas_call x2, Pallas kernels, expert_call(): pl.pallas_call(kernel, out_shape=(jax.ShapeDtypeStruct((rows, width), BF1...  68 us
    ppermute x9, waiting for transfers between devices, step(): return lax.ppermute(value, 'zi', [(i, (i + by) % n) for i in range(n)])  51.5 us
    dot_general x10, matrix products, dot(): lax.dot_general(left, right, (dims, ((), ())), preferred_element_type=F32)  46.1 us
    pallas_call x1, Pallas kernels, shared_expert(): pl.pallas_call(shared_kernel, out_shape=(jax.ShapeDtypeStruct((tok_count,...  43.2 us
    pallas_call x4, Pallas kernels, expert_grads(): pl.pallas_call(expert_grads_kernel, out_shape=out, grid_spec=pltpu.Prefet...  42.1 us
    ppermute x6, waiting for transfers between devices, over_x(): return lax.ppermute(value, 'exp', [(i, i ^ 2) for i in range(4)])  26.4 us
    ppermute x1, waiting for transfers between devices, step_aside(): return lax.ppermute(value, FSDP, [(i, (i + 2) % n ^ 1) for i in range(n)])  20.1 us
    unnamed x155, local copies, waits for them, and re-layouts  19.3 us
  transfers between devices with their start and end apart: 42, of which 18 were waited for; matrix products, arithmetic and copies ran while one was open for 21% of the time, Pallas kernels for 37%

profile of v4, /device:TPU:0, one launch (start us, length us, event | category | flops | bytes accessed | tf_op | source)
XLA Modules:
  0.0 617.5 jit_solution(8432941076875761376)
XLA Ops:
  41.2 16.5 %all-to-all-done.1 = bf16[32,4,1152]{2,1,0:T(4,128)(2,1)} async-done(((bf16[32,4,1152]{2,1,0:T(4,128)(2,1)}), bf16[32,4,1152]{2,1,0:T(4,128)(2,1)}, u32[]{:S(2)}, u32[]{:S(2)}) %all-to-all-start.1) | async-done | bytes 294944 | tf_op jit(solution)/shard_map/all_to_all | solution.py:922
  63.4 7.6 %collective-permute-done.5 = bf16[4,48,832]{2,1,0:T(8,128)(2,1)S(1)} collective-permute-done((bf16[4,48,832]{2,1,0:T(8,128)(2,1)S(1)}, bf16[4,48,832]{2,1,0:T(8,128)(2,1)S(1)}, u32[]{:S(2)}, u32[]{:S(2)}) %collective-permute-start.5) | collective-permute-done | bytes 319520 | tf_op jit(solution)/shard_map/ppermute | solution.py:818
  73.3 14.2 %collective-permute-done.6 = bf16[2,4,48,832]{3,2,1,0:T(8,128)(2,1)S(1)} collective-permute-done((bf16[2,4,48,832]{3,2,1,0:T(8,128)(2,1)S(1)}, bf16[2,4,48,832]{3,2,1,0:T(8,128)(2,1)S(1)}, u32[]{:S(2)}, u32[]{:S(2)}) %collective-permute-start.6) | collective-permute-done | bytes 639008 | tf_op jit(solution)/shard_map/ppermute | solution.py:821
  101.2 12.7 %triple.1 = (bf16[1024,768]{1,0:T(8,128)(2,1)S(1)}, bf16[1024,2304]{1,0:T(8,128)(2,1)}, bf16[768,2304]{1,0:T(8,128)(2,1)S(1)}) custom-call(s32[4]{0:T(128)S(1)} %pad_add_fusion.me, bf16[1024,768]{1,0:T(8,128)(2,1)S(1)} %copy-done.3, f32[4,1,768]{2,1,0:T(1,128)S(1)} %get-tuple-element.299.shift_ref, f32[4,1,768]{2,1,0:T(1,128)S(1)} %get-tuple-element.298.scale_ref, ...), custom_call_target="tpu_custom_call" | custom-call | flops 56623104 | bytes 98304 | tf_op jit(solution)/shard_map/triple/pallas_call | solution.py:312
  144.8 11.6 %project.1 = (f32[1024,768]{1,0:T(8,128)S(1)}, f32[1024,768]{1,0:T(8,128)S(1)}, bf16[1024,768]{1,0:T(8,128)(2,1)S(1)}, f32[1024,128]{1,0:T(8,128)S(1)}, bf16[768...) custom-call(s32[4]{0:T(128)S(1)} %pad_add_fusion.me, bf16[1024,384]{1,0:T(8,128)(2,1)S(1)} %get-tuple-element.82.left_ref.mixed_ref, ...), custom_call_target="tpu_custom_call" | custom-call | flops 18874368 | bytes 196608 | tf_op jit(solution)/shard_map/project/pallas_call | solution.py:397
  163.2 7.8 %convolution_convert_fusion = bf16[2304,768]{1,0:T(8,128)(2,1)} fusion(bf16[1024,768]{1,0:T(8,128)(2,1)} %copy-done.25, s32[1024]{0:T(1024)S(1)} %bitcast.330, s32[1024]{0:T(1024)S(1)} %bitcast.326), kind=kOutput, calls=%fused_computation.10 | convolution fusion | flops 3644522496 | bytes 5120000 | tf_op jit(solution)/shard_map/dot_general | solution.py:51
  202.7 43.2 %shared_expert.1 = (f32[1024,768]{1,0:T(8,128)}, f32[1024,768]{1,0:T(8,128)}, bf16[4,8,192,768]{3,2,1,0:T(8,128)(2,1)}) custom-call(s32[4]{0:T(128)} %copy-done.41, bf16[1024,768]{1,0:T(8,128)(2,1)} %copy-done.25, bf16[1024,768]{1,0:T(8,128)(2,1)} %get-tuple-element.247.grad_ref, bf16[2,2,4,96,768]{4,3,2,1,0:T(8,128)(2,1)} %pad_maximum_fusion.1.in_own, ...), custom_call_target="tpu_custom_call" | custom-call | flops 28991029248 | bytes 12582912 | tf_op jit(solution)/shard_map/shared_expert/pallas_call | solution.py:503
  251.1 36.6 %experts.1 = (bf16[2304,768]{1,0:T(8,128)(2,1)S(1)}, bf16[2304,3072]{1,0:T(8,128)(2,1)}, bf16[2304,3072]{1,0:T(8,128)(2,1)}) custom-call(bf16[2304,768]{1,0:T(8,128)(2,1)} %bitcast.49.x_ref, bf16[4,1536,768]{2,1,0:T(8,128)(2,1)} %bitcast.293), custom_call_target="tpu_custom_call" | custom-call | flops 679477248 | bytes 663552 | tf_op jit(solution)/shard_map/experts/pallas_call | solution.py:695
  298.6 31.4 %experts_back.1 = (bf16[2304,768]{1,0:T(8,128)(2,1)S(1)}, bf16[2304,3072]{1,0:T(8,128)(2,1)}) custom-call(bf16[2304,768]{1,0:T(8,128)(2,1)} %bitcast.51.grad_ref, bf16[2304,3072]{1,0:T(8,128)(2,1)} %get-tuple-element.107.slope_ref, bf16[4,1536,768]{2,1,0:T(8,128)(2,1)} %bitcast.294), custom_call_target="tpu_custom_call" | custom-call | flops 679477248 | bytes 442368 | tf_op jit(solution)/shard_map/experts_back/pallas_call | solution.py:695
  331.8 11.6 %expert_grads.4 = bf16[2,4,384,384]{3,2,1,0:T(8,128)(2,1)} custom-call(s32[1]{0:T(128)} %bitcast.57.part, bf16[2304,768]{1,0:T(8,128)(2,1)} %bitcast.49.x_ref, bf16[2304,3072]{1,0:T(8,128)(2,1)} %get-tuple-element.110.pre_ref, bf16[2304,3072]{1,0:T(8,128)(2,1)} %get-tuple-element.114.act_ref, bf16[2304,768]{1,0:T(8,128)(2,1)} %bitcast.51.grad_ref), custom_call_target="tpu_custom_call" | custom-call | flops 84934656 | bytes 221184 | tf_op jit(solution)/shard_map/expert_grads/pallas_call | solution.py:722
  351.2 6.5 %fusion = f32[1024,768]{1,0:T(8,128)S(1)} fusion(bf16[2304,768]{1,0:T(8,128)(2,1)} %bitcast.53, s32[1024]{0:T(1024)S(1)} %bitcast.332), kind=kOutput, calls=%fused_computation.1 | convolution fusion | flops 3626237952 | bytes 6688768 | tf_op jit(solution)/shard_map/dot_general | solution.py:51
  357.7 8.6 %multiply_reduce_fusion.6 = (f32[1024]{0:T(1024)S(1)}, f32[1024]{0:T(1024)S(1)}, f32[1024,768]{1,0:T(8,128)}) fusion(bf16[1024,768]{1,0:T(8,128)(2,1)S(1)} %copy-done.53, f32[1024,768]{1,0:T(8,128)S(1)} %fusion, f32[1024]{0:T(1024)S(1)} %bitcast.335, f32[1024]{0:T(1024)S(1)} %bitcast.334, bf16[2304,768]{1,0:T(8,128)(2,1)} %bitcast.53, s32[1024]{0:T(1024)S(1)} %bitcast.328), kind=kOutput, calls=%fused_computation.47 | convolution fusion | flops 3632527360 | bytes 11423744 | tf_op jit(solution)/shard_map/dot_general | solution.py:51
  366.3 10.1 %expert_grads.5 = bf16[2,4,384,384]{3,2,1,0:T(8,128)(2,1)S(1)} custom-call(s32[1]{0:T(128)} %bitcast.58.part, bf16[2304,768]{1,0:T(8,128)(2,1)} %bitcast.49.x_ref, bf16[2304,3072]{1,0:T(8,128)(2,1)} %get-tuple-element.110.pre_ref, bf16[2304,3072]{1,0:T(8,128)(2,1)} %get-tuple-element.114.act_ref, bf16[2304,768]{1,0:T(8,128)(2,1)} %bitcast.51.grad_ref), custom_call_target="tpu_custom_call" | custom-call | flops 84934656 | bytes 221184 | tf_op jit(solution)/shard_map/expert_grads/pallas_call | solution.py:722
  376.4 10.3 %expert_grads.6 = bf16[2,4,384,384]{3,2,1,0:T(8,128)(2,1)S(1)} custom-call(s32[1]{0:T(128)} %bitcast.59.part, bf16[2304,768]{1,0:T(8,128)(2,1)} %bitcast.49.x_ref, bf16[2304,3072]{1,0:T(8,128)(2,1)} %get-tuple-element.110.pre_ref, bf16[2304,3072]{1,0:T(8,128)(2,1)} %get-tuple-element.114.act_ref, bf16[2304,768]{1,0:T(8,128)(2,1)} %bitcast.51.grad_ref), custom_call_target="tpu_custom_call" | custom-call | flops 84934656 | bytes 221184 | tf_op jit(solution)/shard_map/expert_grads/pallas_call | solution.py:722
  388.1 10.2 %expert_grads.7 = bf16[2,4,384,384]{3,2,1,0:T(8,128)(2,1)S(1)} custom-call(s32[1]{0:T(128)} %bitcast.60.part, bf16[2304,768]{1,0:T(8,128)(2,1)} %bitcast.49.x_ref, bf16[2304,3072]{1,0:T(8,128)(2,1)} %get-tuple-element.110.pre_ref, bf16[2304,3072]{1,0:T(8,128)(2,1)} %get-tuple-element.114.act_ref, bf16[2304,768]{1,0:T(8,128)(2,1)} %bitcast.51.grad_ref), custom_call_target="tpu_custom_call" | custom-call | flops 84934656 | bytes 221184 | tf_op jit(solution)/shard_map/expert_grads/pallas_call | solution.py:722
  398.2 16.8 %collective-permute-done.17 = bf16[2,4,384,384]{3,2,1,0:T(8,128)(2,1)} collective-permute-done((bf16[2,4,384,384]{3,2,1,0:T(8,128)(2,1)}, bf16[2,4,384,384]{3,2,1,0:T(8,128)(2,1)}, u32[]{:S(2)}, u32[]{:S(2)}) %collective-permute-start.17) | collective-permute-done | bytes 2359328 | tf_op jit(solution)/shard_map/ppermute | solution.py:811
  423.0 6.8 %fusion.7 = f32[1024,768]{1,0:T(8,128)S(1)} fusion(bf16[2304,768]{1,0:T(8,128)(2,1)} %bitcast.56, s32[1024]{0:T(1024)S(1)} %bitcast.333, s32[1024]{0:T(1024)S(1)} %bitcast.329), kind=kOutput, calls=%fused_computation.14 | convolution fusion | flops 3642753024 | bytes 6692864 | tf_op jit(solution)/shard_map/dot_general | solution.py:51
  450.6 8.7 %attend_back.2.left_ref = bf16[3,1024,384]{2,1,0:T(8,128)(2,1)S(1)} custom-call(s32[1]{0:T(128)S(6)} %copy.141.kind_ref, bf16[1024,2304]{1,0:T(8,128)(2,1)S(1)} %bitcast.289, bf16[1024,2304]{1,0:T(8,128)(2,1)S(1)} %bitcast.289, bf16[1024,2304]{1,0:T(8,128)(2,1)S(1)} %bitcast.289, bf16[1024,384]{1,0:T(8,128)(2,1)S(1)} %copy-done.18, ...), custom_call_target="tpu_custom_call" | custom-call | flops 251658240 | bytes 147456 | tf_op jit(solution)/shard_map/attend_back/pallas_call | solution.py:229
  459.4 21.9 %collective-permute-done.19 = bf16[2,4,384,384]{3,2,1,0:T(8,128)(2,1)} collective-permute-done((bf16[2,4,384,384]{3,2,1,0:T(8,128)(2,1)}, bf16[2,4,384,384]{3,2,1,0:T(8,128)(2,1)}, u32[]{:S(2)}, u32[]{:S(2)}) %collective-permute-start.19) | collective-permute-done | bytes 2359328 | tf_op jit(solution)/shard_map/ppermute | solution.py:811
  491.4 8.9 %attend_back.3.right_ref = bf16[3,1024,384]{2,1,0:T(8,128)(2,1)S(1)} custom-call(s32[1]{0:T(128)S(6)} %copy.141.kind_ref, bf16[1024,2304]{1,0:T(8,128)(2,1)S(1)} %copy-done.2, bf16[1024,2304]{1,0:T(8,128)(2,1)S(1)} %copy-done.2, bf16[1024,2304]{1,0:T(8,128)(2,1)S(1)} %copy-done.2, bf16[1024,384]{1,0:T(8,128)(2,1)S(1)} %copy-done.16, ...), custom_call_target="tpu_custom_call" | custom-call | flops 251658240 | bytes 147456 | tf_op jit(solution)/shard_map/attend_back/pallas_call | solution.py:229
  500.3 18.6 %triple_back.1 = (f32[1024,768]{1,0:T(8,128)}, bf16[2,2,4,48,832]{4,3,2,1,0:T(8,128)(2,1)S(1)}, bf16[2,2,4,48,832]{4,3,2,1,0:T(8,128)(2,1)S(1)}, bf16[2,2,4,48,8...) custom-call(s32[4]{0:T(128)S(1)} %copy-done.42, bf16[3,1024,384]{2,1,0:T(8,128)(2,1)S(1)} %copy-done.13, ...), custom_call_target="tpu_custom_call" | custom-call | flops 113246208 | bytes 147456 | tf_op jit(solution)/shard_map/triple_back/pallas_call | solution.py:632
  519.0 20.1 %collective-permute-done.21 = bf16[4,384,384]{2,1,0:T(8,128)(2,1)} collective-permute-done((bf16[4,384,384]{2,1,0:T(8,128)(2,1)}, bf16[4,384,384]{2,1,0:T(8,128)(2,1)}, u32[]{:S(2)}, u32[]{:S(2)}) %collective-permute-start.21) | collective-permute-done | bytes 1179680 | tf_op jit(solution)/shard_map/ppermute | solution.py:815
  570.0 7.6 %collective-permute-done.23 = bf16[2,4,48,832]{3,2,1,0:T(8,128)(2,1)} collective-permute-done((bf16[2,4,48,832]{3,2,1,0:T(8,128)(2,1)}, bf16[2,4,48,832]{3,2,1,0:T(8,128)(2,1)}, u32[]{:S(2)}, u32[]{:S(2)}) %collective-permute-start.23) | collective-permute-done | bytes 639008 | tf_op jit(solution)/shard_map/ppermute | solution.py:821
  599.6 9.0 %collective-permute-done.29 = bf16[96,832]{1,0:T(8,128)(2,1)S(1)} collective-permute-done((bf16[96,832]{1,0:T(8,128)(2,1)S(1)}, bf16[96,832]{1,0:T(8,128)(2,1)S(1)}, u32[]{:S(2)}, u32[]{:S(2)}) %collective-permute-start.29) | collective-permute-done | bytes 159776 | tf_op jit(solution)/shard_map/ppermute | solution.py:811
  (361 shorter events, 244.1 us)
Async XLA Ops:
  7.2 54.3 %all-gather.5.cloned.1.call-start = ((), (), s32[]{:S(2)}) async-start(), calls=%async_computation.10 | async-start | bytes 1474560 | tf_op jit(solution)/shard_map/all_gather | solution.py:944
  9.2 16.9 %collective-permute-start.1 = (bf16[96,832]{1,0:T(8,128)(2,1)S(1)}, bf16[96,832]{1,0:T(8,128)(2,1)S(1)}, u32[]{:S(2)}, u32[]{:S(2)}) collective-permute-start(bf16[96,832]{1,0:T(8,128)(2,1)S(1)} %pad_maximum_fusion.13), channel_id=1, source_target_pairs={{0,4},{2,6},{4,0},{6,2},{1,5},{3,7},{5,1},{7,3},{8,12},{10,14},{12... | collective-permute-start | bytes 479240 | tf_op jit(solution)/shard_map/ppermute | solution.py:811
  35.3 22.3 %all-to-all-start.1 = ((bf16[32,4,1152]{2,1,0:T(4,128)(2,1)}), bf16[32,4,1152]{2,1,0:T(4,128)(2,1)}, u32[]{:S(2)}, u32[]{:S(2)}) async-start(bf16[32,4,1152]{2,1,0:T(4,128)(2,1)} %reshape.440), calls=%async_computation.1 | async-start | bytes 589824 | tf_op jit(solution)/shard_map/all_to_all | solution.py:922
  38.6 212.5 %all-gather.7.cloned.1.call-start = ((), (), s32[]{:S(2)}) async-start(), calls=%async_computation.11 | async-start | bytes 11796480 | tf_op jit(solution)/shard_map/all_gather | solution.py:945
  39.6 19.3 %collective-permute-start.4 = (bf16[384,768]{1,0:T(8,128)(2,1)}, bf16[384,768]{1,0:T(8,128)(2,1)S(1)}, u32[]{:S(2)}, u32[]{:S(2)}) collective-permute-start(bf16[384,768]{1,0:T(8,128)(2,1)} %get-tuple-element.273), channel_id=1, source_target_pairs={{0,1},{1,0},{2,3},{3,2},{4,5},{5,4},{6,7},{7,6},{8,9},{9,8},{10,11... | collective-permute-start | bytes 1769480 | tf_op jit(solution)/shard_map/ppermute | solution.py:818
  71.1 16.5 %collective-permute-start.6 = (bf16[2,4,48,832]{3,2,1,0:T(8,128)(2,1)S(1)}, bf16[2,4,48,832]{3,2,1,0:T(8,128)(2,1)S(1)}, u32[]{:S(2)}, u32[]{:S(2)}) collective-permute-start(bf16[2,4,48,832]{3,2,1,0:T(8,128)(2,1)S(1)} %get-tuple-element.284), channel_id=1, source_target_pairs={{0,16},{8,24},{16,0},{24,8},{1,17},{9,25},{17,1},{25,9},{2,18},{10... | collective-permute-start | bytes 1916936 | tf_op jit(solution)/shard_map/ppermute | solution.py:821
  132.2 44.2 %collective-permute-start.13 = (bf16[2,4,96,768]{3,2,1,0:T(8,128)(2,1)}, bf16[2,4,96,768]{3,2,1,0:T(8,128)(2,1)}, u32[]{:S(2)}, u32[]{:S(2)}) collective-permute-start(bf16[2,4,96,768]{3,2,1,0:T(8,128)(2,1)} %pad_maximum_fusion.7), channel_id=1, source_target_pairs={{0,16},{8,24},{16,0},{24,8},{1,17},{9,25},{17,1},{25,9},{2,18},{10... | collective-permute-start | bytes 3538952 | tf_op jit(solution)/shard_map/ppermute | solution.py:821
  137.7 35.4 %collective-permute-start.14 = (bf16[2,4,96,768]{3,2,1,0:T(8,128)(2,1)}, bf16[2,4,96,768]{3,2,1,0:T(8,128)(2,1)}, u32[]{:S(2)}, u32[]{:S(2)}) collective-permute-start(bf16[2,4,96,768]{3,2,1,0:T(8,128)(2,1)} %pad_maximum_fusion.8), channel_id=1, source_target_pairs={{0,1},{1,0},{2,3},{3,2},{4,5},{5,4},{6,7},{7,6},{8,9},{9,8},{10,11... | collective-permute-start | bytes 3538952 | tf_op jit(solution)/shard_map/ppermute | solution.py:818
  179.6 23.1 %collective-permute-start.15 = (bf16[2,2,4,96,768]{4,3,2,1,0:T(8,128)(2,1)}, bf16[2,2,4,96,768]{4,3,2,1,0:T(8,128)(2,1)}, u32[]{:S(2)}, u32[]{:S(2)}) collective-permute-start(bf16[2,2,4,96,768]{4,3,2,1,0:T(8,128)(2,1)} %pad_maximum_fusion.1.in_own), channel_id=1, source_target_pairs={{0,8},{8,0},{16,24},{24,16},{1,9},{9,1},{17,25},{25,17},{2,10},{10... | collective-permute-start | bytes 7077896 | tf_op jit(solution)/shard_map/ppermute | solution.py:824
  185.8 16.9 %collective-permute-start.16 = (bf16[2,2,4,96,768]{4,3,2,1,0:T(8,128)(2,1)}, bf16[2,2,4,96,768]{4,3,2,1,0:T(8,128)(2,1)}, u32[]{:S(2)}, u32[]{:S(2)}) collective-permute-start(bf16[2,2,4,96,768]{4,3,2,1,0:T(8,128)(2,1)} %pad_maximum_fusion.2.out_own), channel_id=1, source_target_pairs={{0,8},{8,0},{16,24},{24,16},{1,9},{9,1},{17,25},{25,17},{2,10},{10... | collective-permute-start | bytes 7077896 | tf_op jit(solution)/shard_map/ppermute | solution.py:824
  185.8 60.0 %all-to-all-start.2 = ((bf16[8,288,768]{2,1,0:T(8,128)(2,1)}), bf16[8,288,768]{2,1,0:T(8,128)(2,1)}, u32[]{:S(2)}, u32[]{:S(2)}) async-start(bf16[8,288,768]{2,1,0:T(8,128)(2,1)} %bitcast.296), calls=%async_computation.2 | async-start | bytes 7077888 | tf_op jit(solution)/shard_map/all_to_all | solution.py:1030
  245.9 45.9 %all-to-all-start.3 = ((bf16[8,288,768]{2,1,0:T(8,128)(2,1)}), bf16[8,288,768]{2,1,0:T(8,128)(2,1)}, u32[]{:S(2)}, u32[]{:S(2)}) async-start(bf16[8,288,768]{2,1,0:T(8,128)(2,1)} %bitcast.297), calls=%async_computation.3 | async-start | bytes 7077888 | tf_op jit(solution)/shard_map/all_to_all | solution.py:1030
  250.4 236.0 %reduce-scatter.2.cloned.1.call-start = ((), (), s32[]{:S(2)}) async-start(), calls=%async_computation.9 | async-start | bytes 9732096 | tf_op jit(solution)/shard_map/reduce_scatter | solution.py:1182
  291.8 54.4 %all-to-all-start.4 = ((bf16[8,288,768]{2,1,0:T(8,128)(2,1)}), bf16[8,288,768]{2,1,0:T(8,128)(2,1)}, u32[]{:S(2)}, u32[]{:S(2)}) async-start(bf16[8,288,768]{2,1,0:T(8,128)(2,1)} %bitcast.290), calls=%async_computation.4 | async-start | bytes 7077888 | tf_op jit(solution)/shard_map/all_to_all | solution.py:1030
  343.4 71.6 %collective-permute-start.17 = (bf16[2,4,384,384]{3,2,1,0:T(8,128)(2,1)}, bf16[2,4,384,384]{3,2,1,0:T(8,128)(2,1)}, u32[]{:S(2)}, u32[]{:S(2)}) collective-permute-start(bf16[2,4,384,384]{3,2,1,0:T(8,128)(2,1)} %expert_grads.4), channel_id=1, source_target_pairs={{0,2},{2,4},{4,6},{6,0},{1,3},{3,5},{5,7},{7,1},{8,10},{10,12},{12... | collective-permute-start | bytes 7077896 | tf_op jit(solution)/shard_map/ppermute | solution.py:811
  346.2 74.0 %all-to-all-start.5 = ((bf16[8,288,768]{2,1,0:T(8,128)(2,1)}), bf16[8,288,768]{2,1,0:T(8,128)(2,1)}, u32[]{:S(2)}, u32[]{:S(2)}) async-start(bf16[8,288,768]{2,1,0:T(8,128)(2,1)} %bitcast.291), calls=%async_computation.5 | async-start | bytes 7077888 | tf_op jit(solution)/shard_map/all_to_all | solution.py:1030
  420.2 61.1 %collective-permute-start.19 = (bf16[2,4,384,384]{3,2,1,0:T(8,128)(2,1)}, bf16[2,4,384,384]{3,2,1,0:T(8,128)(2,1)}, u32[]{:S(2)}, u32[]{:S(2)}) collective-permute-start(bf16[2,4,384,384]{3,2,1,0:T(8,128)(2,1)} %add_convert_fusion.2), channel_id=1, source_target_pairs={{0,2},{2,4},{4,6},{6,0},{1,3},{3,5},{5,7},{7,1},{8,10},{10,12},{12... | collective-permute-start | bytes 7077896 | tf_op jit(solution)/shard_map/ppermute | solution.py:811
  422.7 27.8 %collective-permute-start.18 = (bf16[4,384,384]{2,1,0:T(8,128)(2,1)}, bf16[4,384,384]{2,1,0:T(8,128)(2,1)}, u32[]{:S(2)}, u32[]{:S(2)}) collective-permute-start(bf16[4,384,384]{2,1,0:T(8,128)(2,1)} %slice_bitcast_fusion.3), channel_id=1, source_target_pairs={{0,1},{1,0},{2,3},{3,2},{4,5},{5,4},{6,7},{7,6},{8,9},{9,8},{10,11... | collective-permute-start | bytes 3538952 | tf_op jit(solution)/shard_map/ppermute | solution.py:818
  485.4 33.6 %collective-permute-start.20 = (bf16[4,384,384]{2,1,0:T(8,128)(2,1)}, bf16[4,384,384]{2,1,0:T(8,128)(2,1)}, u32[]{:S(2)}, u32[]{:S(2)}) collective-permute-start(bf16[4,384,384]{2,1,0:T(8,128)(2,1)} %get-tuple-element.131), channel_id=1, source_target_pairs={{0,2},{2,4},{4,6},{6,0},{1,3},{3,5},{5,7},{7,1},{8,10},{10,12},{12... | collective-permute-start | bytes 3538952 | tf_op jit(solution)/shard_map/ppermute | solution.py:811
  485.4 53.7 %collective-permute-start.21 = (bf16[4,384,384]{2,1,0:T(8,128)(2,1)}, bf16[4,384,384]{2,1,0:T(8,128)(2,1)}, u32[]{:S(2)}, u32[]{:S(2)}) collective-permute-start(bf16[4,384,384]{2,1,0:T(8,128)(2,1)} %get-tuple-element.132), channel_id=1, source_target_pairs={{0,3},{1,2},{2,5},{3,4},{4,7},{5,6},{6,1},{7,0},{8,11},{9,10},{10,... | collective-permute-start | bytes 3538952 | tf_op jit(solution)/shard_map/ppermute | solution.py:815
  544.1 21.1 %all-to-all-start.6 = ((bf16[32,4,1152]{2,1,0:T(4,128)(2,1)}), bf16[32,4,1152]{2,1,0:T(4,128)(2,1)S(1)}, u32[]{:S(2)}, u32[]{:S(2)}) async-start(bf16[32,4,1152]{2,1,0:T(4,128)(2,1)} %bitcast.299), calls=%async_computation.6 | async-start | bytes 589824 | tf_op jit(solution)/shard_map/all_to_all | solution.py:1161
  559.2 18.5 %collective-permute-start.23 = (bf16[2,4,48,832]{3,2,1,0:T(8,128)(2,1)}, bf16[2,4,48,832]{3,2,1,0:T(8,128)(2,1)}, u32[]{:S(2)}, u32[]{:S(2)}) collective-permute-start(bf16[2,4,48,832]{3,2,1,0:T(8,128)(2,1)} %get-tuple-element.255), channel_id=1, source_target_pairs={{0,16},{8,24},{16,0},{24,8},{1,17},{9,25},{17,1},{25,9},{2,18},{10... | collective-permute-start | bytes 1916936 | tf_op jit(solution)/shard_map/ppermute | solution.py:821
  562.2 19.0 %collective-permute-start.26 = (bf16[2,4,48,832]{3,2,1,0:T(8,128)(2,1)}, bf16[2,4,48,832]{3,2,1,0:T(8,128)(2,1)S(1)}, u32[]{:S(2)}, u32[]{:S(2)}) collective-permute-start(bf16[2,4,48,832]{3,2,1,0:T(8,128)(2,1)} %get-tuple-element.253), channel_id=1, source_target_pairs={{0,1},{1,0},{2,3},{3,2},{4,5},{5,4},{6,7},{7,6},{8,9},{9,8},{10,11... | collective-permute-start | bytes 1916936 | tf_op jit(solution)/shard_map/ppermute | solution.py:818
  566.1 18.4 %all-to-all-start.7 = ((f32[32,4,96]{2,1,0:T(4,128)}), f32[32,4,96]{2,1,0:T(4,128)}, u32[]{:S(2)}, u32[]{:S(2)}) async-start(f32[32,4,96]{2,1,0:T(4,128)} %copy.119), calls=%async_computation.7 | async-start | bytes 131072 | tf_op jit(solution)/shard_map/all_to_all | solution.py:1173
  (90 other events, 946.2 us)
Sparse Core Ops, SparseCore 0:
  22.7 34.3 all-gather.4
  61.7 165.9 all-gather.6
  257.1 179.7 reduce-scatter.1

commit v5 on v4

--- a/solution.py
+++ b/solution.py
@@ -526,13 +526,21 @@
     weight_ref,
     back_ref,
     out_grad_ref,
-    router_ref,
 ):
-    split = left_ref.shape[1]
     back_ref[...] = mm_rt(grad_ref[...], weight_ref[...]).astype(BF16)
-    out_grad_ref[:split, :] = mm_lt(left_ref[...], grad_ref[...]).astype(BF16)
-    out_grad_ref[split:, :] = mm_lt(right_ref[...], grad_ref[...]).astype(BF16)
-    router_ref[...] = mm_lt(branch_ref[...], logits_ref[...]).astype(BF16)
+    width = weight_ref.shape[0]
+    outs, experts = width // PIECES, E // PIECES
+    router = mm_lt(branch_ref[...], logits_ref[...]).astype(BF16)
+    out_grad = jnp.concatenate(
+        (mm_lt(left_ref[...], grad_ref[...]), mm_lt(right_ref[...], grad_ref[...])), axis=0
+    ).astype(BF16)
+    out_grad_ref[...] = jnp.zeros_like(out_grad_ref)
+    for piece in range(PIECES):
+        low = piece * OUT_LANES
+        out_grad_ref[:, low : low + outs] = out_grad[:, piece * outs : (piece + 1) * outs]
+        out_grad_ref[:, low + outs : low + outs + experts] = router[
+            :, piece * experts : (piece + 1) * experts
+        ]
 
 
 def project_back(left, right, grad, branch, grad_logits, weight):
@@ -543,12 +551,11 @@
         project_back_kernel,
         out_shape=(
             jax.ShapeDtypeStruct((tok_count, width), BF16),
-            jax.ShapeDtypeStruct((width, width), BF16),
-            jax.ShapeDtypeStruct((width, LANES), BF16),
+            jax.ShapeDtypeStruct((width, PIECES * OUT_LANES), BF16),
         ),
         grid=(1,),
         in_specs=[part, part, whole, whole, fixed((tok_count, LANES)), fixed((width, width))],
-        out_specs=(whole, fixed((width, width)), fixed((width, LANES))),
+        out_specs=(whole, fixed((width, PIECES * OUT_LANES))),
         compiler_params=pltpu.CompilerParams(vmem_limit_bytes=32 << 20),
         cost_estimate=cost(4 * tok_count * width * width, 8 * tok_count * width),
         name="project_back",
@@ -562,7 +569,6 @@
     in_ref,
     weight_ref,
     out_grad_ref,
-    router_ref,
     back_ref,
     q1a,
     q1b,
@@ -574,7 +580,6 @@
     step = pl.program_id(0)
     rows, cols = q1a.shape[3], q1a.shape[4] - OUT_LANES
     width = in_ref.shape[1]
-    outs, experts = width // PIECES, E // PIECES
 
     @pl.when(step == 0)
     def _():
@@ -601,15 +606,9 @@
 
                 def place(ref, where, low):
                     at = slice(low, low + rows)
-                    ref[where + (slice(None), slice(0, outs))] = out_grad_ref[
-                        at, piece * outs : (piece + 1) * outs
+                    ref[where + (slice(None), slice(0, OUT_LANES))] = out_grad_ref[
+                        at, piece * OUT_LANES : (piece + 1) * OUT_LANES
                     ]
-                    ref[where + (slice(None), slice(outs, outs + experts))] = router_ref[
-                        at, piece * experts : (piece + 1) * experts
-                    ]
-                    ref[where + (slice(None), slice(outs + experts, OUT_LANES))] = jnp.zeros(
-                        (rows, OUT_LANES - outs - experts), BF16
-                    )
                     ref[where + (slice(None), slice(OUT_LANES, None))] = weight_grad[
                         at, piece * cols : (piece + 1) * cols
                     ]
@@ -624,7 +623,7 @@
                 on_side(other, q2a, q2b, second)
 
 
-def triple_back(me, left, right, attend_in, weight, out_grad, router_grad):
+def triple_back(me, left, right, attend_in, weight, out_grad):
     tok_count, width = attend_in.shape
     hidden = weight.shape[1]
     block = (2, 2, 4, width // STRIPS // 2, OUT_LANES + hidden // PIECES)
@@ -640,8 +639,7 @@
                 pl.BlockSpec((1, tok_count, width // 2), lambda p, me: (p, 0, 0)),
                 fixed((tok_count, width)),
                 pl.BlockSpec((width, width), lambda p, me: (0, p)),
-                fixed((width, width)),
-                fixed((width, LANES)),
+                fixed(out_grad.shape),
             ],
             out_specs=(fixed((tok_count, width)),) + (fixed(block.shape),) * 4,
             scratch_shapes=[
@@ -652,7 +650,7 @@
         compiler_params=pltpu.CompilerParams(vmem_limit_bytes=40 << 20),
         cost_estimate=cost(4 * tok_count * width * hidden, 12 * tok_count * width),
         name="triple_back",
-    )(me, left, right, attend_in, weight, out_grad, router_grad)
+    )(me, left, right, attend_in, weight, out_grad)
 
 
 ROW_TILE = 576
@@ -1102,7 +1100,7 @@
     )
     grad_gate_first = jnp.sum(grad_residual * projected, axis=1)
     grad_projected = (gate_first * grad_residual).astype(BF16).reshape(tok_count, width)
-    grad_attended, out_grad_all, router_grad_all = project_back(
+    grad_attended, out_grad_all = project_back(
         attended_1, attended_2, grad_projected, branch_in, grad_logits, output_weight_all
     )
     if ring.direct:
@@ -1122,14 +1120,14 @@
         attend_in,
         triple_weight,
         out_grad_all,
-        router_grad_all,
     )
     if ring.direct:
         own_1, give_1, own_2, give_2 = dense_grads
         give_1, give_2 = after(give_1, own, aside), after(give_2, own, aside)
-        grad_attend_in = after(grad_attend_in, own, aside)
-        sum_1, give_1 = add_both(own_1, ring.over_core(give_1))
-        sum_2, give_2 = add_both(own_2, ring.over_core(give_2))
+        got_1, got_2 = ring.over_core(give_1), ring.over_core(give_2)
+        grad_attend_in = after(grad_attend_in, got_1, got_2)
+        sum_1, give_1 = add_both(own_1, got_1)
+        sum_2, give_2 = add_both(own_2, got_2)
         got_1, got_2 = ring.outer(give_1, False), ring.outer(give_2, True)
     inputs = patches.astype(F32).reshape(blocks, SHORT, width)
     normed_first, inverse_first = layer_norm(inputs)

time: 624 us -> 620 us (level)
  Pallas kernels: 228 us -> 264 us
  waiting for transfers between devices: 140 us -> 115 us
  starting transfers between devices: 75.7 us -> 63.4 us
    pallas_call x2, Pallas kernels: 17.6 us -> 39.4 us  [attend_back(): pl.pallas_call(attend_back_kernel, out_shape=jax.ShapeDtypeStruct((3, tri...]
    ppermute x9, waiting for transfers between devices: 51.5 us -> 34.9 us  [step(): return lax.ppermute(value, 'zi', [(i, (i + by) % n) for i in range(n)])]
    pallas_call x2, Pallas kernels: 11.3 us -> 27.4 us  [attend(): pl.pallas_call(attend_kernel, out_shape=(jax.ShapeDtypeStruct((triple.sha...]
    ppermute x6, waiting for transfers between devices: 26.4 us -> 16 us  [over_x(): return lax.ppermute(value, 'exp', [(i, i ^ 2) for i in range(4)])]
    ppermute x1, waiting for transfers between devices: 20.1 us -> 11.7 us  [step_aside(): return lax.ppermute(value, FSDP, [(i, (i + 2) % n ^ 1) for i in range(n)])]
    all_to_all x1, waiting for transfers between devices: 0.01 us -> 6.58 us  [local(): lax.all_to_all(mod_send.reshape(n_all, blocks, mod_cols), ALL, 0, 0, tile...]
    unnamed x155 -> x157, local copies, waits for them, and re-layouts: 19.3 us -> 21.4 us
  transfers between devices with their start and end apart: 42 -> 42, of which waited for: 18 -> 18; matrix products, arithmetic and copies ran while one was open for 21% -> 22% of each run, Pallas kernels for 37% -> 43%
where the time goes in v5:
time: 620 us; the launch traced here: 616 us
  Pallas kernels  264 us (43%)
  waiting for transfers between devices  115 us (19%)
  other arithmetic  70.3 us (11%)
  starting transfers between devices  63.4 us (10%)
  matrix products  46.4 us (7%)
  local copies, waits for them, and re-layouts  41.2 us (7%)
  between operations  15.9 us (3%)
    pallas_call x2, Pallas kernels, expert_call(): pl.pallas_call(kernel, out_shape=(jax.ShapeDtypeStruct((rows, width), BF1...  68.1 us
    dot_general x10, matrix products, dot(): lax.dot_general(left, right, (dims, ((), ())), preferred_element_type=F32)  46.4 us
    pallas_call x1, Pallas kernels, shared_expert(): pl.pallas_call(shared_kernel, out_shape=(jax.ShapeDtypeStruct((tok_count,...  43 us
    pallas_call x4, Pallas kernels, expert_grads(): pl.pallas_call(expert_grads_kernel, out_shape=out, grid_spec=pltpu.Prefet...  42.1 us
    pallas_call x2, Pallas kernels, attend_back(): pl.pallas_call(attend_back_kernel, out_shape=jax.ShapeDtypeStruct((3, tri...  39.4 us
    ppermute x9, waiting for transfers between devices, step(): return lax.ppermute(value, 'zi', [(i, (i + by) % n) for i in range(n)])  34.9 us
    pallas_call x2, Pallas kernels, attend(): pl.pallas_call(attend_kernel, out_shape=(jax.ShapeDtypeStruct((triple.sha...  27.4 us
    unnamed x157, local copies, waits for them, and re-layouts  21.4 us
  transfers between devices with their start and end apart: 42, of which 18 were waited for; matrix products, arithmetic and copies ran while one was open for 22% of the time, Pallas kernels for 43%

profile of v5, /device:TPU:0, one launch (start us, length us, event | category | flops | bytes accessed | tf_op | source)
XLA Modules:
  0.0 616.3 jit_solution(15393640661366467249)
XLA Ops:
  41.2 16.5 %all-to-all-done.1 = bf16[32,4,1152]{2,1,0:T(4,128)(2,1)} async-done(((bf16[32,4,1152]{2,1,0:T(4,128)(2,1)}), bf16[32,4,1152]{2,1,0:T(4,128)(2,1)}, u32[]{:S(2)}, u32[]{:S(2)}) %all-to-all-start.1) | async-done | bytes 294944 | tf_op jit(solution)/shard_map/all_to_all | solution.py:920
  63.4 7.6 %collective-permute-done.5 = bf16[4,48,832]{2,1,0:T(8,128)(2,1)S(1)} collective-permute-done((bf16[4,48,832]{2,1,0:T(8,128)(2,1)S(1)}, bf16[4,48,832]{2,1,0:T(8,128)(2,1)S(1)}, u32[]{:S(2)}, u32[]{:S(2)}) %collective-permute-start.5) | collective-permute-done | bytes 319520 | tf_op jit(solution)/shard_map/ppermute | solution.py:816
  73.3 14.2 %collective-permute-done.6 = bf16[2,4,48,832]{3,2,1,0:T(8,128)(2,1)S(1)} collective-permute-done((bf16[2,4,48,832]{3,2,1,0:T(8,128)(2,1)S(1)}, bf16[2,4,48,832]{3,2,1,0:T(8,128)(2,1)S(1)}, u32[]{:S(2)}, u32[]{:S(2)}) %collective-permute-start.6) | collective-permute-done | bytes 639008 | tf_op jit(solution)/shard_map/ppermute | solution.py:819
  101.1 12.7 %triple.1 = (bf16[1024,768]{1,0:T(8,128)(2,1)S(1)}, bf16[1024,2304]{1,0:T(8,128)(2,1)}, bf16[768,2304]{1,0:T(8,128)(2,1)S(1)}) custom-call(s32[4]{0:T(128)S(1)} %pad_add_fusion.me, bf16[1024,768]{1,0:T(8,128)(2,1)S(1)} %copy-done.3, f32[4,1,768]{2,1,0:T(1,128)S(1)} %get-tuple-element.297.shift_ref, f32[4,1,768]{2,1,0:T(1,128)S(1)} %get-tuple-element.296.scale_ref, ...), custom_call_target="tpu_custom_call" | custom-call | flops 56623104 | bytes 98304 | tf_op jit(solution)/shard_map/triple/pallas_call | solution.py:312
  120.7 13.6 %attend.2 = (bf16[1024,384]{1,0:T(8,128)(2,1)S(1)}, f32[1,3,8,1024]{3,2,1,0:T(8,128)S(1)}) custom-call(s32[1]{0:T(128)S(6)} %copy.141.kind_ref, bf16[1024,2304]{1,0:T(8,128)(2,1)S(1)} %copy-done.1, bf16[1024,2304]{1,0:T(8,128)(2,1)S(1)} %copy-done.1, bf16[1024,2304]{1,0:T(8,128)(2,1)S(1)} %copy-done.1), custom_call_target="tpu_custom_call" | custom-call | flops 100663296 | bytes 73728 | tf_op jit(solution)/shard_map/attend/pallas_call | solution.py:128
  138.9 13.8 %attend.3 = (bf16[1024,384]{1,0:T(8,128)(2,1)S(1)}, f32[1,3,8,1024]{3,2,1,0:T(8,128)S(1)}) custom-call(s32[1]{0:T(128)S(6)} %copy.141.kind_ref, bf16[1024,2304]{1,0:T(8,128)(2,1)S(1)} %copy-done.1, bf16[1024,2304]{1,0:T(8,128)(2,1)S(1)} %copy-done.1, bf16[1024,2304]{1,0:T(8,128)(2,1)S(1)} %copy-done.1), custom_call_target="tpu_custom_call" | custom-call | flops 100663296 | bytes 73728 | tf_op jit(solution)/shard_map/attend/pallas_call | solution.py:128
  152.7 11.6 %project.1 = (f32[1024,768]{1,0:T(8,128)S(1)}, f32[1024,768]{1,0:T(8,128)S(1)}, bf16[1024,768]{1,0:T(8,128)(2,1)S(1)}, f32[1024,128]{1,0:T(8,128)S(1)}, bf16[768...) custom-call(s32[4]{0:T(128)S(1)} %pad_add_fusion.me, bf16[1024,384]{1,0:T(8,128)(2,1)S(1)} %get-tuple-element.81.left_ref.mixed_ref, ...), custom_call_target="tpu_custom_call" | custom-call | flops 18874368 | bytes 196608 | tf_op jit(solution)/shard_map/project/pallas_call | solution.py:397
  171.2 7.8 %convolution_convert_fusion = bf16[2304,768]{1,0:T(8,128)(2,1)} fusion(bf16[1024,768]{1,0:T(8,128)(2,1)} %copy-done.25, s32[1024]{0:T(1024)S(1)} %bitcast.331, s32[1024]{0:T(1024)S(1)} %bitcast.327), kind=kOutput, calls=%fused_computation.10 | convolution fusion | flops 3644522496 | bytes 5120000 | tf_op jit(solution)/shard_map/dot_general | solution.py:51
  204.9 43.0 %shared_expert.1 = (f32[1024,768]{1,0:T(8,128)}, f32[1024,768]{1,0:T(8,128)}, bf16[4,8,192,768]{3,2,1,0:T(8,128)(2,1)}) custom-call(s32[4]{0:T(128)} %copy-done.39, bf16[1024,768]{1,0:T(8,128)(2,1)} %copy-done.25, bf16[1024,768]{1,0:T(8,128)(2,1)} %get-tuple-element.245.grad_ref, bf16[2,2,4,96,768]{4,3,2,1,0:T(8,128)(2,1)} %pad_maximum_fusion.1.in_own, ...), custom_call_target="tpu_custom_call" | custom-call | flops 28991029248 | bytes 12582912 | tf_op jit(solution)/shard_map/shared_expert/pallas_call | solution.py:503
  253.2 36.6 %experts.1 = (bf16[2304,768]{1,0:T(8,128)(2,1)S(1)}, bf16[2304,3072]{1,0:T(8,128)(2,1)}, bf16[2304,3072]{1,0:T(8,128)(2,1)}) custom-call(bf16[2304,768]{1,0:T(8,128)(2,1)} %bitcast.49.x_ref, bf16[4,1536,768]{2,1,0:T(8,128)(2,1)} %bitcast.293), custom_call_target="tpu_custom_call" | custom-call | flops 679477248 | bytes 663552 | tf_op jit(solution)/shard_map/experts/pallas_call | solution.py:693
  300.5 31.5 %experts_back.1 = (bf16[2304,768]{1,0:T(8,128)(2,1)S(1)}, bf16[2304,3072]{1,0:T(8,128)(2,1)}) custom-call(bf16[2304,768]{1,0:T(8,128)(2,1)} %bitcast.51.grad_ref, bf16[2304,3072]{1,0:T(8,128)(2,1)} %get-tuple-element.106.slope_ref, bf16[4,1536,768]{2,1,0:T(8,128)(2,1)} %bitcast.294), custom_call_target="tpu_custom_call" | custom-call | flops 679477248 | bytes 442368 | tf_op jit(solution)/shard_map/experts_back/pallas_call | solution.py:693
  333.8 11.5 %expert_grads.4 = bf16[2,4,384,384]{3,2,1,0:T(8,128)(2,1)} custom-call(s32[1]{0:T(128)} %bitcast.57.part, bf16[2304,768]{1,0:T(8,128)(2,1)} %bitcast.49.x_ref, bf16[2304,3072]{1,0:T(8,128)(2,1)} %get-tuple-element.109.pre_ref, bf16[2304,3072]{1,0:T(8,128)(2,1)} %get-tuple-element.113.act_ref, bf16[2304,768]{1,0:T(8,128)(2,1)} %bitcast.51.grad_ref), custom_call_target="tpu_custom_call" | custom-call | flops 84934656 | bytes 221184 | tf_op jit(solution)/shard_map/expert_grads/pallas_call | solution.py:720
  359.9 8.6 %multiply_reduce_fusion.6 = (f32[1024]{0:T(1024)S(1)}, f32[1024]{0:T(1024)S(1)}, f32[1024,768]{1,0:T(8,128)}) fusion(bf16[1024,768]{1,0:T(8,128)(2,1)S(1)} %copy-done.53, f32[1024,768]{1,0:T(8,128)S(1)} %fusion, f32[1024]{0:T(1024)S(1)} %bitcast.336, f32[1024]{0:T(1024)S(1)} %bitcast.335, bf16[2304,768]{1,0:T(8,128)(2,1)} %bitcast.53, s32[1024]{0:T(1024)S(1)} %bitcast.329), kind=kOutput, calls=%fused_computation.47 | convolution fusion | flops 3632527360 | bytes 11423744 | tf_op jit(solution)/shard_map/dot_general | solution.py:51
  368.4 10.2 %expert_grads.5 = bf16[2,4,384,384]{3,2,1,0:T(8,128)(2,1)S(1)} custom-call(s32[1]{0:T(128)} %bitcast.58.part, bf16[2304,768]{1,0:T(8,128)(2,1)} %bitcast.49.x_ref, bf16[2304,3072]{1,0:T(8,128)(2,1)} %get-tuple-element.109.pre_ref, bf16[2304,3072]{1,0:T(8,128)(2,1)} %get-tuple-element.113.act_ref, bf16[2304,768]{1,0:T(8,128)(2,1)} %bitcast.51.grad_ref), custom_call_target="tpu_custom_call" | custom-call | flops 84934656 | bytes 221184 | tf_op jit(solution)/shard_map/expert_grads/pallas_call | solution.py:720
  378.7 10.4 %expert_grads.6 = bf16[2,4,384,384]{3,2,1,0:T(8,128)(2,1)S(1)} custom-call(s32[1]{0:T(128)} %bitcast.59.part, bf16[2304,768]{1,0:T(8,128)(2,1)} %bitcast.49.x_ref, bf16[2304,3072]{1,0:T(8,128)(2,1)} %get-tuple-element.109.pre_ref, bf16[2304,3072]{1,0:T(8,128)(2,1)} %get-tuple-element.113.act_ref, bf16[2304,768]{1,0:T(8,128)(2,1)} %bitcast.51.grad_ref), custom_call_target="tpu_custom_call" | custom-call | flops 84934656 | bytes 221184 | tf_op jit(solution)/shard_map/expert_grads/pallas_call | solution.py:720
  390.4 10.1 %expert_grads.7 = bf16[2,4,384,384]{3,2,1,0:T(8,128)(2,1)S(1)} custom-call(s32[1]{0:T(128)} %bitcast.60.part, bf16[2304,768]{1,0:T(8,128)(2,1)} %bitcast.49.x_ref, bf16[2304,3072]{1,0:T(8,128)(2,1)} %get-tuple-element.109.pre_ref, bf16[2304,3072]{1,0:T(8,128)(2,1)} %get-tuple-element.113.act_ref, bf16[2304,768]{1,0:T(8,128)(2,1)} %bitcast.51.grad_ref), custom_call_target="tpu_custom_call" | custom-call | flops 84934656 | bytes 221184 | tf_op jit(solution)/shard_map/expert_grads/pallas_call | solution.py:720
  400.5 12.6 %collective-permute-done.17 = bf16[2,4,384,384]{3,2,1,0:T(8,128)(2,1)} collective-permute-done((bf16[2,4,384,384]{3,2,1,0:T(8,128)(2,1)}, bf16[2,4,384,384]{3,2,1,0:T(8,128)(2,1)}, u32[]{:S(2)}, u32[]{:S(2)}) %collective-permute-start.17) | collective-permute-done | bytes 2359328 | tf_op jit(solution)/shard_map/ppermute | solution.py:809
  420.8 6.9 %fusion.7 = f32[1024,768]{1,0:T(8,128)S(1)} fusion(bf16[2304,768]{1,0:T(8,128)(2,1)} %bitcast.56, s32[1024]{0:T(1024)S(1)} %bitcast.334, s32[1024]{0:T(1024)S(1)} %bitcast.330), kind=kOutput, calls=%fused_computation.14 | convolution fusion | flops 3642753024 | bytes 6692864 | tf_op jit(solution)/shard_map/dot_general | solution.py:51
  450.8 19.6 %attend_back.2.left_ref = bf16[3,1024,384]{2,1,0:T(8,128)(2,1)S(1)} custom-call(s32[1]{0:T(128)S(6)} %copy.141.kind_ref, bf16[1024,2304]{1,0:T(8,128)(2,1)S(1)} %bitcast.289, bf16[1024,2304]{1,0:T(8,128)(2,1)S(1)} %bitcast.289, bf16[1024,2304]{1,0:T(8,128)(2,1)S(1)} %bitcast.289, bf16[1024,384]{1,0:T(8,128)(2,1)S(1)} %copy-done.18, ...), custom_call_target="tpu_custom_call" | custom-call | flops 251658240 | bytes 147456 | tf_op jit(solution)/shard_map/attend_back/pallas_call | solution.py:229
  470.4 10.1 %collective-permute-done.19 = bf16[2,4,384,384]{3,2,1,0:T(8,128)(2,1)} collective-permute-done((bf16[2,4,384,384]{3,2,1,0:T(8,128)(2,1)}, bf16[2,4,384,384]{3,2,1,0:T(8,128)(2,1)}, u32[]{:S(2)}, u32[]{:S(2)}) %collective-permute-start.19) | collective-permute-done | bytes 2359328 | tf_op jit(solution)/shard_map/ppermute | solution.py:809
  490.6 19.8 %attend_back.3.right_ref = bf16[3,1024,384]{2,1,0:T(8,128)(2,1)S(1)} custom-call(s32[1]{0:T(128)S(6)} %copy.141.kind_ref, bf16[1024,2304]{1,0:T(8,128)(2,1)S(1)} %copy-done.2, bf16[1024,2304]{1,0:T(8,128)(2,1)S(1)} %copy-done.2, bf16[1024,2304]{1,0:T(8,128)(2,1)S(1)} %copy-done.2, bf16[1024,384]{1,0:T(8,128)(2,1)S(1)} %copy-done.16, ...), custom_call_target="tpu_custom_call" | custom-call | flops 251658240 | bytes 147456 | tf_op jit(solution)/shard_map/attend_back/pallas_call | solution.py:229
  510.4 16.2 %triple_back.1 = (f32[1024,768]{1,0:T(8,128)}, bf16[2,2,4,48,832]{4,3,2,1,0:T(8,128)(2,1)S(1)}, bf16[2,2,4,48,832]{4,3,2,1,0:T(8,128)(2,1)S(1)}, bf16[2,2,4,48,8...) custom-call(s32[4]{0:T(128)S(1)} %copy-done.40, bf16[3,1024,384]{2,1,0:T(8,128)(2,1)S(1)} %copy-done.13, ...), custom_call_target="tpu_custom_call" | custom-call | flops 113246208 | bytes 147456 | tf_op jit(solution)/shard_map/triple_back/pallas_call | solution.py:631
  526.6 11.7 %collective-permute-done.21 = bf16[4,384,384]{2,1,0:T(8,128)(2,1)} collective-permute-done((bf16[4,384,384]{2,1,0:T(8,128)(2,1)}, bf16[4,384,384]{2,1,0:T(8,128)(2,1)}, u32[]{:S(2)}, u32[]{:S(2)}) %collective-permute-start.21) | collective-permute-done | bytes 1179680 | tf_op jit(solution)/shard_map/ppermute | solution.py:813
  597.8 9.5 %collective-permute-done.29 = bf16[96,832]{1,0:T(8,128)(2,1)S(1)} collective-permute-done((bf16[96,832]{1,0:T(8,128)(2,1)S(1)}, bf16[96,832]{1,0:T(8,128)(2,1)S(1)}, u32[]{:S(2)}, u32[]{:S(2)}) %collective-permute-start.29) | collective-permute-done | bytes 159776 | tf_op jit(solution)/shard_map/ppermute | solution.py:809
  (363 shorter events, 234.2 us)
Async XLA Ops:
  7.2 54.3 %all-gather.5.cloned.1.call-start = ((), (), s32[]{:S(2)}) async-start(), calls=%async_computation.10 | async-start | bytes 1474560 | tf_op jit(solution)/shard_map/all_gather | solution.py:942
  9.2 16.9 %collective-permute-start.1 = (bf16[96,832]{1,0:T(8,128)(2,1)S(1)}, bf16[96,832]{1,0:T(8,128)(2,1)S(1)}, u32[]{:S(2)}, u32[]{:S(2)}) collective-permute-start(bf16[96,832]{1,0:T(8,128)(2,1)S(1)} %pad_maximum_fusion.13), channel_id=1, source_target_pairs={{0,4},{2,6},{4,0},{6,2},{1,5},{3,7},{5,1},{7,3},{8,12},{10,14},{12... | collective-permute-start | bytes 479240 | tf_op jit(solution)/shard_map/ppermute | solution.py:809
  35.3 22.3 %all-to-all-start.1 = ((bf16[32,4,1152]{2,1,0:T(4,128)(2,1)}), bf16[32,4,1152]{2,1,0:T(4,128)(2,1)}, u32[]{:S(2)}, u32[]{:S(2)}) async-start(bf16[32,4,1152]{2,1,0:T(4,128)(2,1)} %reshape.440), calls=%async_computation.1 | async-start | bytes 589824 | tf_op jit(solution)/shard_map/all_to_all | solution.py:920
  38.6 214.6 %all-gather.7.cloned.1.call-start = ((), (), s32[]{:S(2)}) async-start(), calls=%async_computation.11 | async-start | bytes 11796480 | tf_op jit(solution)/shard_map/all_gather | solution.py:943
  39.6 19.3 %collective-permute-start.4 = (bf16[384,768]{1,0:T(8,128)(2,1)}, bf16[384,768]{1,0:T(8,128)(2,1)S(1)}, u32[]{:S(2)}, u32[]{:S(2)}) collective-permute-start(bf16[384,768]{1,0:T(8,128)(2,1)} %get-tuple-element.271), channel_id=1, source_target_pairs={{0,1},{1,0},{2,3},{3,2},{4,5},{5,4},{6,7},{7,6},{8,9},{9,8},{10,11... | collective-permute-start | bytes 1769480 | tf_op jit(solution)/shard_map/ppermute | solution.py:816
  114.1 20.3 %collective-permute-start.12 = (bf16[4,96,768]{2,1,0:T(8,128)(2,1)S(1)}, bf16[4,96,768]{2,1,0:T(8,128)(2,1)S(1)}, u32[]{:S(2)}, u32[]{:S(2)}) collective-permute-start(bf16[4,96,768]{2,1,0:T(8,128)(2,1)S(1)} %get-tuple-element.266), channel_id=1, source_target_pairs={{0,16},{8,24},{16,0},{24,8},{1,17},{9,25},{17,1},{25,9},{2,18},{10... | collective-permute-start | bytes 1769480 | tf_op jit(solution)/shard_map/ppermute | solution.py:819
  115.0 20.6 %collective-permute-start.11 = (bf16[4,96,768]{2,1,0:T(8,128)(2,1)S(1)}, bf16[4,96,768]{2,1,0:T(8,128)(2,1)S(1)}, u32[]{:S(2)}, u32[]{:S(2)}) collective-permute-start(bf16[4,96,768]{2,1,0:T(8,128)(2,1)S(1)} %get-tuple-element.267), channel_id=1, source_target_pairs={{0,1},{1,0},{2,3},{3,2},{4,5},{5,4},{6,7},{7,6},{8,9},{9,8},{10,11... | collective-permute-start | bytes 1769480 | tf_op jit(solution)/shard_map/ppermute | solution.py:816
  136.8 47.6 %collective-permute-start.13 = (bf16[2,4,96,768]{3,2,1,0:T(8,128)(2,1)}, bf16[2,4,96,768]{3,2,1,0:T(8,128)(2,1)}, u32[]{:S(2)}, u32[]{:S(2)}) collective-permute-start(bf16[2,4,96,768]{3,2,1,0:T(8,128)(2,1)} %pad_maximum_fusion.7), channel_id=1, source_target_pairs={{0,16},{8,24},{16,0},{24,8},{1,17},{9,25},{17,1},{25,9},{2,18},{10... | collective-permute-start | bytes 3538952 | tf_op jit(solution)/shard_map/ppermute | solution.py:819
  137.6 43.4 %collective-permute-start.14 = (bf16[2,4,96,768]{3,2,1,0:T(8,128)(2,1)}, bf16[2,4,96,768]{3,2,1,0:T(8,128)(2,1)}, u32[]{:S(2)}, u32[]{:S(2)}) collective-permute-start(bf16[2,4,96,768]{3,2,1,0:T(8,128)(2,1)} %pad_maximum_fusion.8), channel_id=1, source_target_pairs={{0,1},{1,0},{2,3},{3,2},{4,5},{5,4},{6,7},{7,6},{8,9},{9,8},{10,11... | collective-permute-start | bytes 3538952 | tf_op jit(solution)/shard_map/ppermute | solution.py:816
  187.6 17.3 %collective-permute-start.15 = (bf16[2,2,4,96,768]{4,3,2,1,0:T(8,128)(2,1)}, bf16[2,2,4,96,768]{4,3,2,1,0:T(8,128)(2,1)}, u32[]{:S(2)}, u32[]{:S(2)}) collective-permute-start(bf16[2,2,4,96,768]{4,3,2,1,0:T(8,128)(2,1)} %pad_maximum_fusion.1.in_own), channel_id=1, source_target_pairs={{0,8},{8,0},{16,24},{24,16},{1,9},{9,1},{17,25},{25,17},{2,10},{10... | collective-permute-start | bytes 7077896 | tf_op jit(solution)/shard_map/ppermute | solution.py:822
  187.6 17.3 %collective-permute-start.16 = (bf16[2,2,4,96,768]{4,3,2,1,0:T(8,128)(2,1)}, bf16[2,2,4,96,768]{4,3,2,1,0:T(8,128)(2,1)}, u32[]{:S(2)}, u32[]{:S(2)}) collective-permute-start(bf16[2,2,4,96,768]{4,3,2,1,0:T(8,128)(2,1)} %pad_maximum_fusion.2.out_own), channel_id=1, source_target_pairs={{0,8},{8,0},{16,24},{24,16},{1,9},{9,1},{17,25},{25,17},{2,10},{10... | collective-permute-start | bytes 7077896 | tf_op jit(solution)/shard_map/ppermute | solution.py:822
  188.1 59.9 %all-to-all-start.2 = ((bf16[8,288,768]{2,1,0:T(8,128)(2,1)}), bf16[8,288,768]{2,1,0:T(8,128)(2,1)}, u32[]{:S(2)}, u32[]{:S(2)}) async-start(bf16[8,288,768]{2,1,0:T(8,128)(2,1)} %bitcast.296), calls=%async_computation.2 | async-start | bytes 7077888 | tf_op jit(solution)/shard_map/all_to_all | solution.py:1028
  247.9 45.7 %all-to-all-start.3 = ((bf16[8,288,768]{2,1,0:T(8,128)(2,1)}), bf16[8,288,768]{2,1,0:T(8,128)(2,1)}, u32[]{:S(2)}, u32[]{:S(2)}) async-start(bf16[8,288,768]{2,1,0:T(8,128)(2,1)} %bitcast.297), calls=%async_computation.3 | async-start | bytes 7077888 | tf_op jit(solution)/shard_map/all_to_all | solution.py:1028
  252.4 233.1 %reduce-scatter.2.cloned.1.call-start = ((), (), s32[]{:S(2)}) async-start(), calls=%async_computation.9 | async-start | bytes 9732096 | tf_op jit(solution)/shard_map/reduce_scatter | solution.py:1180
  293.7 54.5 %all-to-all-start.4 = ((bf16[8,288,768]{2,1,0:T(8,128)(2,1)}), bf16[8,288,768]{2,1,0:T(8,128)(2,1)}, u32[]{:S(2)}, u32[]{:S(2)}) async-start(bf16[8,288,768]{2,1,0:T(8,128)(2,1)} %bitcast.290), calls=%async_computation.4 | async-start | bytes 7077888 | tf_op jit(solution)/shard_map/all_to_all | solution.py:1028
  345.2 67.9 %collective-permute-start.17 = (bf16[2,4,384,384]{3,2,1,0:T(8,128)(2,1)}, bf16[2,4,384,384]{3,2,1,0:T(8,128)(2,1)}, u32[]{:S(2)}, u32[]{:S(2)}) collective-permute-start(bf16[2,4,384,384]{3,2,1,0:T(8,128)(2,1)} %expert_grads.4), channel_id=1, source_target_pairs={{0,2},{2,4},{4,6},{6,0},{1,3},{3,5},{5,7},{7,1},{8,10},{10,12},{12... | collective-permute-start | bytes 7077896 | tf_op jit(solution)/shard_map/ppermute | solution.py:809
  348.1 70.1 %all-to-all-start.5 = ((bf16[8,288,768]{2,1,0:T(8,128)(2,1)}), bf16[8,288,768]{2,1,0:T(8,128)(2,1)}, u32[]{:S(2)}, u32[]{:S(2)}) async-start(bf16[8,288,768]{2,1,0:T(8,128)(2,1)} %bitcast.291), calls=%async_computation.5 | async-start | bytes 7077888 | tf_op jit(solution)/shard_map/all_to_all | solution.py:1028
  418.2 62.3 %collective-permute-start.19 = (bf16[2,4,384,384]{3,2,1,0:T(8,128)(2,1)}, bf16[2,4,384,384]{3,2,1,0:T(8,128)(2,1)}, u32[]{:S(2)}, u32[]{:S(2)}) collective-permute-start(bf16[2,4,384,384]{3,2,1,0:T(8,128)(2,1)} %add_convert_fusion.2), channel_id=1, source_target_pairs={{0,2},{2,4},{4,6},{6,0},{1,3},{3,5},{5,7},{7,1},{8,10},{10,12},{12... | collective-permute-start | bytes 7077896 | tf_op jit(solution)/shard_map/ppermute | solution.py:809
  420.8 30.0 %collective-permute-start.18 = (bf16[4,384,384]{2,1,0:T(8,128)(2,1)}, bf16[4,384,384]{2,1,0:T(8,128)(2,1)}, u32[]{:S(2)}, u32[]{:S(2)}) collective-permute-start(bf16[4,384,384]{2,1,0:T(8,128)(2,1)} %slice_bitcast_fusion.3), channel_id=1, source_target_pairs={{0,1},{1,0},{2,3},{3,2},{4,5},{5,4},{6,7},{7,6},{8,9},{9,8},{10,11... | collective-permute-start | bytes 3538952 | tf_op jit(solution)/shard_map/ppermute | solution.py:816
  484.7 41.9 %collective-permute-start.20 = (bf16[4,384,384]{2,1,0:T(8,128)(2,1)}, bf16[4,384,384]{2,1,0:T(8,128)(2,1)}, u32[]{:S(2)}, u32[]{:S(2)}) collective-permute-start(bf16[4,384,384]{2,1,0:T(8,128)(2,1)} %get-tuple-element.130), channel_id=1, source_target_pairs={{0,2},{2,4},{4,6},{6,0},{1,3},{3,5},{5,7},{7,1},{8,10},{10,12},{12... | collective-permute-start | bytes 3538952 | tf_op jit(solution)/shard_map/ppermute | solution.py:809
  484.7 53.7 %collective-permute-start.21 = (bf16[4,384,384]{2,1,0:T(8,128)(2,1)}, bf16[4,384,384]{2,1,0:T(8,128)(2,1)}, u32[]{:S(2)}, u32[]{:S(2)}) collective-permute-start(bf16[4,384,384]{2,1,0:T(8,128)(2,1)} %get-tuple-element.131), channel_id=1, source_target_pairs={{0,3},{1,2},{2,5},{3,4},{4,7},{5,6},{6,1},{7,0},{8,11},{9,10},{10,... | collective-permute-start | bytes 3538952 | tf_op jit(solution)/shard_map/ppermute | solution.py:813
  546.9 26.1 %collective-permute-start.24 = (bf16[2,4,48,832]{3,2,1,0:T(8,128)(2,1)}, bf16[2,4,48,832]{3,2,1,0:T(8,128)(2,1)}, u32[]{:S(2)}, u32[]{:S(2)}) collective-permute-start(bf16[2,4,48,832]{3,2,1,0:T(8,128)(2,1)} %get-tuple-element.253), channel_id=1, source_target_pairs={{0,16},{8,24},{16,0},{24,8},{1,17},{9,25},{17,1},{25,9},{2,18},{10... | collective-permute-start | bytes 1916936 | tf_op jit(solution)/shard_map/ppermute | solution.py:819
  551.6 17.9 %all-to-all-start.6 = ((bf16[32,4,1152]{2,1,0:T(4,128)(2,1)}), bf16[32,4,1152]{2,1,0:T(4,128)(2,1)S(1)}, u32[]{:S(2)}, u32[]{:S(2)}) async-start(bf16[32,4,1152]{2,1,0:T(4,128)(2,1)} %bitcast.299), calls=%async_computation.6 | async-start | bytes 589824 | tf_op jit(solution)/shard_map/all_to_all | solution.py:1159
  558.5 19.8 %collective-permute-start.26 = (bf16[2,4,48,832]{3,2,1,0:T(8,128)(2,1)}, bf16[2,4,48,832]{3,2,1,0:T(8,128)(2,1)}, u32[]{:S(2)}, u32[]{:S(2)}) collective-permute-start(bf16[2,4,48,832]{3,2,1,0:T(8,128)(2,1)} %get-tuple-element.251), channel_id=1, source_target_pairs={{0,1},{1,0},{2,3},{3,2},{4,5},{5,4},{6,7},{7,6},{8,9},{9,8},{10,11... | collective-permute-start | bytes 1916936 | tf_op jit(solution)/shard_map/ppermute | solution.py:816
  (91 other events, 950.8 us)
Sparse Core Ops, SparseCore 0:
  22.7 34.3 all-gather.4
  61.7 165.9 all-gather.6
  259.2 222.1 reduce-scatter.1

commit v6 on v5

--- a/solution.py
+++ b/solution.py
@@ -1123,9 +1123,8 @@
     )
     if ring.direct:
         own_1, give_1, own_2, give_2 = dense_grads
-        give_1, give_2 = after(give_1, own, aside), after(give_2, own, aside)
         got_1, got_2 = ring.over_core(give_1), ring.over_core(give_2)
-        grad_attend_in = after(grad_attend_in, got_1, got_2)
+        grad_attend_in = after(grad_attend_in, own, aside)
         sum_1, give_1 = add_both(own_1, got_1)
         sum_2, give_2 = add_both(own_2, got_2)
         got_1, got_2 = ring.outer(give_1, False), ring.outer(give_2, True)

time: 620 us -> 624 us (level)
  Pallas kernels: 264 us -> 227 us
  waiting for transfers between devices: 115 us -> 141 us
  starting transfers between devices: 63.4 us -> 74.5 us
    pallas_call x2, Pallas kernels: 39.4 us -> 17.6 us  [attend_back(): pl.pallas_call(attend_back_kernel, out_shape=jax.ShapeDtypeStruct((3, tri...]
    ppermute x9, waiting for transfers between devices: 34.9 us -> 52.4 us  [step(): return lax.ppermute(value, 'zi', [(i, (i + by) % n) for i in range(n)])]
    pallas_call x2, Pallas kernels: 27.4 us -> 11.3 us  [attend(): pl.pallas_call(attend_kernel, out_shape=(jax.ShapeDtypeStruct((triple.sha...]
    ppermute x6, waiting for transfers between devices: 16 us -> 25.4 us  [over_x(): return lax.ppermute(value, 'exp', [(i, i ^ 2) for i in range(4)])]
    ppermute x1, waiting for transfers between devices: 11.7 us -> 19.8 us  [step_aside(): return lax.ppermute(value, FSDP, [(i, (i + 2) % n ^ 1) for i in range(n)])]
    all_to_all x1, waiting for transfers between devices: 6.58 us -> 0.01 us  [local(): lax.all_to_all(mod_send.reshape(n_all, blocks, mod_cols), ALL, 0, 0, tile...]
    unnamed x157 -> x151, local copies, waits for them, and re-layouts: 21.4 us -> 20.4 us
  transfers between devices with their start and end apart: 42 -> 42, of which waited for: 18 -> 19; matrix products, arithmetic and copies ran while one was open for 22% -> 23% of each run, Pallas kernels for 43% -> 37%
where the time goes in v6:
time: 624 us; the launch traced here: 620 us
  Pallas kernels  227 us (36%)
  waiting for transfers between devices  141 us (23%)
  other arithmetic  75.3 us (12%)
  starting transfers between devices  74.5 us (12%)
  matrix products  46.3 us (7%)
  local copies, waits for them, and re-layouts  40.2 us (6%)
  between operations  15.9 us (3%)
    pallas_call x2, Pallas kernels, expert_call(): pl.pallas_call(kernel, out_shape=(jax.ShapeDtypeStruct((rows, width), BF1...  68.1 us
    ppermute x9, waiting for transfers between devices, step(): return lax.ppermute(value, 'zi', [(i, (i + by) % n) for i in range(n)])  52.4 us
    dot_general x10, matrix products, dot(): lax.dot_general(left, right, (dims, ((), ())), preferred_element_type=F32)  46.3 us
    pallas_call x1, Pallas kernels, shared_expert(): pl.pallas_call(shared_kernel, out_shape=(jax.ShapeDtypeStruct((tok_count,...  43.2 us
    pallas_call x4, Pallas kernels, expert_grads(): pl.pallas_call(expert_grads_kernel, out_shape=out, grid_spec=pltpu.Prefet...  42 us
    ppermute x6, waiting for transfers between devices, over_x(): return lax.ppermute(value, 'exp', [(i, i ^ 2) for i in range(4)])  25.4 us
    all_to_all x4, starting transfers between devices, exchange(): return lax.all_to_all(rows, ('exp', 'yi'), 0, 0, tiled=True)  24.5 us
    unnamed x151, local copies, waits for them, and re-layouts  20.4 us
  transfers between devices with their start and end apart: 42, of which 19 were waited for; matrix products, arithmetic and copies ran while one was open for 23% of the time, Pallas kernels for 37%

profile of v6, /device:TPU:0, one launch (start us, length us, event | category | flops | bytes accessed | tf_op | source)
XLA Modules:
  0.0 619.8 jit_solution(7203067544833635641)
XLA Ops:
  41.2 16.5 %all-to-all-done.1 = bf16[32,4,1152]{2,1,0:T(4,128)(2,1)} async-done(((bf16[32,4,1152]{2,1,0:T(4,128)(2,1)}), bf16[32,4,1152]{2,1,0:T(4,128)(2,1)}, u32[]{:S(2)}, u32[]{:S(2)}) %all-to-all-start.1) | async-done | bytes 294944 | tf_op jit(solution)/shard_map/all_to_all | solution.py:920
  63.4 7.6 %collective-permute-done.5 = bf16[4,48,832]{2,1,0:T(8,128)(2,1)S(1)} collective-permute-done((bf16[4,48,832]{2,1,0:T(8,128)(2,1)S(1)}, bf16[4,48,832]{2,1,0:T(8,128)(2,1)S(1)}, u32[]{:S(2)}, u32[]{:S(2)}) %collective-permute-start.5) | collective-permute-done | bytes 319520 | tf_op jit(solution)/shard_map/ppermute | solution.py:816
  73.3 14.2 %collective-permute-done.6 = bf16[2,4,48,832]{3,2,1,0:T(8,128)(2,1)S(1)} collective-permute-done((bf16[2,4,48,832]{3,2,1,0:T(8,128)(2,1)S(1)}, bf16[2,4,48,832]{3,2,1,0:T(8,128)(2,1)S(1)}, u32[]{:S(2)}, u32[]{:S(2)}) %collective-permute-start.6) | collective-permute-done | bytes 639008 | tf_op jit(solution)/shard_map/ppermute | solution.py:819
  101.1 12.7 %triple.1 = (bf16[1024,768]{1,0:T(8,128)(2,1)S(1)}, bf16[1024,2304]{1,0:T(8,128)(2,1)}, bf16[768,2304]{1,0:T(8,128)(2,1)S(1)}) custom-call(s32[4]{0:T(128)S(1)} %pad_add_fusion.me, bf16[1024,768]{1,0:T(8,128)(2,1)S(1)} %copy-done.3, f32[4,1,768]{2,1,0:T(1,128)S(1)} %get-tuple-element.293.shift_ref, f32[4,1,768]{2,1,0:T(1,128)S(1)} %get-tuple-element.292.scale_ref, ...), custom_call_target="tpu_custom_call" | custom-call | flops 56623104 | bytes 98304 | tf_op jit(solution)/shard_map/triple/pallas_call | solution.py:312
  143.4 11.6 %project.1 = (f32[1024,768]{1,0:T(8,128)S(1)}, f32[1024,768]{1,0:T(8,128)S(1)}, bf16[1024,768]{1,0:T(8,128)(2,1)S(1)}, f32[1024,128]{1,0:T(8,128)S(1)}, bf16[768...) custom-call(s32[4]{0:T(128)S(1)} %pad_add_fusion.me, bf16[1024,384]{1,0:T(8,128)(2,1)S(1)} %get-tuple-element.79.left_ref.mixed_ref, ...), custom_call_target="tpu_custom_call" | custom-call | flops 18874368 | bytes 196608 | tf_op jit(solution)/shard_map/project/pallas_call | solution.py:397
  161.9 7.8 %convolution_convert_fusion = bf16[2304,768]{1,0:T(8,128)(2,1)} fusion(bf16[1024,768]{1,0:T(8,128)(2,1)} %copy-done.25, s32[1024]{0:T(1024)S(1)} %bitcast.330, s32[1024]{0:T(1024)S(1)} %bitcast.326), kind=kOutput, calls=%fused_computation.10 | convolution fusion | flops 3644522496 | bytes 5120000 | tf_op jit(solution)/shard_map/dot_general | solution.py:51
  179.0 10.0 %all-to-all-start.2 = ((bf16[8,288,768]{2,1,0:T(8,128)(2,1)}), bf16[8,288,768]{2,1,0:T(8,128)(2,1)}, u32[]{:S(2)}, u32[]{:S(2)}) async-start(bf16[8,288,768]{2,1,0:T(8,128)(2,1)} %bitcast.296), calls=%async_computation.2 | async-start | bytes 7077888 | tf_op jit(solution)/shard_map/all_to_all | solution.py:1028
  200.9 43.2 %shared_expert.1 = (f32[1024,768]{1,0:T(8,128)}, f32[1024,768]{1,0:T(8,128)}, bf16[4,8,192,768]{3,2,1,0:T(8,128)(2,1)}) custom-call(s32[4]{0:T(128)} %copy-done.41, bf16[1024,768]{1,0:T(8,128)(2,1)} %copy-done.25, bf16[1024,768]{1,0:T(8,128)(2,1)} %get-tuple-element.241.grad_ref, bf16[2,2,4,96,768]{4,3,2,1,0:T(8,128)(2,1)} %pad_maximum_fusion.1.in_own, ...), custom_call_target="tpu_custom_call" | custom-call | flops 28991029248 | bytes 12582912 | tf_op jit(solution)/shard_map/shared_expert/pallas_call | solution.py:503
  249.7 36.6 %experts.1 = (bf16[2304,768]{1,0:T(8,128)(2,1)S(1)}, bf16[2304,3072]{1,0:T(8,128)(2,1)}, bf16[2304,3072]{1,0:T(8,128)(2,1)}) custom-call(bf16[2304,768]{1,0:T(8,128)(2,1)} %bitcast.49.x_ref, bf16[4,1536,768]{2,1,0:T(8,128)(2,1)} %bitcast.293), custom_call_target="tpu_custom_call" | custom-call | flops 679477248 | bytes 663552 | tf_op jit(solution)/shard_map/experts/pallas_call | solution.py:693
  298.4 31.5 %experts_back.1 = (bf16[2304,768]{1,0:T(8,128)(2,1)S(1)}, bf16[2304,3072]{1,0:T(8,128)(2,1)}) custom-call(bf16[2304,768]{1,0:T(8,128)(2,1)} %bitcast.51.grad_ref, bf16[2304,3072]{1,0:T(8,128)(2,1)} %get-tuple-element.104.slope_ref, bf16[4,1536,768]{2,1,0:T(8,128)(2,1)} %bitcast.294), custom_call_target="tpu_custom_call" | custom-call | flops 679477248 | bytes 442368 | tf_op jit(solution)/shard_map/experts_back/pallas_call | solution.py:693
  331.7 11.4 %expert_grads.4 = bf16[2,4,384,384]{3,2,1,0:T(8,128)(2,1)} custom-call(s32[1]{0:T(128)} %bitcast.57.part, bf16[2304,768]{1,0:T(8,128)(2,1)} %bitcast.49.x_ref, bf16[2304,3072]{1,0:T(8,128)(2,1)} %get-tuple-element.107.pre_ref, bf16[2304,3072]{1,0:T(8,128)(2,1)} %get-tuple-element.111.act_ref, bf16[2304,768]{1,0:T(8,128)(2,1)} %bitcast.51.grad_ref), custom_call_target="tpu_custom_call" | custom-call | flops 84934656 | bytes 221184 | tf_op jit(solution)/shard_map/expert_grads/pallas_call | solution.py:720
  350.9 6.6 %fusion = f32[1024,768]{1,0:T(8,128)S(1)} fusion(bf16[2304,768]{1,0:T(8,128)(2,1)} %bitcast.53, s32[1024]{0:T(1024)S(1)} %bitcast.332), kind=kOutput, calls=%fused_computation.1 | convolution fusion | flops 3626237952 | bytes 6688768 | tf_op jit(solution)/shard_map/dot_general | solution.py:51
  357.5 8.7 %multiply_reduce_fusion.6 = (f32[1024]{0:T(1024)S(1)}, f32[1024]{0:T(1024)S(1)}, f32[1024,768]{1,0:T(8,128)}) fusion(bf16[1024,768]{1,0:T(8,128)(2,1)S(1)} %copy-done.51, f32[1024,768]{1,0:T(8,128)S(1)} %fusion, f32[1024]{0:T(1024)S(1)} %bitcast.335, f32[1024]{0:T(1024)S(1)} %bitcast.334, bf16[2304,768]{1,0:T(8,128)(2,1)} %bitcast.53, s32[1024]{0:T(1024)S(1)} %bitcast.328), kind=kOutput, calls=%fused_computation.47 | convolution fusion | flops 3632527360 | bytes 11423744 | tf_op jit(solution)/shard_map/dot_general | solution.py:51
  366.2 10.1 %expert_grads.5 = bf16[2,4,384,384]{3,2,1,0:T(8,128)(2,1)S(1)} custom-call(s32[1]{0:T(128)} %bitcast.58.part, bf16[2304,768]{1,0:T(8,128)(2,1)} %bitcast.49.x_ref, bf16[2304,3072]{1,0:T(8,128)(2,1)} %get-tuple-element.107.pre_ref, bf16[2304,3072]{1,0:T(8,128)(2,1)} %get-tuple-element.111.act_ref, bf16[2304,768]{1,0:T(8,128)(2,1)} %bitcast.51.grad_ref), custom_call_target="tpu_custom_call" | custom-call | flops 84934656 | bytes 221184 | tf_op jit(solution)/shard_map/expert_grads/pallas_call | solution.py:720
  376.3 10.4 %expert_grads.6 = bf16[2,4,384,384]{3,2,1,0:T(8,128)(2,1)S(1)} custom-call(s32[1]{0:T(128)} %bitcast.59.part, bf16[2304,768]{1,0:T(8,128)(2,1)} %bitcast.49.x_ref, bf16[2304,3072]{1,0:T(8,128)(2,1)} %get-tuple-element.107.pre_ref, bf16[2304,3072]{1,0:T(8,128)(2,1)} %get-tuple-element.111.act_ref, bf16[2304,768]{1,0:T(8,128)(2,1)} %bitcast.51.grad_ref), custom_call_target="tpu_custom_call" | custom-call | flops 84934656 | bytes 221184 | tf_op jit(solution)/shard_map/expert_grads/pallas_call | solution.py:720
  388.1 10.1 %expert_grads.7 = bf16[2,4,384,384]{3,2,1,0:T(8,128)(2,1)S(1)} custom-call(s32[1]{0:T(128)} %bitcast.60.part, bf16[2304,768]{1,0:T(8,128)(2,1)} %bitcast.49.x_ref, bf16[2304,3072]{1,0:T(8,128)(2,1)} %get-tuple-element.107.pre_ref, bf16[2304,3072]{1,0:T(8,128)(2,1)} %get-tuple-element.111.act_ref, bf16[2304,768]{1,0:T(8,128)(2,1)} %bitcast.51.grad_ref), custom_call_target="tpu_custom_call" | custom-call | flops 84934656 | bytes 221184 | tf_op jit(solution)/shard_map/expert_grads/pallas_call | solution.py:720
  398.2 17.8 %collective-permute-done.17 = bf16[2,4,384,384]{3,2,1,0:T(8,128)(2,1)} collective-permute-done((bf16[2,4,384,384]{3,2,1,0:T(8,128)(2,1)}, bf16[2,4,384,384]{3,2,1,0:T(8,128)(2,1)}, u32[]{:S(2)}, u32[]{:S(2)}) %collective-permute-start.17) | collective-permute-done | bytes 2359328 | tf_op jit(solution)/shard_map/ppermute | solution.py:809
  423.7 6.8 %fusion.7 = f32[1024,768]{1,0:T(8,128)S(1)} fusion(bf16[2304,768]{1,0:T(8,128)(2,1)} %bitcast.56, s32[1024]{0:T(1024)S(1)} %bitcast.333, s32[1024]{0:T(1024)S(1)} %bitcast.329), kind=kOutput, calls=%fused_computation.14 | convolution fusion | flops 3642753024 | bytes 6692864 | tf_op jit(solution)/shard_map/dot_general | solution.py:51
  451.6 8.7 %attend_back.2.left_ref = bf16[3,1024,384]{2,1,0:T(8,128)(2,1)S(1)} custom-call(s32[1]{0:T(128)S(6)} %copy.141.kind_ref, bf16[1024,2304]{1,0:T(8,128)(2,1)S(1)} %bitcast.289, bf16[1024,2304]{1,0:T(8,128)(2,1)S(1)} %bitcast.289, bf16[1024,2304]{1,0:T(8,128)(2,1)S(1)} %bitcast.289, bf16[1024,384]{1,0:T(8,128)(2,1)S(1)} %copy-done.18, ...), custom_call_target="tpu_custom_call" | custom-call | flops 251658240 | bytes 147456 | tf_op jit(solution)/shard_map/attend_back/pallas_call | solution.py:229
  460.3 21.9 %collective-permute-done.19 = bf16[2,4,384,384]{3,2,1,0:T(8,128)(2,1)} collective-permute-done((bf16[2,4,384,384]{3,2,1,0:T(8,128)(2,1)}, bf16[2,4,384,384]{3,2,1,0:T(8,128)(2,1)}, u32[]{:S(2)}, u32[]{:S(2)}) %collective-permute-start.19) | collective-permute-done | bytes 2359328 | tf_op jit(solution)/shard_map/ppermute | solution.py:809
  492.3 8.9 %attend_back.3.right_ref = bf16[3,1024,384]{2,1,0:T(8,128)(2,1)S(1)} custom-call(s32[1]{0:T(128)S(6)} %copy.141.kind_ref, bf16[1024,2304]{1,0:T(8,128)(2,1)S(1)} %copy-done.2, bf16[1024,2304]{1,0:T(8,128)(2,1)S(1)} %copy-done.2, bf16[1024,2304]{1,0:T(8,128)(2,1)S(1)} %copy-done.2, bf16[1024,384]{1,0:T(8,128)(2,1)S(1)} %copy-done.16, ...), custom_call_target="tpu_custom_call" | custom-call | flops 251658240 | bytes 147456 | tf_op jit(solution)/shard_map/attend_back/pallas_call | solution.py:229
  501.3 17.1 %triple_back.1 = (f32[1024,768]{1,0:T(8,128)}, bf16[2,2,4,48,832]{4,3,2,1,0:T(8,128)(2,1)S(1)}, bf16[2,2,4,48,832]{4,3,2,1,0:T(8,128)(2,1)}, bf16[2,2,4,48,832]{...) custom-call(s32[4]{0:T(128)S(1)} %copy-done.42, bf16[3,1024,384]{2,1,0:T(8,128)(2,1)S(1)} %copy-done.13, ...), custom_call_target="tpu_custom_call" | custom-call | flops 113246208 | bytes 147456 | tf_op jit(solution)/shard_map/triple_back/pallas_call | solution.py:631
  518.9 19.8 %collective-permute-done.21 = bf16[4,384,384]{2,1,0:T(8,128)(2,1)} collective-permute-done((bf16[4,384,384]{2,1,0:T(8,128)(2,1)}, bf16[4,384,384]{2,1,0:T(8,128)(2,1)}, u32[]{:S(2)}, u32[]{:S(2)}) %collective-permute-start.21) | collective-permute-done | bytes 1179680 | tf_op jit(solution)/shard_map/ppermute | solution.py:813
  601.9 9.0 %collective-permute-done.29 = bf16[96,832]{1,0:T(8,128)(2,1)S(1)} collective-permute-done((bf16[96,832]{1,0:T(8,128)(2,1)S(1)}, bf16[96,832]{1,0:T(8,128)(2,1)S(1)}, u32[]{:S(2)}, u32[]{:S(2)}) %collective-permute-start.29) | collective-permute-done | bytes 159776 | tf_op jit(solution)/shard_map/ppermute | solution.py:809
  (357 shorter events, 244.8 us)
Async XLA Ops:
  7.2 54.3 %all-gather.5.cloned.1.call-start = ((), (), s32[]{:S(2)}) async-start(), calls=%async_computation.10 | async-start | bytes 1474560 | tf_op jit(solution)/shard_map/all_gather | solution.py:942
  35.3 22.3 %all-to-all-start.1 = ((bf16[32,4,1152]{2,1,0:T(4,128)(2,1)}), bf16[32,4,1152]{2,1,0:T(4,128)(2,1)}, u32[]{:S(2)}, u32[]{:S(2)}) async-start(bf16[32,4,1152]{2,1,0:T(4,128)(2,1)} %reshape.440), calls=%async_computation.1 | async-start | bytes 589824 | tf_op jit(solution)/shard_map/all_to_all | solution.py:920
  38.6 211.1 %all-gather.7.cloned.1.call-start = ((), (), s32[]{:S(2)}) async-start(), calls=%async_computation.11 | async-start | bytes 11796480 | tf_op jit(solution)/shard_map/all_gather | solution.py:943
  39.6 19.3 %collective-permute-start.4 = (bf16[384,768]{1,0:T(8,128)(2,1)}, bf16[384,768]{1,0:T(8,128)(2,1)S(1)}, u32[]{:S(2)}, u32[]{:S(2)}) collective-permute-start(bf16[384,768]{1,0:T(8,128)(2,1)} %get-tuple-element.267), channel_id=1, source_target_pairs={{0,1},{1,0},{2,3},{3,2},{4,5},{5,4},{6,7},{7,6},{8,9},{9,8},{10,11... | collective-permute-start | bytes 1769480 | tf_op jit(solution)/shard_map/ppermute | solution.py:816
  132.1 42.9 %collective-permute-start.13 = (bf16[2,4,96,768]{3,2,1,0:T(8,128)(2,1)}, bf16[2,4,96,768]{3,2,1,0:T(8,128)(2,1)}, u32[]{:S(2)}, u32[]{:S(2)}) collective-permute-start(bf16[2,4,96,768]{3,2,1,0:T(8,128)(2,1)} %pad_maximum_fusion.7), channel_id=1, source_target_pairs={{0,16},{8,24},{16,0},{24,8},{1,17},{9,25},{17,1},{25,9},{2,18},{10... | collective-permute-start | bytes 3538952 | tf_op jit(solution)/shard_map/ppermute | solution.py:819
  137.6 34.1 %collective-permute-start.14 = (bf16[2,4,96,768]{3,2,1,0:T(8,128)(2,1)}, bf16[2,4,96,768]{3,2,1,0:T(8,128)(2,1)}, u32[]{:S(2)}, u32[]{:S(2)}) collective-permute-start(bf16[2,4,96,768]{3,2,1,0:T(8,128)(2,1)} %pad_maximum_fusion.8), channel_id=1, source_target_pairs={{0,1},{1,0},{2,3},{3,2},{4,5},{5,4},{6,7},{7,6},{8,9},{9,8},{10,11... | collective-permute-start | bytes 3538952 | tf_op jit(solution)/shard_map/ppermute | solution.py:816
  178.3 22.6 %collective-permute-start.15 = (bf16[2,2,4,96,768]{4,3,2,1,0:T(8,128)(2,1)}, bf16[2,2,4,96,768]{4,3,2,1,0:T(8,128)(2,1)}, u32[]{:S(2)}, u32[]{:S(2)}) collective-permute-start(bf16[2,2,4,96,768]{4,3,2,1,0:T(8,128)(2,1)} %pad_maximum_fusion.1.in_own), channel_id=1, source_target_pairs={{0,8},{8,0},{16,24},{24,16},{1,9},{9,1},{17,25},{25,17},{2,10},{10... | collective-permute-start | bytes 7077896 | tf_op jit(solution)/shard_map/ppermute | solution.py:822
  179.0 21.9 %collective-permute-start.16 = (bf16[2,2,4,96,768]{4,3,2,1,0:T(8,128)(2,1)}, bf16[2,2,4,96,768]{4,3,2,1,0:T(8,128)(2,1)}, u32[]{:S(2)}, u32[]{:S(2)}) collective-permute-start(bf16[2,2,4,96,768]{4,3,2,1,0:T(8,128)(2,1)} %pad_maximum_fusion.2.out_own), channel_id=1, source_target_pairs={{0,8},{8,0},{16,24},{24,16},{1,9},{9,1},{17,25},{25,17},{2,10},{10... | collective-permute-start | bytes 7077896 | tf_op jit(solution)/shard_map/ppermute | solution.py:822
  179.0 65.0 %all-to-all-start.2 = ((bf16[8,288,768]{2,1,0:T(8,128)(2,1)}), bf16[8,288,768]{2,1,0:T(8,128)(2,1)}, u32[]{:S(2)}, u32[]{:S(2)}) async-start(bf16[8,288,768]{2,1,0:T(8,128)(2,1)} %bitcast.296), calls=%async_computation.2 | async-start | bytes 7077888 | tf_op jit(solution)/shard_map/all_to_all | solution.py:1028
  244.1 47.4 %all-to-all-start.3 = ((bf16[8,288,768]{2,1,0:T(8,128)(2,1)}), bf16[8,288,768]{2,1,0:T(8,128)(2,1)}, u32[]{:S(2)}, u32[]{:S(2)}) async-start(bf16[8,288,768]{2,1,0:T(8,128)(2,1)} %bitcast.297), calls=%async_computation.3 | async-start | bytes 7077888 | tf_op jit(solution)/shard_map/all_to_all | solution.py:1028
  248.9 238.4 %reduce-scatter.2.cloned.1.call-start = ((), (), s32[]{:S(2)}) async-start(), calls=%async_computation.9 | async-start | bytes 9732096 | tf_op jit(solution)/shard_map/reduce_scatter | solution.py:1179
  291.5 54.4 %all-to-all-start.4 = ((bf16[8,288,768]{2,1,0:T(8,128)(2,1)}), bf16[8,288,768]{2,1,0:T(8,128)(2,1)}, u32[]{:S(2)}, u32[]{:S(2)}) async-start(bf16[8,288,768]{2,1,0:T(8,128)(2,1)} %bitcast.290), calls=%async_computation.4 | async-start | bytes 7077888 | tf_op jit(solution)/shard_map/all_to_all | solution.py:1028
  343.1 72.8 %collective-permute-start.17 = (bf16[2,4,384,384]{3,2,1,0:T(8,128)(2,1)}, bf16[2,4,384,384]{3,2,1,0:T(8,128)(2,1)}, u32[]{:S(2)}, u32[]{:S(2)}) collective-permute-start(bf16[2,4,384,384]{3,2,1,0:T(8,128)(2,1)} %expert_grads.4), channel_id=1, source_target_pairs={{0,2},{2,4},{4,6},{6,0},{1,3},{3,5},{5,7},{7,1},{8,10},{10,12},{12... | collective-permute-start | bytes 7077896 | tf_op jit(solution)/shard_map/ppermute | solution.py:809
  345.9 75.2 %all-to-all-start.5 = ((bf16[8,288,768]{2,1,0:T(8,128)(2,1)}), bf16[8,288,768]{2,1,0:T(8,128)(2,1)}, u32[]{:S(2)}, u32[]{:S(2)}) async-start(bf16[8,288,768]{2,1,0:T(8,128)(2,1)} %bitcast.291), calls=%async_computation.5 | async-start | bytes 7077888 | tf_op jit(solution)/shard_map/all_to_all | solution.py:1028
  421.1 61.2 %collective-permute-start.19 = (bf16[2,4,384,384]{3,2,1,0:T(8,128)(2,1)}, bf16[2,4,384,384]{3,2,1,0:T(8,128)(2,1)}, u32[]{:S(2)}, u32[]{:S(2)}) collective-permute-start(bf16[2,4,384,384]{3,2,1,0:T(8,128)(2,1)} %add_convert_fusion.2), channel_id=1, source_target_pairs={{0,2},{2,4},{4,6},{6,0},{1,3},{3,5},{5,7},{7,1},{8,10},{10,12},{12... | collective-permute-start | bytes 7077896 | tf_op jit(solution)/shard_map/ppermute | solution.py:809
  423.6 27.9 %collective-permute-start.18 = (bf16[4,384,384]{2,1,0:T(8,128)(2,1)}, bf16[4,384,384]{2,1,0:T(8,128)(2,1)}, u32[]{:S(2)}, u32[]{:S(2)}) collective-permute-start(bf16[4,384,384]{2,1,0:T(8,128)(2,1)} %slice_bitcast_fusion.3), channel_id=1, source_target_pairs={{0,1},{1,0},{2,3},{3,2},{4,5},{5,4},{6,7},{7,6},{8,9},{9,8},{10,11... | collective-permute-start | bytes 3538952 | tf_op jit(solution)/shard_map/ppermute | solution.py:816
  486.4 32.5 %collective-permute-start.20 = (bf16[4,384,384]{2,1,0:T(8,128)(2,1)}, bf16[4,384,384]{2,1,0:T(8,128)(2,1)}, u32[]{:S(2)}, u32[]{:S(2)}) collective-permute-start(bf16[4,384,384]{2,1,0:T(8,128)(2,1)} %get-tuple-element.127), channel_id=1, source_target_pairs={{0,2},{2,4},{4,6},{6,0},{1,3},{3,5},{5,7},{7,1},{8,10},{10,12},{12... | collective-permute-start | bytes 3538952 | tf_op jit(solution)/shard_map/ppermute | solution.py:809
  486.4 52.4 %collective-permute-start.21 = (bf16[4,384,384]{2,1,0:T(8,128)(2,1)}, bf16[4,384,384]{2,1,0:T(8,128)(2,1)}, u32[]{:S(2)}, u32[]{:S(2)}) collective-permute-start(bf16[4,384,384]{2,1,0:T(8,128)(2,1)} %get-tuple-element.128), channel_id=1, source_target_pairs={{0,3},{1,2},{2,5},{3,4},{4,7},{5,6},{6,1},{7,0},{8,11},{9,10},{10,... | collective-permute-start | bytes 3538952 | tf_op jit(solution)/shard_map/ppermute | solution.py:813
  518.4 40.2 %collective-permute-start.22 = (bf16[2,2,4,48,832]{4,3,2,1,0:T(8,128)(2,1)}, bf16[2,2,4,48,832]{4,3,2,1,0:T(8,128)(2,1)}, u32[]{:S(2)}, u32[]{:S(2)}) collective-permute-start(bf16[2,2,4,48,832]{4,3,2,1,0:T(8,128)(2,1)} %get-tuple-element.132), channel_id=1, source_target_pairs={{0,8},{8,0},{16,24},{24,16},{1,9},{9,1},{17,25},{25,17},{2,10},{10... | collective-permute-start | bytes 3833864 | tf_op jit(solution)/shard_map/ppermute | solution.py:822
  518.4 44.5 %collective-permute-start.25 = (bf16[2,2,4,48,832]{4,3,2,1,0:T(8,128)(2,1)}, bf16[2,2,4,48,832]{4,3,2,1,0:T(8,128)(2,1)}, u32[]{:S(2)}, u32[]{:S(2)}) collective-permute-start(bf16[2,2,4,48,832]{4,3,2,1,0:T(8,128)(2,1)} %get-tuple-element.134), channel_id=1, source_target_pairs={{0,8},{8,0},{16,24},{24,16},{1,9},{9,1},{17,25},{25,17},{2,10},{10... | collective-permute-start | bytes 3833864 | tf_op jit(solution)/shard_map/ppermute | solution.py:822
  543.7 24.8 %all-to-all-start.6 = ((bf16[32,4,1152]{2,1,0:T(4,128)(2,1)}), bf16[32,4,1152]{2,1,0:T(4,128)(2,1)S(1)}, u32[]{:S(2)}, u32[]{:S(2)}) async-start(bf16[32,4,1152]{2,1,0:T(4,128)(2,1)} %bitcast.299), calls=%async_computation.6 | async-start | bytes 589824 | tf_op jit(solution)/shard_map/all_to_all | solution.py:1158
  561.1 18.5 %collective-permute-start.23 = (bf16[2,4,48,832]{3,2,1,0:T(8,128)(2,1)}, bf16[2,4,48,832]{3,2,1,0:T(8,128)(2,1)}, u32[]{:S(2)}, u32[]{:S(2)}) collective-permute-start(bf16[2,4,48,832]{3,2,1,0:T(8,128)(2,1)} %get-tuple-element.249), channel_id=1, source_target_pairs={{0,16},{8,24},{16,0},{24,8},{1,17},{9,25},{17,1},{25,9},{2,18},{10... | collective-permute-start | bytes 1916936 | tf_op jit(solution)/shard_map/ppermute | solution.py:819
  565.5 18.2 %collective-permute-start.26 = (bf16[2,4,48,832]{3,2,1,0:T(8,128)(2,1)}, bf16[2,4,48,832]{3,2,1,0:T(8,128)(2,1)S(1)}, u32[]{:S(2)}, u32[]{:S(2)}) collective-permute-start(bf16[2,4,48,832]{3,2,1,0:T(8,128)(2,1)} %get-tuple-element.247), channel_id=1, source_target_pairs={{0,1},{1,0},{2,3},{3,2},{4,5},{5,4},{6,7},{7,6},{8,9},{9,8},{10,11... | collective-permute-start | bytes 1916936 | tf_op jit(solution)/shard_map/ppermute | solution.py:816
  569.4 17.0 %all-to-all-start.7 = ((f32[32,4,96]{2,1,0:T(4,128)}), f32[32,4,96]{2,1,0:T(4,128)}, u32[]{:S(2)}, u32[]{:S(2)}) async-start(f32[32,4,96]{2,1,0:T(4,128)} %copy.119), calls=%async_computation.7 | async-start | bytes 131072 | tf_op jit(solution)/shard_map/all_to_all | solution.py:1170
  (88 other events, 891.2 us)
Sparse Core Ops, SparseCore 0:
  22.7 34.3 all-gather.4
  61.7 165.9 all-gather.6
  255.7 182.1 reduce-scatter.1

commit v7 on v6

--- a/solution.py
+++ b/solution.py
@@ -1124,7 +1124,7 @@
     if ring.direct:
         own_1, give_1, own_2, give_2 = dense_grads
         got_1, got_2 = ring.over_core(give_1), ring.over_core(give_2)
-        grad_attend_in = after(grad_attend_in, own, aside)
+        grad_attend_in = after(grad_attend_in, own, aside, got_1, got_2)
         sum_1, give_1 = add_both(own_1, got_1)
         sum_2, give_2 = add_both(own_2, got_2)
         got_1, got_2 = ring.outer(give_1, False), ring.outer(give_2, True)

time: 624 us -> 620 us (level)
  Pallas kernels: 227 us -> 264 us
  waiting for transfers between devices: 141 us -> 115 us
  starting transfers between devices: 74.5 us -> 61 us
    pallas_call x2, Pallas kernels: 17.6 us -> 39.4 us  [attend_back(): pl.pallas_call(attend_back_kernel, out_shape=jax.ShapeDtypeStruct((3, tri...]
    ppermute x9, waiting for transfers between devices: 52.4 us -> 32.8 us  [step(): return lax.ppermute(value, 'zi', [(i, (i + by) % n) for i in range(n)])]
    pallas_call x2, Pallas kernels: 11.3 us -> 27.4 us  [attend(): pl.pallas_call(attend_kernel, out_shape=(jax.ShapeDtypeStruct((triple.sha...]
    ppermute x6, waiting for transfers between devices: 25.4 us -> 16.3 us  [over_x(): return lax.ppermute(value, 'exp', [(i, i ^ 2) for i in range(4)])]
    ppermute x1, waiting for transfers between devices: 19.8 us -> 12.3 us  [step_aside(): return lax.ppermute(value, FSDP, [(i, (i + 2) % n ^ 1) for i in range(n)])]
    unnamed x151 -> x157, local copies, waits for them, and re-layouts: 20.4 us -> 20.6 us
  transfers between devices with their start and end apart: 42 -> 42, of which waited for: 19 -> 18; matrix products, arithmetic and copies ran while one was open for 23% -> 22% of each run, Pallas kernels for 37% -> 43%
where the time goes in v7:
time: 620 us; the launch traced here: 612 us
  Pallas kernels  264 us (43%)
  waiting for transfers between devices  115 us (19%)
  other arithmetic  70.2 us (11%)
  starting transfers between devices  61 us (10%)
  matrix products  46.1 us (7%)
  local copies, waits for them, and re-layouts  40.4 us (7%)
  between operations  15.9 us (3%)
    pallas_call x2, Pallas kernels, expert_call(): pl.pallas_call(kernel, out_shape=(jax.ShapeDtypeStruct((rows, width), BF1...  68.1 us
    dot_general x10, matrix products, dot(): lax.dot_general(left, right, (dims, ((), ())), preferred_element_type=F32)  46.1 us
    pallas_call x1, Pallas kernels, shared_expert(): pl.pallas_call(shared_kernel, out_shape=(jax.ShapeDtypeStruct((tok_count,...  43 us
    pallas_call x4, Pallas kernels, expert_grads(): pl.pallas_call(expert_grads_kernel, out_shape=out, grid_spec=pltpu.Prefet...  42 us
    pallas_call x2, Pallas kernels, attend_back(): pl.pallas_call(attend_back_kernel, out_shape=jax.ShapeDtypeStruct((3, tri...  39.4 us
    ppermute x9, waiting for transfers between devices, step(): return lax.ppermute(value, 'zi', [(i, (i + by) % n) for i in range(n)])  32.8 us
    pallas_call x2, Pallas kernels, attend(): pl.pallas_call(attend_kernel, out_shape=(jax.ShapeDtypeStruct((triple.sha...  27.4 us
    unnamed x157, local copies, waits for them, and re-layouts  20.6 us
  transfers between devices with their start and end apart: 42, of which 18 were waited for; matrix products, arithmetic and copies ran while one was open for 22% of the time, Pallas kernels for 43%

profile of v7, /device:TPU:0, one launch (start us, length us, event | category | flops | bytes accessed | tf_op | source)
XLA Modules:
  0.0 611.9 jit_solution(14446909370417347600)
XLA Ops:
  41.2 16.5 %all-to-all-done.1 = bf16[32,4,1152]{2,1,0:T(4,128)(2,1)} async-done(((bf16[32,4,1152]{2,1,0:T(4,128)(2,1)}), bf16[32,4,1152]{2,1,0:T(4,128)(2,1)}, u32[]{:S(2)}, u32[]{:S(2)}) %all-to-all-start.1) | async-done | bytes 294944 | tf_op jit(solution)/shard_map/all_to_all | solution.py:920
  63.4 7.6 %collective-permute-done.5 = bf16[4,48,832]{2,1,0:T(8,128)(2,1)S(1)} collective-permute-done((bf16[4,48,832]{2,1,0:T(8,128)(2,1)S(1)}, bf16[4,48,832]{2,1,0:T(8,128)(2,1)S(1)}, u32[]{:S(2)}, u32[]{:S(2)}) %collective-permute-start.5) | collective-permute-done | bytes 319520 | tf_op jit(solution)/shard_map/ppermute | solution.py:816
  73.3 14.2 %collective-permute-done.6 = bf16[2,4,48,832]{3,2,1,0:T(8,128)(2,1)S(1)} collective-permute-done((bf16[2,4,48,832]{3,2,1,0:T(8,128)(2,1)S(1)}, bf16[2,4,48,832]{3,2,1,0:T(8,128)(2,1)S(1)}, u32[]{:S(2)}, u32[]{:S(2)}) %collective-permute-start.6) | collective-permute-done | bytes 639008 | tf_op jit(solution)/shard_map/ppermute | solution.py:819
  101.1 12.7 %triple.1 = (bf16[1024,768]{1,0:T(8,128)(2,1)S(1)}, bf16[1024,2304]{1,0:T(8,128)(2,1)}, bf16[768,2304]{1,0:T(8,128)(2,1)S(1)}) custom-call(s32[4]{0:T(128)S(1)} %pad_add_fusion.me, bf16[1024,768]{1,0:T(8,128)(2,1)S(1)} %copy-done.3, f32[4,1,768]{2,1,0:T(1,128)S(1)} %get-tuple-element.293.shift_ref, f32[4,1,768]{2,1,0:T(1,128)S(1)} %get-tuple-element.292.scale_ref, ...), custom_call_target="tpu_custom_call" | custom-call | flops 56623104 | bytes 98304 | tf_op jit(solution)/shard_map/triple/pallas_call | solution.py:312
  120.7 13.6 %attend.2 = (bf16[1024,384]{1,0:T(8,128)(2,1)S(1)}, f32[1,3,8,1024]{3,2,1,0:T(8,128)S(1)}) custom-call(s32[1]{0:T(128)S(6)} %copy.141.kind_ref, bf16[1024,2304]{1,0:T(8,128)(2,1)S(1)} %copy-done.1, bf16[1024,2304]{1,0:T(8,128)(2,1)S(1)} %copy-done.1, bf16[1024,2304]{1,0:T(8,128)(2,1)S(1)} %copy-done.1), custom_call_target="tpu_custom_call" | custom-call | flops 100663296 | bytes 73728 | tf_op jit(solution)/shard_map/attend/pallas_call | solution.py:128
  137.6 13.8 %attend.3 = (bf16[1024,384]{1,0:T(8,128)(2,1)S(1)}, f32[1,3,8,1024]{3,2,1,0:T(8,128)S(1)}) custom-call(s32[1]{0:T(128)S(6)} %copy.141.kind_ref, bf16[1024,2304]{1,0:T(8,128)(2,1)S(1)} %copy-done.1, bf16[1024,2304]{1,0:T(8,128)(2,1)S(1)} %copy-done.1, bf16[1024,2304]{1,0:T(8,128)(2,1)S(1)} %copy-done.1), custom_call_target="tpu_custom_call" | custom-call | flops 100663296 | bytes 73728 | tf_op jit(solution)/shard_map/attend/pallas_call | solution.py:128
  151.5 11.6 %project.1 = (f32[1024,768]{1,0:T(8,128)S(1)}, f32[1024,768]{1,0:T(8,128)S(1)}, bf16[1024,768]{1,0:T(8,128)(2,1)S(1)}, f32[1024,128]{1,0:T(8,128)S(1)}, bf16[768...) custom-call(s32[4]{0:T(128)S(1)} %pad_add_fusion.me, bf16[1024,384]{1,0:T(8,128)(2,1)S(1)} %get-tuple-element.79.left_ref.mixed_ref, ...), custom_call_target="tpu_custom_call" | custom-call | flops 18874368 | bytes 196608 | tf_op jit(solution)/shard_map/project/pallas_call | solution.py:397
  169.9 7.8 %convolution_convert_fusion = bf16[2304,768]{1,0:T(8,128)(2,1)} fusion(bf16[1024,768]{1,0:T(8,128)(2,1)} %copy-done.25, s32[1024]{0:T(1024)S(1)} %bitcast.331, s32[1024]{0:T(1024)S(1)} %bitcast.327), kind=kOutput, calls=%fused_computation.10 | convolution fusion | flops 3644522496 | bytes 5120000 | tf_op jit(solution)/shard_map/dot_general | solution.py:51
  203.8 43.0 %shared_expert.1 = (f32[1024,768]{1,0:T(8,128)}, f32[1024,768]{1,0:T(8,128)}, bf16[4,8,192,768]{3,2,1,0:T(8,128)(2,1)}) custom-call(s32[4]{0:T(128)} %copy-done.39, bf16[1024,768]{1,0:T(8,128)(2,1)} %copy-done.25, bf16[1024,768]{1,0:T(8,128)(2,1)} %get-tuple-element.241.grad_ref, bf16[2,2,4,96,768]{4,3,2,1,0:T(8,128)(2,1)} %pad_maximum_fusion.1.in_own, ...), custom_call_target="tpu_custom_call" | custom-call | flops 28991029248 | bytes 12582912 | tf_op jit(solution)/shard_map/shared_expert/pallas_call | solution.py:503
  252.1 36.6 %experts.1 = (bf16[2304,768]{1,0:T(8,128)(2,1)S(1)}, bf16[2304,3072]{1,0:T(8,128)(2,1)}, bf16[2304,3072]{1,0:T(8,128)(2,1)}) custom-call(bf16[2304,768]{1,0:T(8,128)(2,1)} %bitcast.49.x_ref, bf16[4,1536,768]{2,1,0:T(8,128)(2,1)} %bitcast.293), custom_call_target="tpu_custom_call" | custom-call | flops 679477248 | bytes 663552 | tf_op jit(solution)/shard_map/experts/pallas_call | solution.py:693
  299.5 31.5 %experts_back.1 = (bf16[2304,768]{1,0:T(8,128)(2,1)S(1)}, bf16[2304,3072]{1,0:T(8,128)(2,1)}) custom-call(bf16[2304,768]{1,0:T(8,128)(2,1)} %bitcast.51.grad_ref, bf16[2304,3072]{1,0:T(8,128)(2,1)} %get-tuple-element.104.slope_ref, bf16[4,1536,768]{2,1,0:T(8,128)(2,1)} %bitcast.294), custom_call_target="tpu_custom_call" | custom-call | flops 679477248 | bytes 442368 | tf_op jit(solution)/shard_map/experts_back/pallas_call | solution.py:693
  332.7 11.5 %expert_grads.4 = bf16[2,4,384,384]{3,2,1,0:T(8,128)(2,1)} custom-call(s32[1]{0:T(128)} %bitcast.57.part, bf16[2304,768]{1,0:T(8,128)(2,1)} %bitcast.49.x_ref, bf16[2304,3072]{1,0:T(8,128)(2,1)} %get-tuple-element.107.pre_ref, bf16[2304,3072]{1,0:T(8,128)(2,1)} %get-tuple-element.111.act_ref, bf16[2304,768]{1,0:T(8,128)(2,1)} %bitcast.51.grad_ref), custom_call_target="tpu_custom_call" | custom-call | flops 84934656 | bytes 221184 | tf_op jit(solution)/shard_map/expert_grads/pallas_call | solution.py:720
  352.0 6.5 %fusion = f32[1024,768]{1,0:T(8,128)S(1)} fusion(bf16[2304,768]{1,0:T(8,128)(2,1)} %bitcast.53, s32[1024]{0:T(1024)S(1)} %bitcast.333), kind=kOutput, calls=%fused_computation.1 | convolution fusion | flops 3626237952 | bytes 6688768 | tf_op jit(solution)/shard_map/dot_general | solution.py:51
  358.6 8.6 %multiply_reduce_fusion.6 = (f32[1024]{0:T(1024)S(1)}, f32[1024]{0:T(1024)S(1)}, f32[1024,768]{1,0:T(8,128)}) fusion(bf16[1024,768]{1,0:T(8,128)(2,1)S(1)} %copy-done.53, f32[1024,768]{1,0:T(8,128)S(1)} %fusion, f32[1024]{0:T(1024)S(1)} %bitcast.336, f32[1024]{0:T(1024)S(1)} %bitcast.335, bf16[2304,768]{1,0:T(8,128)(2,1)} %bitcast.53, s32[1024]{0:T(1024)S(1)} %bitcast.329), kind=kOutput, calls=%fused_computation.47 | convolution fusion | flops 3632527360 | bytes 11423744 | tf_op jit(solution)/shard_map/dot_general | solution.py:51
  367.1 10.1 %expert_grads.5 = bf16[2,4,384,384]{3,2,1,0:T(8,128)(2,1)S(1)} custom-call(s32[1]{0:T(128)} %bitcast.58.part, bf16[2304,768]{1,0:T(8,128)(2,1)} %bitcast.49.x_ref, bf16[2304,3072]{1,0:T(8,128)(2,1)} %get-tuple-element.107.pre_ref, bf16[2304,3072]{1,0:T(8,128)(2,1)} %get-tuple-element.111.act_ref, bf16[2304,768]{1,0:T(8,128)(2,1)} %bitcast.51.grad_ref), custom_call_target="tpu_custom_call" | custom-call | flops 84934656 | bytes 221184 | tf_op jit(solution)/shard_map/expert_grads/pallas_call | solution.py:720
  377.2 10.4 %expert_grads.6 = bf16[2,4,384,384]{3,2,1,0:T(8,128)(2,1)S(1)} custom-call(s32[1]{0:T(128)} %bitcast.59.part, bf16[2304,768]{1,0:T(8,128)(2,1)} %bitcast.49.x_ref, bf16[2304,3072]{1,0:T(8,128)(2,1)} %get-tuple-element.107.pre_ref, bf16[2304,3072]{1,0:T(8,128)(2,1)} %get-tuple-element.111.act_ref, bf16[2304,768]{1,0:T(8,128)(2,1)} %bitcast.51.grad_ref), custom_call_target="tpu_custom_call" | custom-call | flops 84934656 | bytes 221184 | tf_op jit(solution)/shard_map/expert_grads/pallas_call | solution.py:720
  389.0 10.1 %expert_grads.7 = bf16[2,4,384,384]{3,2,1,0:T(8,128)(2,1)S(1)} custom-call(s32[1]{0:T(128)} %bitcast.60.part, bf16[2304,768]{1,0:T(8,128)(2,1)} %bitcast.49.x_ref, bf16[2304,3072]{1,0:T(8,128)(2,1)} %get-tuple-element.107.pre_ref, bf16[2304,3072]{1,0:T(8,128)(2,1)} %get-tuple-element.111.act_ref, bf16[2304,768]{1,0:T(8,128)(2,1)} %bitcast.51.grad_ref), custom_call_target="tpu_custom_call" | custom-call | flops 84934656 | bytes 221184 | tf_op jit(solution)/shard_map/expert_grads/pallas_call | solution.py:720
  412.7 6.9 %fusion.7 = f32[1024,768]{1,0:T(8,128)S(1)} fusion(bf16[2304,768]{1,0:T(8,128)(2,1)} %bitcast.56, s32[1024]{0:T(1024)S(1)} %bitcast.334, s32[1024]{0:T(1024)S(1)} %bitcast.330), kind=kOutput, calls=%fused_computation.14 | convolution fusion | flops 3642753024 | bytes 6692864 | tf_op jit(solution)/shard_map/dot_general | solution.py:51
  442.7 19.6 %attend_back.2.left_ref = bf16[3,1024,384]{2,1,0:T(8,128)(2,1)S(1)} custom-call(s32[1]{0:T(128)S(6)} %copy.141.kind_ref, bf16[1024,2304]{1,0:T(8,128)(2,1)S(1)} %bitcast.289, bf16[1024,2304]{1,0:T(8,128)(2,1)S(1)} %bitcast.289, bf16[1024,2304]{1,0:T(8,128)(2,1)S(1)} %bitcast.289, bf16[1024,384]{1,0:T(8,128)(2,1)S(1)} %copy-done.18, ...), custom_call_target="tpu_custom_call" | custom-call | flops 251658240 | bytes 147456 | tf_op jit(solution)/shard_map/attend_back/pallas_call | solution.py:229
  462.3 14.3 %collective-permute-done.19 = bf16[2,4,384,384]{3,2,1,0:T(8,128)(2,1)} collective-permute-done((bf16[2,4,384,384]{3,2,1,0:T(8,128)(2,1)}, bf16[2,4,384,384]{3,2,1,0:T(8,128)(2,1)}, u32[]{:S(2)}, u32[]{:S(2)}) %collective-permute-start.19) | collective-permute-done | bytes 2359328 | tf_op jit(solution)/shard_map/ppermute | solution.py:809
  486.7 19.8 %attend_back.3.right_ref = bf16[3,1024,384]{2,1,0:T(8,128)(2,1)S(1)} custom-call(s32[1]{0:T(128)S(6)} %copy.141.kind_ref, bf16[1024,2304]{1,0:T(8,128)(2,1)S(1)} %copy-done.2, bf16[1024,2304]{1,0:T(8,128)(2,1)S(1)} %copy-done.2, bf16[1024,2304]{1,0:T(8,128)(2,1)S(1)} %copy-done.2, bf16[1024,384]{1,0:T(8,128)(2,1)S(1)} %copy-done.16, ...), custom_call_target="tpu_custom_call" | custom-call | flops 251658240 | bytes 147456 | tf_op jit(solution)/shard_map/attend_back/pallas_call | solution.py:229
  506.6 16.2 %triple_back.1 = (f32[1024,768]{1,0:T(8,128)}, bf16[2,2,4,48,832]{4,3,2,1,0:T(8,128)(2,1)S(1)}, bf16[2,2,4,48,832]{4,3,2,1,0:T(8,128)(2,1)S(1)}, bf16[2,2,4,48,8...) custom-call(s32[4]{0:T(128)S(1)} %copy-done.40, bf16[3,1024,384]{2,1,0:T(8,128)(2,1)S(1)} %copy-done.13, ...), custom_call_target="tpu_custom_call" | custom-call | flops 113246208 | bytes 147456 | tf_op jit(solution)/shard_map/triple_back/pallas_call | solution.py:631
  523.3 12.3 %collective-permute-done.21 = bf16[4,384,384]{2,1,0:T(8,128)(2,1)} collective-permute-done((bf16[4,384,384]{2,1,0:T(8,128)(2,1)}, bf16[4,384,384]{2,1,0:T(8,128)(2,1)}, u32[]{:S(2)}, u32[]{:S(2)}) %collective-permute-start.21) | collective-permute-done | bytes 1179680 | tf_op jit(solution)/shard_map/ppermute | solution.py:813
  593.3 9.7 %collective-permute-done.29 = bf16[96,832]{1,0:T(8,128)(2,1)S(1)} collective-permute-done((bf16[96,832]{1,0:T(8,128)(2,1)S(1)}, bf16[96,832]{1,0:T(8,128)(2,1)S(1)}, u32[]{:S(2)}, u32[]{:S(2)}) %collective-permute-start.29) | collective-permute-done | bytes 159776 | tf_op jit(solution)/shard_map/ppermute | solution.py:809
  (363 shorter events, 231.3 us)
Async XLA Ops:
  7.2 54.3 %all-gather.5.cloned.1.call-start = ((), (), s32[]{:S(2)}) async-start(), calls=%async_computation.10 | async-start | bytes 1474560 | tf_op jit(solution)/shard_map/all_gather | solution.py:942
  9.2 16.9 %collective-permute-start.1 = (bf16[96,832]{1,0:T(8,128)(2,1)S(1)}, bf16[96,832]{1,0:T(8,128)(2,1)S(1)}, u32[]{:S(2)}, u32[]{:S(2)}) collective-permute-start(bf16[96,832]{1,0:T(8,128)(2,1)S(1)} %pad_maximum_fusion.13), channel_id=1, source_target_pairs={{0,4},{2,6},{4,0},{6,2},{1,5},{3,7},{5,1},{7,3},{8,12},{10,14},{12... | collective-permute-start | bytes 479240 | tf_op jit(solution)/shard_map/ppermute | solution.py:809
  35.3 22.3 %all-to-all-start.1 = ((bf16[32,4,1152]{2,1,0:T(4,128)(2,1)}), bf16[32,4,1152]{2,1,0:T(4,128)(2,1)}, u32[]{:S(2)}, u32[]{:S(2)}) async-start(bf16[32,4,1152]{2,1,0:T(4,128)(2,1)} %reshape.440), calls=%async_computation.1 | async-start | bytes 589824 | tf_op jit(solution)/shard_map/all_to_all | solution.py:920
  38.6 213.5 %all-gather.7.cloned.1.call-start = ((), (), s32[]{:S(2)}) async-start(), calls=%async_computation.11 | async-start | bytes 11796480 | tf_op jit(solution)/shard_map/all_gather | solution.py:943
  39.6 19.3 %collective-permute-start.4 = (bf16[384,768]{1,0:T(8,128)(2,1)}, bf16[384,768]{1,0:T(8,128)(2,1)S(1)}, u32[]{:S(2)}, u32[]{:S(2)}) collective-permute-start(bf16[384,768]{1,0:T(8,128)(2,1)} %get-tuple-element.267), channel_id=1, source_target_pairs={{0,1},{1,0},{2,3},{3,2},{4,5},{5,4},{6,7},{7,6},{8,9},{9,8},{10,11... | collective-permute-start | bytes 1769480 | tf_op jit(solution)/shard_map/ppermute | solution.py:816
  114.1 20.3 %collective-permute-start.12 = (bf16[4,96,768]{2,1,0:T(8,128)(2,1)S(1)}, bf16[4,96,768]{2,1,0:T(8,128)(2,1)S(1)}, u32[]{:S(2)}, u32[]{:S(2)}) collective-permute-start(bf16[4,96,768]{2,1,0:T(8,128)(2,1)S(1)} %get-tuple-element.262), channel_id=1, source_target_pairs={{0,16},{8,24},{16,0},{24,8},{1,17},{9,25},{17,1},{25,9},{2,18},{10... | collective-permute-start | bytes 1769480 | tf_op jit(solution)/shard_map/ppermute | solution.py:819
  115.0 20.6 %collective-permute-start.11 = (bf16[4,96,768]{2,1,0:T(8,128)(2,1)S(1)}, bf16[4,96,768]{2,1,0:T(8,128)(2,1)S(1)}, u32[]{:S(2)}, u32[]{:S(2)}) collective-permute-start(bf16[4,96,768]{2,1,0:T(8,128)(2,1)S(1)} %get-tuple-element.263), channel_id=1, source_target_pairs={{0,1},{1,0},{2,3},{3,2},{4,5},{5,4},{6,7},{7,6},{8,9},{9,8},{10,11... | collective-permute-start | bytes 1769480 | tf_op jit(solution)/shard_map/ppermute | solution.py:816
  136.8 46.3 %collective-permute-start.13 = (bf16[2,4,96,768]{3,2,1,0:T(8,128)(2,1)}, bf16[2,4,96,768]{3,2,1,0:T(8,128)(2,1)}, u32[]{:S(2)}, u32[]{:S(2)}) collective-permute-start(bf16[2,4,96,768]{3,2,1,0:T(8,128)(2,1)} %pad_maximum_fusion.7), channel_id=1, source_target_pairs={{0,16},{8,24},{16,0},{24,8},{1,17},{9,25},{17,1},{25,9},{2,18},{10... | collective-permute-start | bytes 3538952 | tf_op jit(solution)/shard_map/ppermute | solution.py:819
  137.6 42.1 %collective-permute-start.14 = (bf16[2,4,96,768]{3,2,1,0:T(8,128)(2,1)}, bf16[2,4,96,768]{3,2,1,0:T(8,128)(2,1)}, u32[]{:S(2)}, u32[]{:S(2)}) collective-permute-start(bf16[2,4,96,768]{3,2,1,0:T(8,128)(2,1)} %pad_maximum_fusion.8), channel_id=1, source_target_pairs={{0,1},{1,0},{2,3},{3,2},{4,5},{5,4},{6,7},{7,6},{8,9},{9,8},{10,11... | collective-permute-start | bytes 3538952 | tf_op jit(solution)/shard_map/ppermute | solution.py:816
  186.3 17.5 %collective-permute-start.15 = (bf16[2,2,4,96,768]{4,3,2,1,0:T(8,128)(2,1)}, bf16[2,2,4,96,768]{4,3,2,1,0:T(8,128)(2,1)}, u32[]{:S(2)}, u32[]{:S(2)}) collective-permute-start(bf16[2,2,4,96,768]{4,3,2,1,0:T(8,128)(2,1)} %pad_maximum_fusion.1.in_own), channel_id=1, source_target_pairs={{0,8},{8,0},{16,24},{24,16},{1,9},{9,1},{17,25},{25,17},{2,10},{10... | collective-permute-start | bytes 7077896 | tf_op jit(solution)/shard_map/ppermute | solution.py:822
  187.0 59.9 %all-to-all-start.2 = ((bf16[8,288,768]{2,1,0:T(8,128)(2,1)}), bf16[8,288,768]{2,1,0:T(8,128)(2,1)}, u32[]{:S(2)}, u32[]{:S(2)}) async-start(bf16[8,288,768]{2,1,0:T(8,128)(2,1)} %bitcast.296), calls=%async_computation.2 | async-start | bytes 7077888 | tf_op jit(solution)/shard_map/all_to_all | solution.py:1028
  246.9 45.7 %all-to-all-start.3 = ((bf16[8,288,768]{2,1,0:T(8,128)(2,1)}), bf16[8,288,768]{2,1,0:T(8,128)(2,1)}, u32[]{:S(2)}, u32[]{:S(2)}) async-start(bf16[8,288,768]{2,1,0:T(8,128)(2,1)} %bitcast.297), calls=%async_computation.3 | async-start | bytes 7077888 | tf_op jit(solution)/shard_map/all_to_all | solution.py:1028
  251.4 230.3 %reduce-scatter.2.cloned.1.call-start = ((), (), s32[]{:S(2)}) async-start(), calls=%async_computation.9 | async-start | bytes 9732096 | tf_op jit(solution)/shard_map/reduce_scatter | solution.py:1179
  292.6 54.4 %all-to-all-start.4 = ((bf16[8,288,768]{2,1,0:T(8,128)(2,1)}), bf16[8,288,768]{2,1,0:T(8,128)(2,1)}, u32[]{:S(2)}, u32[]{:S(2)}) async-start(bf16[8,288,768]{2,1,0:T(8,128)(2,1)} %bitcast.290), calls=%async_computation.4 | async-start | bytes 7077888 | tf_op jit(solution)/shard_map/all_to_all | solution.py:1028
  344.2 60.9 %collective-permute-start.17 = (bf16[2,4,384,384]{3,2,1,0:T(8,128)(2,1)}, bf16[2,4,384,384]{3,2,1,0:T(8,128)(2,1)}, u32[]{:S(2)}, u32[]{:S(2)}) collective-permute-start(bf16[2,4,384,384]{3,2,1,0:T(8,128)(2,1)} %expert_grads.4), channel_id=1, source_target_pairs={{0,2},{2,4},{4,6},{6,0},{1,3},{3,5},{5,7},{7,1},{8,10},{10,12},{12... | collective-permute-start | bytes 7077896 | tf_op jit(solution)/shard_map/ppermute | solution.py:809
  347.0 63.2 %all-to-all-start.5 = ((bf16[8,288,768]{2,1,0:T(8,128)(2,1)}), bf16[8,288,768]{2,1,0:T(8,128)(2,1)}, u32[]{:S(2)}, u32[]{:S(2)}) async-start(bf16[8,288,768]{2,1,0:T(8,128)(2,1)} %bitcast.291), calls=%async_computation.5 | async-start | bytes 7077888 | tf_op jit(solution)/shard_map/all_to_all | solution.py:1028
  410.2 66.5 %collective-permute-start.19 = (bf16[2,4,384,384]{3,2,1,0:T(8,128)(2,1)}, bf16[2,4,384,384]{3,2,1,0:T(8,128)(2,1)}, u32[]{:S(2)}, u32[]{:S(2)}) collective-permute-start(bf16[2,4,384,384]{3,2,1,0:T(8,128)(2,1)} %add_convert_fusion.2), channel_id=1, source_target_pairs={{0,2},{2,4},{4,6},{6,0},{1,3},{3,5},{5,7},{7,1},{8,10},{10,12},{12... | collective-permute-start | bytes 7077896 | tf_op jit(solution)/shard_map/ppermute | solution.py:809
  412.7 29.9 %collective-permute-start.18 = (bf16[4,384,384]{2,1,0:T(8,128)(2,1)}, bf16[4,384,384]{2,1,0:T(8,128)(2,1)}, u32[]{:S(2)}, u32[]{:S(2)}) collective-permute-start(bf16[4,384,384]{2,1,0:T(8,128)(2,1)} %slice_bitcast_fusion.3), channel_id=1, source_target_pairs={{0,1},{1,0},{2,3},{3,2},{4,5},{5,4},{6,7},{7,6},{8,9},{9,8},{10,11... | collective-permute-start | bytes 3538952 | tf_op jit(solution)/shard_map/ppermute | solution.py:816
  480.8 42.5 %collective-permute-start.20 = (bf16[4,384,384]{2,1,0:T(8,128)(2,1)}, bf16[4,384,384]{2,1,0:T(8,128)(2,1)}, u32[]{:S(2)}, u32[]{:S(2)}) collective-permute-start(bf16[4,384,384]{2,1,0:T(8,128)(2,1)} %get-tuple-element.127), channel_id=1, source_target_pairs={{0,2},{2,4},{4,6},{6,0},{1,3},{3,5},{5,7},{7,1},{8,10},{10,12},{12... | collective-permute-start | bytes 3538952 | tf_op jit(solution)/shard_map/ppermute | solution.py:809
  480.8 54.7 %collective-permute-start.21 = (bf16[4,384,384]{2,1,0:T(8,128)(2,1)}, bf16[4,384,384]{2,1,0:T(8,128)(2,1)}, u32[]{:S(2)}, u32[]{:S(2)}) collective-permute-start(bf16[4,384,384]{2,1,0:T(8,128)(2,1)} %get-tuple-element.128), channel_id=1, source_target_pairs={{0,3},{1,2},{2,5},{3,4},{4,7},{5,6},{6,1},{7,0},{8,11},{9,10},{10,... | collective-permute-start | bytes 3538952 | tf_op jit(solution)/shard_map/ppermute | solution.py:813
  522.8 19.4 %collective-permute-start.22 = (bf16[2,2,4,48,832]{4,3,2,1,0:T(8,128)(2,1)S(1)}, bf16[2,2,4,48,832]{4,3,2,1,0:T(8,128)(2,1)S(1)}, u32[]{:S(2)}, u32[]{:S(2)}) collective-permute-start(bf16[2,2,4,48,832]{4,3,2,1,0:T(8,128)(2,1)S(1)} %get-tuple-element.129), channel_id=1, source_target_pairs={{0,8},{8,0},{16,24},{24,16},{1,9},{9,1},{17,25},{25,17},{2,10},{10... | collective-permute-start | bytes 3833864 | tf_op jit(solution)/shard_map/ppermute | solution.py:822
  522.8 22.3 %collective-permute-start.23 = (bf16[2,2,4,48,832]{4,3,2,1,0:T(8,128)(2,1)S(1)}, bf16[2,2,4,48,832]{4,3,2,1,0:T(8,128)(2,1)S(1)}, u32[]{:S(2)}, u32[]{:S(2)}) collective-permute-start(bf16[2,2,4,48,832]{4,3,2,1,0:T(8,128)(2,1)S(1)} %get-tuple-element.130), channel_id=1, source_target_pairs={{0,8},{8,0},{16,24},{24,16},{1,9},{9,1},{17,25},{25,17},{2,10},{10... | collective-permute-start | bytes 3833864 | tf_op jit(solution)/shard_map/ppermute | solution.py:822
  543.6 23.3 %collective-permute-start.24 = (bf16[2,4,48,832]{3,2,1,0:T(8,128)(2,1)}, bf16[2,4,48,832]{3,2,1,0:T(8,128)(2,1)}, u32[]{:S(2)}, u32[]{:S(2)}) collective-permute-start(bf16[2,4,48,832]{3,2,1,0:T(8,128)(2,1)} %get-tuple-element.249), channel_id=1, source_target_pairs={{0,16},{8,24},{16,0},{24,8},{1,17},{9,25},{17,1},{25,9},{2,18},{10... | collective-permute-start | bytes 1916936 | tf_op jit(solution)/shard_map/ppermute | solution.py:819
  554.0 20.1 %collective-permute-start.26 = (bf16[2,4,48,832]{3,2,1,0:T(8,128)(2,1)}, bf16[2,4,48,832]{3,2,1,0:T(8,128)(2,1)}, u32[]{:S(2)}, u32[]{:S(2)}) collective-permute-start(bf16[2,4,48,832]{3,2,1,0:T(8,128)(2,1)} %get-tuple-element.247), channel_id=1, source_target_pairs={{0,1},{1,0},{2,3},{3,2},{4,5},{5,4},{6,7},{7,6},{8,9},{9,8},{10,11... | collective-permute-start | bytes 1916936 | tf_op jit(solution)/shard_map/ppermute | solution.py:816
  (91 other events, 970.1 us)
Sparse Core Ops, SparseCore 0:
  22.7 34.3 all-gather.4
  61.7 165.9 all-gather.6
  258.1 189.3 reduce-scatter.1
